TPU v7x, 32 devices: a whole 2x2x4 slice. The times are simulated.
32 devices in a mesh: tx: 4 (over z), ty: 4 (over y, core), pa: 2 (over x).
Axes of the slice: x: 2, y: 2, z: 4, core: 2. Of those that a mesh axis runs over, the one named last changes fastest.
Arguments:
- object_re: float32 [512, 512], P('tx', 'ty'), may hold values from -4 to 4
- object_im: float32 [512, 512], P('tx', 'ty'), may hold values from -4 to 4
- probe_real: float32 [256, 256], replicated, may hold values from -5 to 5
- probe_imaginary: float32 [256, 256], replicated, may hold values from -5 to 5
- gain: float32 [256, 256], replicated, may hold values from 0.5 to 1.5
- dark: float32 [256, 256], replicated, may hold values from 0.05 to 0.5
- measured: float32 [64, 256, 256], P(('tx', 'ty', 'pa')), may hold values from 0.05 to 5
- positions: int32 [64, 2], P(('tx', 'ty', 'pa')), may hold values from 0 to 511, as said below
- counts: int32 [32], P(('tx', 'ty', 'pa')), may hold values from 1 to 2, as said below
- pixel_good: int32 [256, 256], replicated, may hold values 0 or 1
Outputs:
- new_object_re: float32 [512, 512], P(('tx', 'pa'), 'ty')
- new_object_im: float32 [512, 512], P(('tx', 'pa'), 'ty')
- new_probe_re: float32 [256, 256], replicated
- new_probe_im: float32 [256, 256], replicated
- new_gain: float32 [256, 256], replicated
- new_dark: float32 [256, 256], replicated
Inputs may be any that keep to these rules, and one draw needn't show every extreme that they name: `positions`: each pattern's window centre lies in the object tile of the device that holds the slot; the object tile of device (tx, ty, pa) has rows tx * 128 to tx * 128 + 127 and columns ty * 128 to ty * 128 + 127. `counts`: the number of live slots of each device, its first slots.
All inputs are finite; a program needn't handle non-finite values.
Results may differ from a plain program's by a relative error of at most 0.0002.
Values sent between devices are 32-bit elements; how exact they have to be, the bound alone decides.
No kernel may reach another device: no remote copies, remote signals or barrier semaphores. Data moves between devices by JAX's collectives and lax.ppermute only.
A program may use at most 64 MiB of HBM per device.

v0:
```python
import math

import jax
import jax.numpy as jnp
from jax import lax
from jax.sharding import PartitionSpec as P


def from_behind(value, axis, steps):
    count = lax.axis_size(axis)
    leading, last = (max(0, -steps), min(count, count - steps))
    return lax.ppermute(value, axis, [(source, source + steps) for source in range(leading, last)])


def extended(shard, sides, width):
    for axis, dim in sides:
        devices, length = (lax.axis_size(axis), shard.shape[dim])
        up = [(i, (i + 1) % devices) for i in range(devices - 1)]
        down = [(j, i) for i, j in up]
        last = lax.slice_in_dim(shard, length - width, length, axis=dim)
        leading = lax.slice_in_dim(shard, 0, width, axis=dim)
        before = lax.ppermute(last, axis, up)
        after = lax.ppermute(leading, axis, down)
        shard = jnp.concatenate([before, shard, after], axis=dim)
    return shard


def dft_tables(size):
    index = jnp.arange(size, dtype=jnp.int32)
    product = index[:, None] * index[None, :] % size
    angle = product.astype(jnp.float32) * (2.0 * math.pi / size)
    scale = 1.0 / math.sqrt(size)
    return (jnp.cos(angle) * scale, -jnp.sin(angle) * scale)


def matmul(left, right):
    return jnp.dot(left, right, precision=lax.Precision.HIGHEST, preferred_element_type=jnp.float32)


def complex_product(ar, ai, br, bi):
    return (matmul(ar, br) - matmul(ai, bi), matmul(ar, bi) + matmul(ai, br))


def transform(xr, xi, fourier_table_real, fourier_table_imaginary):
    left_re, left_im = complex_product(fourier_table_real, fourier_table_imaginary, xr, xi)
    return complex_product(left_re, left_im, fourier_table_real, fourier_table_imaginary)


def pattern_contributions(
    object_window_real,
    object_window_imaginary,
    probe_real,
    probe_imaginary,
    measured_intensity,
    gain,
    dark,
    valid_pixels,
    fourier_table_real,
    fourier_table_imaginary,
):
    psi_re = probe_real * object_window_real - probe_imaginary * object_window_imaginary
    psi_im = probe_real * object_window_imaginary + probe_imaginary * object_window_real
    far_re, far_im = transform(psi_re, psi_im, fourier_table_real, fourier_table_imaginary)
    inten = far_re * far_re + far_im * far_im
    model_intensity = gain * inten + dark
    residual_values = measured_intensity - model_intensity
    intensity_ratio = valid_pixels * (jnp.sqrt(measured_intensity / model_intensity) - 1.0)
    back_re, back_im = transform(
        intensity_ratio * far_re,
        intensity_ratio * far_im,
        fourier_table_real,
        -fourier_table_imaginary,
    )
    obj_terms = jnp.stack(
        [
            probe_real * back_re + probe_imaginary * back_im,
            probe_real * back_im - probe_imaginary * back_re,
            probe_real * probe_real + probe_imaginary * probe_imaginary,
        ]
    )
    det_terms = jnp.stack(
        [
            object_window_real * back_re + object_window_imaginary * back_im,
            object_window_real * back_im - object_window_imaginary * back_re,
            object_window_real * object_window_real
            + object_window_imaginary * object_window_imaginary,
            valid_pixels * residual_values * inten,
            valid_pixels * inten * inten,
            valid_pixels * residual_values,
            valid_pixels,
        ]
    )
    return (obj_terms, det_terms)


def pass_row_bands(strip, offset):
    return from_behind(strip, "tx", offset)


def pass_column_bands(strip, offset):
    return from_behind(strip, "ty", offset)


def body(
    object_re,
    object_im,
    probe_real,
    probe_imaginary,
    gain,
    dark,
    measured,
    positions,
    counts,
    pixel_good,
):
    tile_side = object_re.shape[0]
    window = probe_real.shape[0]
    half = window // 2
    fourier_table_real, fourier_table_imaginary = dft_tables(window)
    valid_pixels = pixel_good.astype(jnp.float32)
    tile = jnp.stack([object_re, object_im])
    padded = extended(tile, (("tx", 1), ("ty", 2)), half)
    anchor_row = lax.axis_index("tx") * tile_side
    anchor_col = lax.axis_index("ty") * tile_side
    zero = jnp.int32(0)

    def step(slot, carry):
        accum, totals = carry
        row = positions[slot, 0] - anchor_row
        col = positions[slot, 1] - anchor_col
        patch = lax.dynamic_slice(padded, (zero, row, col), (2, window, window))
        obj_terms, det_terms = pattern_contributions(
            patch[0],
            patch[1],
            probe_real,
            probe_imaginary,
            measured[slot],
            gain,
            dark,
            valid_pixels,
            fourier_table_real,
            fourier_table_imaginary,
        )
        current = lax.dynamic_slice(accum, (zero, row, col), (3, window, window))
        accum = lax.dynamic_update_slice(accum, current + obj_terms, (zero, row, col))
        return (accum, totals + det_terms)

    side = tile_side + 2 * half
    accum0 = jnp.zeros((3, side, side), jnp.float32)
    totals0 = jnp.zeros((7, window, window), jnp.float32)
    accum, totals = lax.fori_loop(0, counts[0], step, (accum0, totals0))
    from_below = pass_row_bands(accum[:, :half, :], -1)
    from_above = pass_row_bands(accum[:, half + tile_side :, :], 1)
    band = accum[:, half : half + tile_side, :]
    band = band.at[:, tile_side - half :, :].add(from_below)
    band = band.at[:, :half, :].add(from_above)
    from_next = pass_column_bands(band[:, :, :half], -1)
    from_prev = pass_column_bands(band[:, :, half + tile_side :], 1)
    inner = band[:, :, half : half + tile_side]
    inner = inner.at[:, :, tile_side - half :].add(from_next)
    inner = inner.at[:, :, :half].add(from_prev)
    own_sums = lax.psum_scatter(inner, "pa", scatter_dimension=1, tiled=True)
    grand = lax.psum(totals, ("tx", "ty", "pa"))
    own_rows = own_sums.shape[1]
    first = lax.axis_index("pa") * own_rows
    own_tile = lax.dynamic_slice_in_dim(tile, first, own_rows, 1)
    new_re = own_tile[0] + own_sums[0] / (own_sums[2] + 0.5)
    new_im = own_tile[1] + own_sums[1] / (own_sums[2] + 0.5)
    new_probe_re = probe_real + grand[0] / (grand[2] + 0.5)
    new_probe_im = probe_imaginary + grand[1] / (grand[2] + 0.5)
    new_gain = gain + grand[3] / (grand[4] + 1.0)
    new_dark = dark + 0.5 * grand[5] / (grand[6] + 1.0)
    return (new_re, new_im, new_probe_re, new_probe_im, new_gain, new_dark)


def solution(mesh):
    placed = (
        P("tx", "ty"),
        P("tx", "ty"),
        P(),
        P(),
        P(),
        P(),
        P(("tx", "ty", "pa"), None, None),
        P(("tx", "ty", "pa"), None),
        P(("tx", "ty", "pa")),
        P(),
    )
    return jax.shard_map(
        body,
        mesh=mesh,
        in_specs=placed,
        out_specs=(P(("tx", "pa"), "ty"), P(("tx", "pa"), "ty"), P(), P(), P(), P()),
        check_vma=False,
    )
```

profile of v0, /device:TPU:0, one launch (start us, length us, event | category | flops | bytes accessed | tf_op | source)
XLA Modules:
  0.0 270.0 jit_solution(10805477936085276930)
XLA Ops:
  9.0 5.0 %collective-permute-start = (f32[2,128,128]{2,1,0:T(8,128)S(1)}, f32[2,128,128]{2,1,0:T(8,128)S(1)}, u32[]{:S(2)}, u32[]{:S(2)}) collective-permute-start(f32[2,128,128]{2,1,0:T(8,128)S(1)} %pad_maximum_fusion.2), channel_id=1, source_target_pairs={{0,8},{8,16},{16,24},{1,9},{9,17},{17,25},{2,10},{10,18},{18,26},{... | collective-permute-start | bytes 393224 | tf_op jit(solution)/shard_map/ppermute | solution.py:22
  16.7 4.1 %collective-permute-done.1 = f32[2,128,128]{2,1,0:T(8,128)S(1)} collective-permute-done((f32[2,128,128]{2,1,0:T(8,128)S(1)}, f32[2,128,128]{2,1,0:T(8,128)S(1)}, u32[]{:S(2)}, u32[]{:S(2)}) %collective-permute-start.1) | collective-permute-done | bytes 131104 | tf_op jit(solution)/shard_map/ppermute | solution.py:23
  25.3 1.8 add_bitcast_fusion.1
  30.0 81.2 %while.24 = (s32[]{:T(128)}, f32[3,384,384]{2,1,0:T(8,128)}, f32[7,256,256]{2,1,0:T(8,128)S(1)}, s32[]{:T(128)}, s32[2,2]{1,0:T(2,128)S(1)}, /*index=5*/s32[]{:T...) while((s32[]{:T(128)}, f32[3,384,384]{2,1,0:T(8,128)}, ...), condition=%wide.region_1.2_spmd.clone.clone, body=%wide.region_0.1_spmd.clone.clone.sunk | while | flops 3242328064 | bytes 39584296 | solution.py:151
  33.7 1.5 fusion.202
  35.2 1.5 convolution_add_fusion.6
  36.7 1.5 fusion.200
  38.2 1.5 convolution_subtract_fusion.8
  39.7 1.5 fusion.201
  41.2 1.5 convolution_subtract_fusion.9
  42.6 1.5 fusion.203
  44.2 1.6 fusion.204
  45.7 1.5 fusion.207
  47.2 1.5 convolution_add_fusion.7
  48.7 1.5 fusion.205
  50.2 1.5 convolution_subtract_fusion.10
  51.7 1.5 fusion.206
  53.2 1.5 convolution_subtract_fusion.11
  54.7 1.5 fusion.208
  56.2 1.5 bitcast_dynamic-update-slice_fusion.10
  59.4 2.5 maximum_add_fusion.2
  61.9 8.1 %dynamic_update_slice.9 = f32[3,384,384]{2,1,0:T(8,128)} dynamic-update-slice(f32[3,384,384]{2,1,0:T(8,128)} %get-tuple-element.621, f32[3,256,256]{2,1,0:T(8,128)} %maximum_add_fusion.2, s32[]{:T(128)} %constant.185.clone.1..sunk, s32[]{:T(128)S(6)} %select_n.157, s32[]{:T(128)S(6)} %select_n.158) | dynamic-update-slice | bytes 1572868 | tf_op jit(solution)/shard_map/while/body/dynamic_update_slice | solution.py:145
  73.8 1.5 fusion.202
  75.2 1.5 convolution_add_fusion.6
  76.7 1.5 fusion.200
  78.2 1.5 convolution_subtract_fusion.8
  79.7 1.5 fusion.201
  81.2 1.5 convolution_subtract_fusion.9
  82.7 1.5 fusion.203
  84.2 1.6 fusion.204
  85.8 1.5 fusion.207
  87.3 1.5 convolution_add_fusion.7
  88.8 1.5 fusion.205
  90.3 1.5 convolution_subtract_fusion.10
  91.8 1.5 fusion.206
  93.3 1.5 convolution_subtract_fusion.11
  94.7 1.5 fusion.208
  96.2 1.5 bitcast_dynamic-update-slice_fusion.10
  99.5 2.5 maximum_add_fusion.2
  102.0 8.6 %dynamic_update_slice.9 = f32[3,384,384]{2,1,0:T(8,128)} dynamic-update-slice(f32[3,384,384]{2,1,0:T(8,128)} %get-tuple-element.621, f32[3,256,256]{2,1,0:T(8,128)} %maximum_add_fusion.2, s32[]{:T(128)} %constant.185.clone.1..sunk, s32[]{:T(128)S(6)} %select_n.157, s32[]{:T(128)S(6)} %select_n.158) | dynamic-update-slice | bytes 1572868 | tf_op jit(solution)/shard_map/while/body/dynamic_update_slice | solution.py:145
  111.2 2.8 %fusion.134 = (f32[3,128,384]{2,1,0:T(8,128)}, f32[3,128,384]{2,1,0:T(8,128)S(1)}) fusion(f32[3,384,384]{2,1,0:T(8,128)} %get-tuple-element.341), kind=kLoop, calls=%fused_computation.185 | loop fusion | bytes 2359296 | tf_op jit(solution)/shard_map/slice | solution.py:152
  115.3 5.4 %collective-permute-start.5 = (f32[3,128,384]{2,1,0:T(8,128)S(1)}, f32[3,128,384]{2,1,0:T(8,128)}, u32[]{:S(2)}, u32[]{:S(2)}) collective-permute-start(f32[3,128,384]{2,1,0:T(8,128)S(1)} %get-tuple-element.481), channel_id=1, source_target_pairs={{0,8},{8,16},{16,24},{1,9},{9,17},{17,25},{2,10},{10,18},{18,26},{... | collective-permute-start | bytes 1769480 | tf_op jit(solution)/shard_map/ppermute | solution.py:12
  120.8 5.4 %collective-permute-done.4 = f32[3,128,384]{2,1,0:T(8,128)S(1)} collective-permute-done((f32[3,128,384]{2,1,0:T(8,128)}, f32[3,128,384]{2,1,0:T(8,128)S(1)}, u32[]{:S(2)}, u32[]{:S(2)}) %collective-permute-start.4) | collective-permute-done | bytes 589856 | tf_op jit(solution)/shard_map/ppermute | solution.py:12
  126.3 1.5 collective-permute-done.5
  130.5 10.6 %collective-permute-start.7 = (f32[3,128,128]{2,1,0:T(8,128)S(1)}, f32[3,128,128]{2,1,0:T(8,128)S(1)}, u32[]{:S(2)}, u32[]{:S(2)}) collective-permute-start(f32[3,128,128]{2,1,0:T(8,128)S(1)} %get-tuple-element.483), channel_id=1, source_target_pairs={{0,2},{2,4},{4,6},{1,3},{3,5},{5,7},{8,10},{10,12},{12,14},{9,11},... | collective-permute-start | bytes 589832 | tf_op jit(solution)/shard_map/ppermute | solution.py:12
  142.9 115.7 %all-reduce.2.cloned.1.call-done = f32[7,256,256]{2,1,0:T(8,128)} async-done(((f32[7,256,256]{2,1,0:T(8,128)}), f32[7,256,256]{2,1,0:T(8,128)}) %all-reduce.2.cloned.1.call-update) | async-done | bytes 1835024 | tf_op jit(solution)/shard_map/psum | solution.py:163
  258.6 2.5 fusion.120
  261.1 1.4 fusion.131
  (85 shorter events, 23.7 us)
Async XLA Ops:
  8.0 20.4 %copy-start.8 = (f32[128,128]{1,0:T(8,128)S(1)}, f32[128,128]{1,0:T(8,128)}, u32[]{:S(2)}) copy-start(f32[128,128]{1,0:T(8,128)} %param.28) | copy-start | bytes 196612
  8.0 20.4 %copy-start.6 = (f32[128,128]{1,0:T(8,128)S(1)}, f32[128,128]{1,0:T(8,128)}, u32[]{:S(2)}) copy-start(f32[128,128]{1,0:T(8,128)} %param.29) | copy-start | bytes 196612
  8.0 250.6 %all-reduce.2.cloned.1.call-start = ((), (), s32[]{:S(2)}) async-start(), calls=%async_computation.2 | async-start | bytes 3670016 | tf_op jit(solution)/shard_map/psum | solution.py:163
  9.0 7.7 %collective-permute-start = (f32[2,128,128]{2,1,0:T(8,128)S(1)}, f32[2,128,128]{2,1,0:T(8,128)S(1)}, u32[]{:S(2)}, u32[]{:S(2)}) collective-permute-start(f32[2,128,128]{2,1,0:T(8,128)S(1)} %pad_maximum_fusion.2), channel_id=1, source_target_pairs={{0,8},{8,16},{16,24},{1,9},{9,17},{17,25},{2,10},{10,18},{18,26},{... | collective-permute-start | bytes 393224 | tf_op jit(solution)/shard_map/ppermute | solution.py:22
  13.9 6.9 %collective-permute-start.1 = (f32[2,128,128]{2,1,0:T(8,128)S(1)}, f32[2,128,128]{2,1,0:T(8,128)S(1)}, u32[]{:S(2)}, u32[]{:S(2)}) collective-permute-start(f32[2,128,128]{2,1,0:T(8,128)S(1)} %pad_maximum_fusion.2), channel_id=1, source_target_pairs={{8,0},{16,8},{24,16},{9,1},{17,9},{25,17},{10,2},{18,10},{26,18},{... | collective-permute-start | bytes 393224 | tf_op jit(solution)/shard_map/ppermute | solution.py:23
  21.7 5.4 %collective-permute-start.2 = (f32[2,384,128]{2,1,0:T(8,128)S(1)}, f32[2,384,128]{2,1,0:T(8,128)S(1)}, u32[]{:S(2)}, u32[]{:S(2)}) collective-permute-start(f32[2,384,128]{2,1,0:T(8,128)S(1)} %pad_maximum_fusion.1), channel_id=1, source_target_pairs={{0,2},{2,4},{4,6},{1,3},{3,5},{5,7},{8,10},{10,12},{12,14},{9,11},... | collective-permute-start | bytes 1179656 | tf_op jit(solution)/shard_map/ppermute | solution.py:22
  23.0 5.3 %collective-permute-start.3 = (f32[2,384,128]{2,1,0:T(8,128)S(1)}, f32[2,384,128]{2,1,0:T(8,128)S(1)}, u32[]{:S(2)}, u32[]{:S(2)}) collective-permute-start(f32[2,384,128]{2,1,0:T(8,128)S(1)} %pad_maximum_fusion.1), channel_id=1, source_target_pairs={{2,0},{4,2},{6,4},{3,1},{5,3},{7,5},{10,8},{12,10},{14,12},{11,9},... | collective-permute-start | bytes 1179656 | tf_op jit(solution)/shard_map/ppermute | solution.py:23
  28.4 1.5 copy-start.1
  28.5 1.5 copy-start.14
  39.6 4.5 %copy-start.4 = (f32[2,256,256]{2,1,0:T(8,128)S(1)}, f32[2,256,256]{2,1,0:T(8,128)}, u32[]{:S(2)}) copy-start(f32[2,256,256]{2,1,0:T(8,128)} %get-tuple-element.647) | copy-start | bytes 1572868 | tf_op jit(solution)/shard_map/while
  39.6 4.5 %copy-start.10 = (f32[256,256]{1,0:T(8,128)S(1)}, f32[256,256]{1,0:T(8,128)}, u32[]{:S(2)}) copy-start(f32[256,256]{1,0:T(8,128)} %get-tuple-element.651) | copy-start | bytes 786436 | tf_op jit(solution)/shard_map/while
  39.7 4.5 %copy-start.12 = (f32[256,256]{1,0:T(8,128)S(1)}, f32[256,256]{1,0:T(8,128)}, u32[]{:S(2)}) copy-start(f32[256,256]{1,0:T(8,128)} %get-tuple-element.652) | copy-start | bytes 786436 | tf_op jit(solution)/shard_map/while
  58.4 1.0 copy-start.2
  58.4 1.0 copy-start.5
  79.7 4.5 %copy-start.4 = (f32[2,256,256]{2,1,0:T(8,128)S(1)}, f32[2,256,256]{2,1,0:T(8,128)}, u32[]{:S(2)}) copy-start(f32[2,256,256]{2,1,0:T(8,128)} %get-tuple-element.647) | copy-start | bytes 1572868 | tf_op jit(solution)/shard_map/while
  79.7 4.5 %copy-start.10 = (f32[256,256]{1,0:T(8,128)S(1)}, f32[256,256]{1,0:T(8,128)}, u32[]{:S(2)}) copy-start(f32[256,256]{1,0:T(8,128)} %get-tuple-element.651) | copy-start | bytes 786436 | tf_op jit(solution)/shard_map/while
  79.7 4.5 %copy-start.12 = (f32[256,256]{1,0:T(8,128)S(1)}, f32[256,256]{1,0:T(8,128)}, u32[]{:S(2)}) copy-start(f32[256,256]{1,0:T(8,128)} %get-tuple-element.652) | copy-start | bytes 786436 | tf_op jit(solution)/shard_map/while
  98.5 1.0 copy-start.2
  98.5 1.0 copy-start.5
  111.2 9.5 %copy-start = (f32[7,256,256]{2,1,0:T(8,128)}, f32[7,256,256]{2,1,0:T(8,128)S(1)}, u32[]{:S(2)}) copy-start(f32[7,256,256]{2,1,0:T(8,128)S(1)} %get-tuple-element.342) | copy-start | bytes 5505028
  114.0 12.2 %collective-permute-start.4 = (f32[3,128,384]{2,1,0:T(8,128)}, f32[3,128,384]{2,1,0:T(8,128)S(1)}, u32[]{:S(2)}, u32[]{:S(2)}) collective-permute-start(f32[3,128,384]{2,1,0:T(8,128)} %get-tuple-element.480), channel_id=1, source_target_pairs={{8,0},{16,8},{24,16},{9,1},{17,9},{25,17},{10,2},{18,10},{26,18},{... | collective-permute-start | bytes 1769480 | tf_op jit(solution)/shard_map/ppermute | solution.py:12
  115.3 12.5 %collective-permute-start.5 = (f32[3,128,384]{2,1,0:T(8,128)S(1)}, f32[3,128,384]{2,1,0:T(8,128)}, u32[]{:S(2)}, u32[]{:S(2)}) collective-permute-start(f32[3,128,384]{2,1,0:T(8,128)S(1)} %get-tuple-element.481), channel_id=1, source_target_pairs={{0,8},{8,16},{16,24},{1,9},{9,17},{17,25},{2,10},{10,18},{18,26},{... | collective-permute-start | bytes 1769480 | tf_op jit(solution)/shard_map/ppermute | solution.py:12
  120.7 22.2 %copy-start.7 = (f32[128,128]{1,0:T(8,128)S(1)}, f32[128,128]{1,0:T(8,128)}, u32[]{:S(2)}) copy-start(f32[128,128]{1,0:T(8,128)} %param.29) | copy-start | bytes 196612
  120.7 22.2 %copy-start.9 = (f32[128,128]{1,0:T(8,128)S(1)}, f32[128,128]{1,0:T(8,128)}, u32[]{:S(2)}) copy-start(f32[128,128]{1,0:T(8,128)} %param.28) | copy-start | bytes 196612
  120.7 137.9 %copy-start.3 = (f32[256,256]{1,0:T(8,128)S(1)}, f32[256,256]{1,0:T(8,128)}, u32[]{:S(2)}) copy-start(f32[256,256]{1,0:T(8,128)} %get-tuple-element.665) | copy-start | bytes 786436
  120.7 137.9 %copy-start.11 = (f32[256,256]{1,0:T(8,128)S(1)}, f32[256,256]{1,0:T(8,128)}, u32[]{:S(2)}) copy-start(f32[256,256]{1,0:T(8,128)} %get-tuple-element.677) | copy-start | bytes 786436
  120.8 137.9 %copy-start.13 = (f32[256,256]{1,0:T(8,128)S(1)}, f32[256,256]{1,0:T(8,128)}, u32[]{:S(2)}) copy-start(f32[256,256]{1,0:T(8,128)} %get-tuple-element.678) | copy-start | bytes 786436
  120.8 140.3 %reduce-scatter.2.cloned.1.call-start = ((), (), s32[]{:S(2)}) async-start(), calls=%async_computation.1 | async-start | bytes 294912 | tf_op jit(solution)/shard_map/reduce_scatter | solution.py:162
  129.2 11.9 %collective-permute-start.6 = (f32[3,128,128]{2,1,0:T(8,128)S(1)}, f32[3,128,128]{2,1,0:T(8,128)S(1)}, u32[]{:S(2)}, u32[]{:S(2)}) collective-permute-start(f32[3,128,128]{2,1,0:T(8,128)S(1)} %get-tuple-element.482), channel_id=1, source_target_pairs={{2,0},{4,2},{6,4},{3,1},{5,3},{7,5},{10,8},{12,10},{14,12},{11,9},... | collective-permute-start | bytes 589832 | tf_op jit(solution)/shard_map/ppermute | solution.py:12
  130.5 11.7 %collective-permute-start.7 = (f32[3,128,128]{2,1,0:T(8,128)S(1)}, f32[3,128,128]{2,1,0:T(8,128)S(1)}, u32[]{:S(2)}, u32[]{:S(2)}) collective-permute-start(f32[3,128,128]{2,1,0:T(8,128)S(1)} %get-tuple-element.483), channel_id=1, source_target_pairs={{0,2},{2,4},{4,6},{1,3},{3,5},{5,7},{8,10},{10,12},{12,14},{9,11},... | collective-permute-start | bytes 589832 | tf_op jit(solution)/shard_map/ppermute | solution.py:12
Sparse Core Ops, SparseCore 0:
  120.8 137.7 all-reduce.1
Sparse Core Ops, SparseCore 1:
  143.0 17.1 reduce-scatter.1
where the time goes:
time: 272 us; the launch traced here: 270 us
  waiting for transfers between devices  131 us (48%)
  matrix products  47.6 us (18%)
  starting transfers between devices  27.5 us (10%)
  local copies, waits for them, and re-layouts  23.2 us (9%)
  other arithmetic  20.2 us (7%)
  between operations  15.7 us (6%)
  loops' own time  5.08 us (2%)
    psum x1, waiting for transfers between devices, body(): grand = lax.psum(totals, ('tx', 'ty', 'pa'))  116 us
    dot_general x32, matrix products, matmul(): jnp.dot(left, right, precision=lax.Precision.HIGHEST, preferred_element_t...  47.6 us
    ppermute x4, starting transfers between devices, from_behind(): lax.ppermute(value, axis, [(source, source + steps) for source in range(l...  18.6 us
    dynamic_update_slice x2, local copies, waits for them, and re-layouts, step(): lax.dynamic_update_slice(accum, current + obj_terms, (zero, row, col))  16.6 us
    ppermute x4, waiting for transfers between devices, from_behind(): lax.ppermute(value, axis, [(source, source + steps) for source in range(l...  8.05 us
    ppermute x2, starting transfers between devices, extended(): before = lax.ppermute(last, axis, up)  6.28 us
  transfers between devices with their start and end apart: 10, of which 7 were waited for; matrix products, arithmetic and copies ran while one was open for 3% of the time, Pallas kernels for 0%

commit v1 on v0

v1 whole, which is shorter than its diff:
```python
import functools
import math

import jax
import jax.numpy as jnp
import numpy as np
from jax import lax
from jax.experimental import pallas as pl
from jax.experimental.pallas import tpu as pltpu
from jax.sharding import PartitionSpec as P

MESH_AXES = ("tx", "ty", "pa")
ROWS = 32
SUBLANES = 8


def pairs(size, parity):
    found = []
    for low in range(parity, size - 1, 2):
        found += [(low, low + 1), (low + 1, low)]
    return found


def neighbour_swap(value, axis, parity):
    return lax.ppermute(value, axis, pairs(lax.axis_size(axis), parity))


def ordered(parity, first, second):
    even = parity == 0
    return jnp.where(even, first, second), jnp.where(even, second, first)


def split_table(table):
    high = table.astype(jnp.bfloat16)
    low = (table - high.astype(np.float32)).astype(jnp.bfloat16)
    return high, low


def dft_tables(size):
    index = np.arange(size)
    angle = (np.outer(index, index) % size) * (2.0 * math.pi / size)
    real = (np.cos(angle) / math.sqrt(size)).astype(np.float32)
    imag = (-np.sin(angle) / math.sqrt(size)).astype(np.float32)
    row_form = np.block([[real, imag], [-imag, real]])
    col_form = np.block([[real, -imag], [imag, real]])
    return (*split_table(row_form), *split_table(col_form))


def split(value):
    high = value.astype(jnp.bfloat16)
    return high, (value - high.astype(jnp.float32)).astype(jnp.bfloat16)


def three_pass(left_high, left_low, right_high, right_low):
    dot = functools.partial(jnp.dot, preferred_element_type=jnp.float32)
    return dot(left_high, right_high) + dot(left_high, right_low) + dot(left_low, right_high)


def aligned(row):
    part = lax.rem(row, SUBLANES)
    return row - part, part


def update_kernel(
    offsets,
    live_count,
    padded,
    probe_re,
    probe_im,
    measured,
    gain,
    dark,
    good,
    row_high,
    row_low,
    col_high,
    col_low,
    accum,
    totals,
    win,
    x_high,
    x_low,
    y_high,
    y_low,
    line,
    plane,
):
    slots = measured.shape[0]
    size = probe_re.shape[0]
    side = padded.shape[1]
    steps = size // ROWS
    accum[...] = jnp.zeros_like(accum)
    totals[...] = jnp.zeros_like(totals)

    def right_then_left(first_high, first_low, second_high, second_low):
        for slot in range(slots):
            here = pl.ds(slot * size, size)
            line[...] = three_pass(x_high[here, :], x_low[here, :], first_high[...], first_low[...])
            for part in range(2):
                high, low = split(line[:, part * size : (part + 1) * size])
                y_high[part * size : (part + 1) * size, here] = high
                y_low[part * size : (part + 1) * size, here] = low
        for slot in range(slots):
            here = pl.ds(slot * size, size)
            plane[slot] = three_pass(
                second_high[...], second_low[...], y_high[:, here], y_low[:, here]
            )

    def put_x(slot, at, real, imag):
        rows = pl.ds(slot * size + at, ROWS)
        for part, value in enumerate((real, imag)):
            high, low = split(value)
            x_high[rows, part * size : (part + 1) * size] = high
            x_low[rows, part * size : (part + 1) * size] = low

    for slot in range(slots):
        row, row_part = aligned(offsets[slot, 0])
        back_rows = lax.rem(ROWS + SUBLANES - row_part, ROWS + SUBLANES)
        back_cols = lax.rem(side - offsets[slot, 1], side)

        def load(step, _):
            at = pl.multiple_of(step * ROWS, ROWS)
            here = pl.ds(at, ROWS)
            parts = []
            for part in range(2):
                band = padded[part, pl.ds(pl.multiple_of(row + at, SUBLANES), ROWS + SUBLANES), :]
                band = pltpu.roll(band, back_rows, axis=0)[:ROWS]
                parts.append(pltpu.roll(band, back_cols, axis=1)[:, :size])
                win[slot, part, here, :] = parts[part]
            wr, wi = parts
            pr, pi = probe_re[here, :], probe_im[here, :]
            put_x(slot, at, pr * wr - pi * wi, pr * wi + pi * wr)
            return 0

        lax.fori_loop(0, steps, load, 0)

    right_then_left(row_high, row_low, col_high, col_low)

    for slot in range(slots):
        live = jnp.where(slot < live_count[0], 1.0, 0.0).astype(jnp.float32)

        def detect(step, _):
            at = pl.multiple_of(step * ROWS, ROWS)
            here = pl.ds(at, ROWS)
            fr = plane[slot, here, :]
            fi = plane[slot, pl.ds(size + at, ROWS), :]
            inten = fr * fr + fi * fi
            model = gain[here, :] * inten + dark[here, :]
            seen = measured[slot, here, :]
            valid = good[here, :].astype(jnp.float32)
            ratio = valid * (jnp.sqrt(seen / model) - 1.0)
            put_x(slot, at, ratio * fr, ratio * fi)
            weight = valid * live
            resid = weight * (seen - model)
            wr, wi = win[slot, 0, here, :], win[slot, 1, here, :]
            totals[0, here, :] += live * (wr * wr + wi * wi)
            totals[1, here, :] += resid * inten
            totals[2, here, :] += weight * inten * inten
            totals[3, here, :] += resid
            return 0

        lax.fori_loop(0, steps, detect, 0)

    right_then_left(col_high, col_low, row_high, row_low)

    for slot in range(slots):
        live = jnp.where(slot < live_count[0], 1.0, 0.0).astype(jnp.float32)
        row, row_part = aligned(offsets[slot, 0])
        col = offsets[slot, 1]

        def place(step, _):
            at = pl.multiple_of(step * ROWS, ROWS)
            here = pl.ds(at, ROWS)
            br = live * plane[slot, here, :]
            bi = live * plane[slot, pl.ds(size + at, ROWS), :]
            wr, wi = win[slot, 0, here, :], win[slot, 1, here, :]
            totals[4, here, :] += wr * br + wi * bi
            totals[5, here, :] += wr * bi - wi * br
            pr, pi = probe_re[here, :], probe_im[here, :]
            terms = (pr * br + pi * bi, pr * bi - pi * br, live * (pr * pr + pi * pi))
            there = pl.ds(pl.multiple_of(row + at, SUBLANES), ROWS + SUBLANES)
            for part, term in enumerate(terms):
                wide = jnp.pad(term, ((0, SUBLANES), (0, side - size)))
                wide = pltpu.roll(pltpu.roll(wide, row_part, axis=0), col, axis=1)
                accum[part, there, :] += wide
            return 0

        lax.fori_loop(0, steps, place, 0)


def update(offsets, counts, padded, probe_re, probe_im, measured, gain, dark, good, tables):
    slots, size = measured.shape[:2]
    side = padded.shape[1]
    smem = pl.BlockSpec(memory_space=pltpu.SMEM)
    vmem = pl.BlockSpec(memory_space=pltpu.VMEM)
    return pl.pallas_call(
        update_kernel,
        out_shape=(
            jax.ShapeDtypeStruct((3, side, side), jnp.float32),
            jax.ShapeDtypeStruct((6, size, size), jnp.float32),
        ),
        in_specs=[smem, smem] + [vmem] * 11,
        out_specs=(vmem, vmem),
        scratch_shapes=[
            pltpu.VMEM((slots, 2, size, size), jnp.float32),
            pltpu.VMEM((slots * size, 2 * size), jnp.bfloat16),
            pltpu.VMEM((slots * size, 2 * size), jnp.bfloat16),
            pltpu.VMEM((2 * size, slots * size), jnp.bfloat16),
            pltpu.VMEM((2 * size, slots * size), jnp.bfloat16),
            pltpu.VMEM((size, 2 * size), jnp.float32),
            pltpu.VMEM((slots, 2 * size, size), jnp.float32),
        ],
        compiler_params=pltpu.CompilerParams(vmem_limit_bytes=40 * 1024 * 1024),
    )(offsets, counts, padded, probe_re, probe_im, measured, gain, dark, good, *tables)


def partner_swap(value, partner_of):
    shape = tuple(lax.axis_size(axis) for axis in MESH_AXES)
    moves = []
    for here in np.ndindex(*shape):
        there = partner_of(*here)
        moves.append((int(np.ravel_multi_index(here, shape)), int(np.ravel_multi_index(there, shape))))
    return lax.ppermute(value, MESH_AXES, moves)


def exchange_steps(n_tx, n_ty, n_pa):
    halving = [(lambda t, y, p: (t, y ^ 1, p), lambda t, y, p: y & 1)]
    y_bits = [1 << k for k in range(1, n_ty.bit_length() - 1)]
    p_bits = [1 << k for k in range(n_pa.bit_length() - 1)]

    def along_y(bit):
        return (lambda t, y, p: (t, y ^ bit, p), lambda t, y, p: (y // bit) & 1)

    def along_p(bit):
        return (lambda t, y, p: (t, y, p ^ bit), lambda t, y, p: (p // bit) & 1)

    def by_core(one, two):
        def partner(t, y, p):
            return one[0](t, y, p) if y % 2 == 0 else two[0](t, y, p)

        def bit(t, y, p):
            return jnp.where(y % 2 == 0, one[1](t, y, p), two[1](t, y, p))

        return partner, bit

    shared = min(len(y_bits), len(p_bits))
    ones = [along_p(b) for b in p_bits[:shared]] + [along_y(b) for b in y_bits[:shared]]
    twos = [along_y(b) for b in y_bits[:shared]] + [along_p(b) for b in p_bits[:shared]]
    halving += [by_core(one, two) for one, two in zip(ones, twos)]
    halving += [along_y(b) for b in y_bits[shared:]] + [along_p(b) for b in p_bits[shared:]]
    whole = [
        (lambda t, y, p, b=1 << k: (t ^ b, y, p), None) for k in range(n_tx.bit_length() - 1)
    ]
    return halving, whole


def body(
    object_re,
    object_im,
    probe_real,
    probe_imaginary,
    gain,
    dark,
    measured,
    positions,
    counts,
    pixel_good,
):
    tile_side = object_re.shape[0]
    window = probe_real.shape[0]
    half = window // 2
    tables = dft_tables(window)
    t, y, p = (lax.axis_index(axis) for axis in MESH_AXES)
    n_tx, n_ty, n_pa = (lax.axis_size(axis) for axis in MESH_AXES)

    tile = jnp.stack([object_re, object_im])
    before, after = ordered(
        t % 2, neighbour_swap(tile, "tx", 1), neighbour_swap(tile, "tx", 0)
    )
    strip = jnp.concatenate([before, tile, after], axis=1)
    before, after = ordered(
        y % 2, neighbour_swap(strip, "ty", 1), neighbour_swap(strip, "ty", 0)
    )
    padded = jnp.concatenate([before, strip, after], axis=2)
    anchor = jnp.stack([t * tile_side, y * tile_side]).astype(jnp.int32)
    accum, totals = update(
        positions - anchor,
        counts,
        padded,
        probe_real,
        probe_imaginary,
        measured,
        gain,
        dark,
        pixel_good,
        tables,
    )

    halving, whole = exchange_steps(n_tx, n_ty, n_pa)
    live = jnp.broadcast_to(counts.astype(jnp.float32)[:, None], (8, window))

    def pack(arrays, tail):
        return jnp.concatenate([arrays.reshape(-1, window), tail], axis=0)

    def unpack(flat, kinds):
        return flat[:-8].reshape(kinds, -1, window), flat[-8:]

    sums = totals
    kinds = totals.shape[0]
    bits = []
    for partner, bit in halving:
        upper = bit(t, y, p)
        bits.append(upper)
        rows = sums.shape[1] // 2
        kept = lax.dynamic_slice_in_dim(sums, upper * rows, rows, 1)
        sent = lax.dynamic_slice_in_dim(sums, (1 - upper) * rows, rows, 1)
        got, got_live = unpack(partner_swap(pack(sent, live), partner), kinds)
        sums, live = kept + got, live + got_live
    for partner, _ in whole:
        got, got_live = unpack(partner_swap(pack(sums, live), partner), kinds)
        sums, live = sums + got, live + got_live
    rows = sums.shape[1]
    first = jnp.int32(0)
    span = window
    for upper in bits:
        span //= 2
        first = first + upper * span
    own = lambda array: lax.dynamic_slice_in_dim(array, first, rows, 0)
    valid = own(pixel_good).astype(jnp.float32)
    new = jnp.stack(
        [
            own(probe_real) + sums[4] / (sums[0] + 0.5),
            own(probe_imaginary) + sums[5] / (sums[0] + 0.5),
            own(gain) + sums[1] / (sums[2] + 1.0),
            own(dark) + 0.5 * sums[3] / (valid * live[:1] + 1.0),
        ]
    )
    for (partner, _), upper in zip(halving[::-1], bits[::-1]):
        low, high = ordered(upper, new, partner_swap(new, partner))
        new = jnp.concatenate([low, high], axis=1)

    edge = half + tile_side
    lower, upper = accum[:, :, :half], accum[:, :, edge:]
    even_y, even_t = y % 2 == 0, t % 2 == 0
    inner = accum[:, :, half:edge]
    to_one, to_zero = ordered(y % 2, lower, upper)
    from_one = neighbour_swap(to_one, "ty", 1)
    from_zero = neighbour_swap(to_zero, "ty", 0)
    strip = inner + from_one + from_zero
    lower, upper = strip[:, :half], strip[:, edge:]
    inner = strip[:, half:edge]
    to_one, to_zero = ordered(t % 2, lower, upper)
    from_one = neighbour_swap(to_one, "tx", 1)
    from_zero = neighbour_swap(to_zero, "tx", 0)
    sums = inner + from_one + from_zero
    for k in range(n_pa.bit_length() - 2, -1, -1):
        bit = 1 << k
        rows = sums.shape[1] // 2
        upper = (p // bit) & 1
        kept = lax.dynamic_slice_in_dim(sums, upper * rows, rows, 1)
        sent = lax.dynamic_slice_in_dim(sums, (1 - upper) * rows, rows, 1)
        sums = kept + lax.ppermute(sent, "pa", [(i, i ^ bit) for i in range(n_pa)])
    rows = sums.shape[1]
    own_tile = lax.dynamic_slice_in_dim(tile, p * rows, rows, 1)
    new_re = own_tile[0] + sums[0] / (sums[2] + 0.5)
    new_im = own_tile[1] + sums[1] / (sums[2] + 0.5)
    return (new_re, new_im, new[0], new[1], new[2], new[3])


def solution(mesh):
    placed = (
        P("tx", "ty"),
        P("tx", "ty"),
        P(),
        P(),
        P(),
        P(),
        P(("tx", "ty", "pa"), None, None),
        P(("tx", "ty", "pa"), None),
        P(("tx", "ty", "pa")),
        P(),
    )
    return jax.shard_map(
        body,
        mesh=mesh,
        in_specs=placed,
        out_specs=(P(("tx", "pa"), "ty"), P(("tx", "pa"), "ty"), P(), P(), P(), P()),
        check_vma=False,
    )
```

time: 272 us -> 89.9 us (0.33)
  waiting for transfers between devices: 131 us -> 34 us
  matrix products: 47.6 us -> 0 us
  local copies, waits for them, and re-layouts: 23.2 us -> 6.01 us
  between operations: 15.7 us -> 1.69 us
  other arithmetic: 20.2 us -> 10.2 us
  Pallas kernels: 0 us -> 9.3 us
  loops' own time: 5.08 us -> 0 us
    psum x1 -> x0, waiting for transfers between devices: 116 us -> none  [body(): grand = lax.psum(totals, ('tx', 'ty', 'pa'))]
    dot_general x32 -> x0, matrix products: 47.6 us -> none  [matmul(): jnp.dot(left, right, precision=lax.Precision.HIGHEST, preferred_element_t...]
    ppermute x8 -> x17, waiting for transfers between devices: 14.9 us -> 34 us  [the longest x8 28.6 us: partner_swap(): return lax.ppermute(value, MESH_AXES, moves)]
    dynamic_update_slice x2 -> x0, local copies, waits for them, and re-layouts: 16.6 us -> none  [step(): lax.dynamic_update_slice(accum, current + obj_terms, (zero, row, col))]
    add x11 -> x14, other arithmetic: 16 us -> 4.47 us  [the longest x6 1.68 us: body(): sums, live = (kept + got, live + got_live)]
    pallas_call x0 -> x1, Pallas kernels: none -> 9.3 us  [update(): pl.pallas_call(update_kernel, out_shape=(jax.ShapeDtypeStruct((3, side, s...]
    another operation x1 -> x0, loops' own time: 5.08 us -> none  [body(): accum, totals = lax.fori_loop(0, counts[0], step, (accum0, totals0))]
    ppermute x8 -> x17, starting transfers between devices: 27.4 us -> 28 us  [the longest x8 13.9 us: partner_swap(): return lax.ppermute(value, MESH_AXES, moves)]
  transfers between devices with their start and end apart: 10 -> 17, of which waited for: 7 -> 12; matrix products, arithmetic and copies ran while one was open for 3% -> 5% of each run, Pallas kernels for 0% -> 0%
where the time goes in v1:
time: 89.9 us; the launch traced here: 89.3 us
  waiting for transfers between devices  34 us (38%)
  starting transfers between devices  28 us (31%)
  other arithmetic  10.2 us (11%)
  Pallas kernels  9.3 us (10%)
  local copies, waits for them, and re-layouts  6.01 us (7%)
  between operations  1.69 us (2%)
    ppermute x8, waiting for transfers between devices, partner_swap(): return lax.ppermute(value, MESH_AXES, moves)  28.6 us
    ppermute x8, starting transfers between devices, partner_swap(): return lax.ppermute(value, MESH_AXES, moves)  13.9 us
    ppermute x8, starting transfers between devices, neighbour_swap(): return lax.ppermute(value, axis, pairs(lax.axis_size(axis), parity))  12.6 us
    pallas_call x1, Pallas kernels, update(): pl.pallas_call(update_kernel, out_shape=(jax.ShapeDtypeStruct((3, side, s...  9.3 us
    ppermute x8, waiting for transfers between devices, neighbour_swap(): return lax.ppermute(value, axis, pairs(lax.axis_size(axis), parity))  4.55 us
    unnamed x30, local copies, waits for them, and re-layouts  2.76 us
    slice x6, local copies, waits for them, and re-layouts, unpack(): return (flat[:-8].reshape(kinds, -1, window), flat[-8:])  2.18 us
  transfers between devices with their start and end apart: 17, of which 12 were waited for; matrix products, arithmetic and copies ran while one was open for 5% of the time, Pallas kernels for 0%

profile of v1, /device:TPU:0, one launch (start us, length us, event | category | flops | bytes accessed | tf_op | source)
XLA Modules:
  0.0 89.3 jit_solution(2153073247155855265)
XLA Ops:
  0.6 0.9 pad_maximum_fusion.9
  1.5 0.7 collective-permute-start
  2.2 5.9 %collective-permute-start.1 = (f32[2,128,128]{2,1,0:T(8,128)S(1)}, f32[2,128,128]{2,1,0:T(8,128)S(1)}, u32[]{:S(2)}, u32[]{:S(2)}) collective-permute-start(f32[2,128,128]{2,1,0:T(8,128)S(1)} %pad_maximum_fusion.9), channel_id=1, source_target_pairs={{0,8},{8,0},{16,24},{24,16},{1,9},{9,1},{17,25},{25,17},{2,10},{10... | collective-permute-start | bytes 393224 | tf_op jit(solution)/shard_map/ppermute | solution.py:25
  8.1 3.2 %collective-permute-done.1 = f32[2,128,128]{2,1,0:T(8,128)S(1)} collective-permute-done((f32[2,128,128]{2,1,0:T(8,128)S(1)}, f32[2,128,128]{2,1,0:T(8,128)S(1)}, u32[]{:S(2)}, u32[]{:S(2)}) %collective-permute-start.1) | collective-permute-done | bytes 131104 | tf_op jit(solution)/shard_map/ppermute | solution.py:25
  11.4 0.9 %pad_maximum_fusion.3 = f32[2,384,128]{2,1,0:T(8,128)S(1)} fusion(f32[2,128,128]{2,1,0:T(8,128)S(1)} %get-tuple-element.27, f32[1,128,128]{2,1,0:T(8,128)} %bitcast.69, f32[1,128,128]{2,1,0:T(8,128)} %bitcast.73, f32[2,128,128]{2,1,0:T(8,128)S(1)} %get-tuple-element.26), kind=kLoop, calls=%fused_computation.13 | loop fusion | flops 294912 | bytes 786432 | tf_op jit(solution)/shard_map/concatenate | solution.py:280
  12.3 0.7 collective-permute-start.2
  13.0 2.9 %collective-permute-start.3 = (f32[2,384,128]{2,1,0:T(8,128)S(1)}, f32[2,384,128]{2,1,0:T(8,128)S(1)}, u32[]{:S(2)}, u32[]{:S(2)}) collective-permute-start(f32[2,384,128]{2,1,0:T(8,128)S(1)} %pad_maximum_fusion.3), channel_id=1, source_target_pairs={{0,2},{2,0},{4,6},{6,4},{1,3},{3,1},{5,7},{7,5},{8,10},{10,8},{12,... | collective-permute-start | bytes 1179656 | tf_op jit(solution)/shard_map/ppermute | solution.py:25
  16.7 0.6 collective-permute-done.3
  17.6 0.8 copy-done.4
  18.7 0.2 copy-done
  18.8 0.2 copy-done.1
  19.0 0.2 copy-done.2
  19.2 0.2 copy-done.3
  19.4 9.3 %shard_map.181 = (f32[3,384,384]{2,1,0:T(8,128)S(1)}, f32[6,256,256]{2,1,0:T(8,128)S(1)}) custom-call(s32[2,2]{1,0:T(2,128)S(1)} %broadcast_subtract_fusion.offsets, s32[1]{0:T(128)S(6)} %copy.20.live_count, f32[2,384,384]{2,1,0:T(8,128)S(1)} %pad_maximum_fusion.padded, f32[256,256]{1,0:T(8,128)S(1)} %copy-done.5, f32[256,256]{1,0:T(8,128)S(1)} %copy-done.6, ...), custom_call_target="tpu_custom_call" | custom-call | tf_op jit(solution)/shard_map/pallas_call | solution.py:196
  28.8 0.9 %concatenate.32 = f32[776,256]{1,0:T(8,128)} pad(f32[768,256]{1,0:T(8,128)S(1)} %bitcast.63, f32[]{:T(128)} %bitcast.7), padding=0_8x0_0 | pad | bytes 1581060 | tf_op jit(solution)/shard_map/concatenate | solution.py:303
  29.7 4.0 %collective-permute-start.9 = (f32[776,256]{1,0:T(8,128)}, f32[776,256]{1,0:T(8,128)}, u32[]{:S(2)}, u32[]{:S(2)}) collective-permute-start(f32[776,256]{1,0:T(8,128)} %concatenate.32), channel_id=1, source_target_pairs={{0,2},{1,3},{2,0},{3,1},{4,6},{5,7},{6,4},{7,5},{8,10},{9,11},{10,... | collective-permute-start | bytes 2383880 | tf_op jit(solution)/shard_map/ppermute | solution.py:223
  33.8 2.3 %collective-permute-done.9 = f32[776,256]{1,0:T(8,128)} collective-permute-done((f32[776,256]{1,0:T(8,128)}, f32[776,256]{1,0:T(8,128)}, u32[]{:S(2)}, u32[]{:S(2)}) %collective-permute-start.9) | collective-permute-done | bytes 794656 | tf_op jit(solution)/shard_map/ppermute | solution.py:223
  36.0 1.2 %slice.138 = f32[768,256]{1,0:T(8,128)S(1)} slice(f32[776,256]{1,0:T(8,128)} %collective-permute-done.9), slice={[0:768], [0:256]} | slice | bytes 1572864 | tf_op jit(solution)/shard_map/slice | solution.py:306
  37.2 0.1 dynamic-slice_add_fusion
  37.3 0.9 copy-done.10
  38.2 0.8 slice_add_fusion.7
  39.0 0.8 pad_maximum_fusion.2
  39.8 1.5 %collective-permute-start.10 = (f32[392,256]{1,0:T(8,128)}, f32[392,256]{1,0:T(8,128)S(1)}, u32[]{:S(2)}, u32[]{:S(2)}) collective-permute-start(f32[392,256]{1,0:T(8,128)} %pad_maximum_fusion.2), channel_id=1, source_target_pairs={{0,1},{1,0},{2,6},{3,7},{4,5},{5,4},{6,2},{7,3},{8,9},{9,8},{10,14... | collective-permute-start | bytes 1204232 | tf_op jit(solution)/shard_map/ppermute | solution.py:223
  41.3 6.6 %collective-permute-done.10 = f32[392,256]{1,0:T(8,128)S(1)} collective-permute-done((f32[392,256]{1,0:T(8,128)}, f32[392,256]{1,0:T(8,128)S(1)}, u32[]{:S(2)}, u32[]{:S(2)}) %collective-permute-start.10) | collective-permute-done | bytes 401440 | tf_op jit(solution)/shard_map/ppermute | solution.py:223
  48.0 0.7 slice_add_fusion.6
  48.7 2.1 %collective-permute-start.11 = (f32[200,256]{1,0:T(8,128)S(1)}, f32[200,256]{1,0:T(8,128)S(1)}, u32[]{:S(2)}, u32[]{:S(2)}) collective-permute-start(f32[200,256]{1,0:T(8,128)S(1)} %pad_maximum_fusion.6), channel_id=1, source_target_pairs={{0,4},{1,5},{2,3},{3,2},{4,0},{5,1},{6,7},{7,6},{8,12},{9,13},{10,... | collective-permute-start | bytes 614408 | tf_op jit(solution)/shard_map/ppermute | solution.py:223
  51.0 1.5 %collective-permute-start.4 = (f32[3,384,128]{2,1,0:T(8,128)S(1)}, f32[3,384,128]{2,1,0:T(8,128)}, u32[]{:S(2)}, u32[]{:S(2)}) collective-permute-start(f32[3,384,128]{2,1,0:T(8,128)S(1)} %get-tuple-element.10), channel_id=1, source_target_pairs={{2,4},{4,2},{3,5},{5,3},{10,12},{12,10},{11,13},{13,11},{18,20},{2... | collective-permute-start | bytes 1769480 | tf_op jit(solution)/shard_map/ppermute | solution.py:25
  52.5 2.1 %collective-permute-done.11 = f32[200,256]{1,0:T(8,128)S(1)} collective-permute-done((f32[200,256]{1,0:T(8,128)S(1)}, f32[200,256]{1,0:T(8,128)S(1)}, u32[]{:S(2)}, u32[]{:S(2)}) %collective-permute-start.11) | collective-permute-done | bytes 204832 | tf_op jit(solution)/shard_map/ppermute | solution.py:223
  54.6 0.7 pad_maximum_fusion.7
  55.3 1.8 %collective-permute-start.12 = (f32[200,256]{1,0:T(8,128)}, f32[200,256]{1,0:T(8,128)}, u32[]{:S(2)}, u32[]{:S(2)}) collective-permute-start(f32[200,256]{1,0:T(8,128)} %pad_maximum_fusion.7), channel_id=1, source_target_pairs={{0,8},{1,9},{2,10},{3,11},{4,12},{5,13},{6,14},{7,15},{8,0},{9,1},... | collective-permute-start | bytes 614408 | tf_op jit(solution)/shard_map/ppermute | solution.py:223
  57.1 4.5 %collective-permute-done.12 = f32[200,256]{1,0:T(8,128)} collective-permute-done((f32[200,256]{1,0:T(8,128)}, f32[200,256]{1,0:T(8,128)}, u32[]{:S(2)}, u32[]{:S(2)}) %collective-permute-start.12) | collective-permute-done | bytes 204832 | tf_op jit(solution)/shard_map/ppermute | solution.py:223
  61.5 0.9 %slice.144 = f32[192,256]{1,0:T(8,128)S(1)} slice(f32[200,256]{1,0:T(8,128)} %collective-permute-done.12), slice={[0:192], [0:256]} | slice | bytes 393216 | tf_op jit(solution)/shard_map/slice | solution.py:306
  62.5 0.7 slice_add_fusion.4
  63.2 1.7 %collective-permute-start.13 = (f32[200,256]{1,0:T(8,128)S(1)}, f32[200,256]{1,0:T(8,128)S(1)}, u32[]{:S(2)}, u32[]{:S(2)}) collective-permute-start(f32[200,256]{1,0:T(8,128)S(1)} %pad_maximum_fusion.8), channel_id=1, source_target_pairs={{0,16},{1,17},{2,18},{3,19},{4,20},{5,21},{6,22},{7,23},{8,24},{9,... | collective-permute-start | bytes 614408 | tf_op jit(solution)/shard_map/ppermute | solution.py:223
  64.9 1.3 %add_add_fusion = f32[3,384,128]{2,1,0:T(8,128)S(1)} fusion(f32[3,384,128]{2,1,0:T(8,128)} %collective-permute-done.5, f32[3,384,128]{2,1,0:T(8,128)} %collective-permute-done.4, f32[3,384,384]{2,1,0:T(8,128)S(1)} %get-tuple-element.8), kind=kLoop, calls=%fused_computation.8 | loop fusion | flops 294912 | bytes 2359296 | tf_op jit(solution)/shard_map/add | solution.py:349
  66.3 7.4 %collective-permute-done.13 = f32[200,256]{1,0:T(8,128)S(1)} collective-permute-done((f32[200,256]{1,0:T(8,128)S(1)}, f32[200,256]{1,0:T(8,128)S(1)}, u32[]{:S(2)}, u32[]{:S(2)}) %collective-permute-start.13) | collective-permute-done | bytes 204832 | tf_op jit(solution)/shard_map/ppermute | solution.py:223
  73.7 0.9 fusion.22
  74.6 1.4 %collective-permute-start.14 = (f32[4,32,256]{2,1,0:T(8,128)S(1)}, f32[4,32,256]{2,1,0:T(8,128)S(1)}, u32[]{:S(2)}, u32[]{:S(2)}) collective-permute-start(f32[4,32,256]{2,1,0:T(8,128)S(1)} %pad_maximum_fusion.10), channel_id=1, source_target_pairs={{0,4},{1,5},{2,3},{3,2},{4,0},{5,1},{6,7},{7,6},{8,12},{9,13},{10,... | collective-permute-start | bytes 393224 | tf_op jit(solution)/shard_map/ppermute | solution.py:223
  76.1 0.7 collective-permute-start.6
  76.8 2.8 %collective-permute-done.14 = f32[4,32,256]{2,1,0:T(8,128)S(1)} collective-permute-done((f32[4,32,256]{2,1,0:T(8,128)S(1)}, f32[4,32,256]{2,1,0:T(8,128)S(1)}, u32[]{:S(2)}, u32[]{:S(2)}) %collective-permute-start.14) | collective-permute-done | bytes 131104 | tf_op jit(solution)/shard_map/ppermute | solution.py:223
  79.7 1.4 %collective-permute-start.15 = (f32[4,64,256]{2,1,0:T(8,128)S(1)}, f32[4,64,256]{2,1,0:T(8,128)S(1)}, u32[]{:S(2)}, u32[]{:S(2)}) collective-permute-start(f32[4,64,256]{2,1,0:T(8,128)S(1)} %pad_maximum_fusion.5), channel_id=1, source_target_pairs={{0,1},{1,0},{2,6},{3,7},{4,5},{5,4},{6,2},{7,3},{8,9},{9,8},{10,14... | collective-permute-start | bytes 786440 | tf_op jit(solution)/shard_map/ppermute | solution.py:223
  81.1 0.7 collective-permute-done.7
  81.9 1.6 %collective-permute-start.8 = (f32[3,64,128]{2,1,0:T(8,128)S(1)}, f32[3,64,128]{2,1,0:T(8,128)S(1)}, u32[]{:S(2)}, u32[]{:S(2)}) collective-permute-start(f32[3,64,128]{2,1,0:T(8,128)S(1)} %constant_dynamic-slice_fusion.3), channel_id=1, source_target_pairs={{0,1},{1,0},{2,3},{3,2},{4,5},{5,4},{6,7},{7,6},{8,9},{9,8},{10,11... | collective-permute-start | bytes 294920 | tf_op jit(solution)/shard_map/ppermute | solution.py:362
  83.4 2.7 %collective-permute-done.15 = f32[4,64,256]{2,1,0:T(8,128)S(1)} collective-permute-done((f32[4,64,256]{2,1,0:T(8,128)S(1)}, f32[4,64,256]{2,1,0:T(8,128)S(1)}, u32[]{:S(2)}, u32[]{:S(2)}) %collective-permute-start.15) | collective-permute-done | bytes 262176 | tf_op jit(solution)/shard_map/ppermute | solution.py:223
  86.3 0.9 collective-permute-done.8
  87.2 0.6 fusion.24
  87.8 0.4 collective-permute-done.16
  88.3 1.0 %fusion.6 = (f32[256,256]{1,0:T(8,128)}, f32[256,256]{1,0:T(8,128)}, f32[256,256]{1,0:T(8,128)}, f32[256,256]{1,0:T(8,128)}) fusion(f32[4,128,256]{2,1,0:T(8,128)S(1)} %get-tuple-element.16, f32[4,128,256]{2,1,0:T(8,128)S(1)} %get-tuple-element.17), kind=kLoop, calls=%fused_computation.22 | loop fusion | flops 262144 | bytes 2097152 | tf_op jit(solution)/shard_map/squeeze | solution.py:367
  (64 shorter events, 1.7 us)
Async XLA Ops:
  0.6 16.1 %copy-start.14 = (s32[2,2]{1,0:T(2,128)S(1)}, s32[2,2]{1,0:T(2,128)}, u32[]{:S(2)}) copy-start(s32[2,2]{1,0:T(2,128)} %param.21) | copy-start | bytes 52
  1.5 6.6 %collective-permute-start = (f32[2,128,128]{2,1,0:T(8,128)S(1)}, f32[2,128,128]{2,1,0:T(8,128)S(1)}, u32[]{:S(2)}, u32[]{:S(2)}) collective-permute-start(f32[2,128,128]{2,1,0:T(8,128)S(1)} %pad_maximum_fusion.9), channel_id=1, source_target_pairs={{8,16},{16,8},{9,17},{17,9},{10,18},{18,10},{11,19},{19,11},{12,20... | collective-permute-start | bytes 393224 | tf_op jit(solution)/shard_map/ppermute | solution.py:25
  2.2 9.2 %collective-permute-start.1 = (f32[2,128,128]{2,1,0:T(8,128)S(1)}, f32[2,128,128]{2,1,0:T(8,128)S(1)}, u32[]{:S(2)}, u32[]{:S(2)}) collective-permute-start(f32[2,128,128]{2,1,0:T(8,128)S(1)} %pad_maximum_fusion.9), channel_id=1, source_target_pairs={{0,8},{8,0},{16,24},{24,16},{1,9},{9,1},{17,25},{25,17},{2,10},{10... | collective-permute-start | bytes 393224 | tf_op jit(solution)/shard_map/ppermute | solution.py:25
  11.4 6.0 %copy-start.12 = (f32[128,128]{1,0:T(8,128)S(1)}, f32[128,128]{1,0:T(8,128)}, u32[]{:S(2)}) copy-start(f32[128,128]{1,0:T(8,128)} %param.15) | copy-start | bytes 196612
  11.4 6.0 %copy-start.13 = (f32[128,128]{1,0:T(8,128)S(1)}, f32[128,128]{1,0:T(8,128)}, u32[]{:S(2)}) copy-start(f32[128,128]{1,0:T(8,128)} %param.14) | copy-start | bytes 196612
  12.3 4.4 %collective-permute-start.2 = (f32[2,384,128]{2,1,0:T(8,128)S(1)}, f32[2,384,128]{2,1,0:T(8,128)S(1)}, u32[]{:S(2)}, u32[]{:S(2)}) collective-permute-start(f32[2,384,128]{2,1,0:T(8,128)S(1)} %pad_maximum_fusion.3), channel_id=1, source_target_pairs={{2,4},{4,2},{3,5},{5,3},{10,12},{12,10},{11,13},{13,11},{18,20},{2... | collective-permute-start | bytes 1179656 | tf_op jit(solution)/shard_map/ppermute | solution.py:25
  13.0 4.3 %collective-permute-start.3 = (f32[2,384,128]{2,1,0:T(8,128)S(1)}, f32[2,384,128]{2,1,0:T(8,128)S(1)}, u32[]{:S(2)}, u32[]{:S(2)}) collective-permute-start(f32[2,384,128]{2,1,0:T(8,128)S(1)} %pad_maximum_fusion.3), channel_id=1, source_target_pairs={{0,2},{2,0},{4,6},{6,4},{1,3},{3,1},{5,7},{7,5},{8,10},{10,8},{12,... | collective-permute-start | bytes 1179656 | tf_op jit(solution)/shard_map/ppermute | solution.py:25
  17.3 1.0 %copy-start.4 = (bf16[512,512]{1,0:T(8,128)(2,1)S(1)}, bf16[512,512]{1,0:T(8,128)(2,1)}, u32[]{:S(2)}) copy-start(bf16[512,512]{1,0:T(8,128)(2,1)} %constant.87.clone.col_low) | copy-start | bytes 1572868
  17.3 1.1 %copy-start.6 = (f32[256,256]{1,0:T(8,128)S(1)}, f32[256,256]{1,0:T(8,128)}, u32[]{:S(2)}) copy-start(f32[256,256]{1,0:T(8,128)} %probe_im.1) | copy-start | bytes 786436
  17.3 1.2 %copy-start.7 = (f32[256,256]{1,0:T(8,128)S(1)}, f32[256,256]{1,0:T(8,128)}, u32[]{:S(2)}) copy-start(f32[256,256]{1,0:T(8,128)} %gain.1) | copy-start | bytes 786436
  17.3 1.3 %copy-start.8 = (f32[256,256]{1,0:T(8,128)S(1)}, f32[256,256]{1,0:T(8,128)}, u32[]{:S(2)}) copy-start(f32[256,256]{1,0:T(8,128)} %dark.1) | copy-start | bytes 786436
  17.3 1.3 %copy-start.9 = (s32[256,256]{1,0:T(8,128)S(1)}, s32[256,256]{1,0:T(8,128)}, u32[]{:S(2)}) copy-start(s32[256,256]{1,0:T(8,128)} %good.1) | copy-start | bytes 786436
  17.4 1.4 %copy-start = (f32[2,256,256]{2,1,0:T(8,128)S(1)}, f32[2,256,256]{2,1,0:T(8,128)}, u32[]{:S(2)}) copy-start(f32[2,256,256]{2,1,0:T(8,128)} %measured.1) | copy-start | bytes 1572868
  17.4 1.6 %copy-start.1 = (bf16[512,512]{1,0:T(8,128)(2,1)S(1)}, bf16[512,512]{1,0:T(8,128)(2,1)}, u32[]{:S(2)}) copy-start(bf16[512,512]{1,0:T(8,128)(2,1)} %constant.84.clone.row_high) | copy-start | bytes 1572868
  17.4 1.7 %copy-start.2 = (bf16[512,512]{1,0:T(8,128)(2,1)S(1)}, bf16[512,512]{1,0:T(8,128)(2,1)}, u32[]{:S(2)}) copy-start(bf16[512,512]{1,0:T(8,128)(2,1)} %constant.85.clone.row_low) | copy-start | bytes 1572868
  17.4 1.9 %copy-start.3 = (bf16[512,512]{1,0:T(8,128)(2,1)S(1)}, bf16[512,512]{1,0:T(8,128)(2,1)}, u32[]{:S(2)}) copy-start(bf16[512,512]{1,0:T(8,128)(2,1)} %constant.86.clone.col_high) | copy-start | bytes 1572868
  17.5 1.9 %copy-start.5 = (f32[256,256]{1,0:T(8,128)S(1)}, f32[256,256]{1,0:T(8,128)}, u32[]{:S(2)}) copy-start(f32[256,256]{1,0:T(8,128)} %probe_re.1) | copy-start | bytes 786436
  29.7 6.3 %collective-permute-start.9 = (f32[776,256]{1,0:T(8,128)}, f32[776,256]{1,0:T(8,128)}, u32[]{:S(2)}, u32[]{:S(2)}) collective-permute-start(f32[776,256]{1,0:T(8,128)} %concatenate.32), channel_id=1, source_target_pairs={{0,2},{1,3},{2,0},{3,1},{4,6},{5,7},{6,4},{7,5},{8,10},{9,11},{10,... | collective-permute-start | bytes 2383880 | tf_op jit(solution)/shard_map/ppermute | solution.py:223
  37.3 0.9 copy-start.10
  38.2 9.7 %copy-start.11 = (f32[6,128,256]{2,1,0:T(8,128)S(1)}, f32[6,128,256]{2,1,0:T(8,128)}, u32[]{:S(2)}) copy-start(f32[6,128,256]{2,1,0:T(8,128)} %copy-done.10) | copy-start | bytes 2359300
  39.8 8.1 %collective-permute-start.10 = (f32[392,256]{1,0:T(8,128)}, f32[392,256]{1,0:T(8,128)S(1)}, u32[]{:S(2)}, u32[]{:S(2)}) collective-permute-start(f32[392,256]{1,0:T(8,128)} %pad_maximum_fusion.2), channel_id=1, source_target_pairs={{0,1},{1,0},{2,6},{3,7},{4,5},{5,4},{6,2},{7,3},{8,9},{9,8},{10,14... | collective-permute-start | bytes 1204232 | tf_op jit(solution)/shard_map/ppermute | solution.py:223
  48.7 5.8 %collective-permute-start.11 = (f32[200,256]{1,0:T(8,128)S(1)}, f32[200,256]{1,0:T(8,128)S(1)}, u32[]{:S(2)}, u32[]{:S(2)}) collective-permute-start(f32[200,256]{1,0:T(8,128)S(1)} %pad_maximum_fusion.6), channel_id=1, source_target_pairs={{0,4},{1,5},{2,3},{3,2},{4,0},{5,1},{6,7},{7,6},{8,12},{9,13},{10,... | collective-permute-start | bytes 614408 | tf_op jit(solution)/shard_map/ppermute | solution.py:223
  50.9 14.1 %collective-permute-start.5 = (f32[3,384,128]{2,1,0:T(8,128)S(1)}, f32[3,384,128]{2,1,0:T(8,128)}, u32[]{:S(2)}, u32[]{:S(2)}) collective-permute-start(f32[3,384,128]{2,1,0:T(8,128)S(1)} %get-tuple-element.11), channel_id=1, source_target_pairs={{0,2},{2,0},{4,6},{6,4},{1,3},{3,1},{5,7},{7,5},{8,10},{10,8},{12,... | collective-permute-start | bytes 1769480 | tf_op jit(solution)/shard_map/ppermute | solution.py:25
  51.0 14.0 %collective-permute-start.4 = (f32[3,384,128]{2,1,0:T(8,128)S(1)}, f32[3,384,128]{2,1,0:T(8,128)}, u32[]{:S(2)}, u32[]{:S(2)}) collective-permute-start(f32[3,384,128]{2,1,0:T(8,128)S(1)} %get-tuple-element.10), channel_id=1, source_target_pairs={{2,4},{4,2},{3,5},{5,3},{10,12},{12,10},{11,13},{13,11},{18,20},{2... | collective-permute-start | bytes 1769480 | tf_op jit(solution)/shard_map/ppermute | solution.py:25
  55.3 6.2 %collective-permute-start.12 = (f32[200,256]{1,0:T(8,128)}, f32[200,256]{1,0:T(8,128)}, u32[]{:S(2)}, u32[]{:S(2)}) collective-permute-start(f32[200,256]{1,0:T(8,128)} %pad_maximum_fusion.7), channel_id=1, source_target_pairs={{0,8},{1,9},{2,10},{3,11},{4,12},{5,13},{6,14},{7,15},{8,0},{9,1},... | collective-permute-start | bytes 614408 | tf_op jit(solution)/shard_map/ppermute | solution.py:223
  63.2 10.4 %collective-permute-start.13 = (f32[200,256]{1,0:T(8,128)S(1)}, f32[200,256]{1,0:T(8,128)S(1)}, u32[]{:S(2)}, u32[]{:S(2)}) collective-permute-start(f32[200,256]{1,0:T(8,128)S(1)} %pad_maximum_fusion.8), channel_id=1, source_target_pairs={{0,16},{1,17},{2,18},{3,19},{4,20},{5,21},{6,22},{7,23},{8,24},{9,... | collective-permute-start | bytes 614408 | tf_op jit(solution)/shard_map/ppermute | solution.py:223
  74.6 5.0 %collective-permute-start.14 = (f32[4,32,256]{2,1,0:T(8,128)S(1)}, f32[4,32,256]{2,1,0:T(8,128)S(1)}, u32[]{:S(2)}, u32[]{:S(2)}) collective-permute-start(f32[4,32,256]{2,1,0:T(8,128)S(1)} %pad_maximum_fusion.10), channel_id=1, source_target_pairs={{0,4},{1,5},{2,3},{3,2},{4,0},{5,1},{6,7},{7,6},{8,12},{9,13},{10,... | collective-permute-start | bytes 393224 | tf_op jit(solution)/shard_map/ppermute | solution.py:223
  76.1 5.7 %collective-permute-start.7 = (f32[3,128,128]{2,1,0:T(8,128)S(1)}, f32[3,128,128]{2,1,0:T(8,128)S(1)}, u32[]{:S(2)}, u32[]{:S(2)}) collective-permute-start(f32[3,128,128]{2,1,0:T(8,128)S(1)} %get-tuple-element.21), channel_id=1, source_target_pairs={{0,8},{8,0},{16,24},{24,16},{1,9},{9,1},{17,25},{25,17},{2,10},{10... | collective-permute-start | bytes 589832 | tf_op jit(solution)/shard_map/ppermute | solution.py:25
  76.1 5.7 %collective-permute-start.6 = (f32[3,128,128]{2,1,0:T(8,128)S(1)}, f32[3,128,128]{2,1,0:T(8,128)S(1)}, u32[]{:S(2)}, u32[]{:S(2)}) collective-permute-start(f32[3,128,128]{2,1,0:T(8,128)S(1)} %get-tuple-element.20), channel_id=1, source_target_pairs={{8,16},{16,8},{9,17},{17,9},{10,18},{18,10},{11,19},{19,11},{12,20... | collective-permute-start | bytes 589832 | tf_op jit(solution)/shard_map/ppermute | solution.py:25
  79.7 6.4 %collective-permute-start.15 = (f32[4,64,256]{2,1,0:T(8,128)S(1)}, f32[4,64,256]{2,1,0:T(8,128)S(1)}, u32[]{:S(2)}, u32[]{:S(2)}) collective-permute-start(f32[4,64,256]{2,1,0:T(8,128)S(1)} %pad_maximum_fusion.5), channel_id=1, source_target_pairs={{0,1},{1,0},{2,6},{3,7},{4,5},{5,4},{6,2},{7,3},{8,9},{9,8},{10,14... | collective-permute-start | bytes 786440 | tf_op jit(solution)/shard_map/ppermute | solution.py:223
  81.9 5.3 %collective-permute-start.8 = (f32[3,64,128]{2,1,0:T(8,128)S(1)}, f32[3,64,128]{2,1,0:T(8,128)S(1)}, u32[]{:S(2)}, u32[]{:S(2)}) collective-permute-start(f32[3,64,128]{2,1,0:T(8,128)S(1)} %constant_dynamic-slice_fusion.3), channel_id=1, source_target_pairs={{0,1},{1,0},{2,3},{3,2},{4,5},{5,4},{6,7},{7,6},{8,9},{9,8},{10,11... | collective-permute-start | bytes 294920 | tf_op jit(solution)/shard_map/ppermute | solution.py:362
  86.2 2.0 %collective-permute-start.16 = (f32[4,128,256]{2,1,0:T(8,128)S(1)}, f32[4,128,256]{2,1,0:T(8,128)S(1)}, u32[]{:S(2)}, u32[]{:S(2)}) collective-permute-start(f32[4,128,256]{2,1,0:T(8,128)S(1)} %pad_maximum_fusion.1), channel_id=1, source_target_pairs={{0,2},{1,3},{2,0},{3,1},{4,6},{5,7},{6,4},{7,5},{8,10},{9,11},{10,... | collective-permute-start | bytes 1572872 | tf_op jit(solution)/shard_map/ppermute | solution.py:223

commit v2 on v1

v2 whole, which is shorter than its diff:
```python
import functools
import math

import jax
import jax.numpy as jnp
import numpy as np
from jax import lax
from jax.experimental import pallas as pl
from jax.experimental.pallas import tpu as pltpu
from jax.sharding import PartitionSpec as P


MESH_AXES = ("tx", "ty", "pa")
ROWS = 32
SUBLANES = 8


def partner_swap(value, partner_of):
    shape = tuple(lax.axis_size(axis) for axis in MESH_AXES)
    moves = []
    for here in np.ndindex(*shape):
        there = partner_of(*here)
        if there != here:
            source, target = (int(np.ravel_multi_index(at, shape)) for at in (here, there))
            moves.append((source, target))
    return lax.ppermute(value, MESH_AXES, moves)


def neighbour_swap(value, axis, parity):
    dim = MESH_AXES.index(axis)
    size = lax.axis_size(axis)
    n_pa = lax.axis_size("pa")

    def paired(at):
        other = (at - parity ^ 1) + parity
        return other if 0 <= other < size else None

    def partner(*here):
        other = paired(here[dim])
        if other is None:
            idle = here[2] ^ 1
            return (here[0], here[1], idle if idle < n_pa else here[2])
        return tuple(other if k == dim else at for k, at in enumerate(here))

    got = partner_swap(value, partner)
    if all(paired(at) is not None for at in range(size)):
        return got
    other = (lax.axis_index(axis) - parity ^ 1) + parity
    return jnp.where((0 <= other) & (other < size), got, 0.0)


def ordered(parity, first, second):
    even = parity == 0
    return jnp.where(even, first, second), jnp.where(even, second, first)


def split_table(table):
    high = table.astype(jnp.bfloat16)
    low = (table - high.astype(np.float32)).astype(jnp.bfloat16)
    return high, low


def dft_tables(size):
    index = np.arange(size)
    angle = (np.outer(index, index) % size) * (2.0 * math.pi / size)
    real = (np.cos(angle) / math.sqrt(size)).astype(np.float32)
    imag = (-np.sin(angle) / math.sqrt(size)).astype(np.float32)
    row_form = np.block([[real, imag], [-imag, real]])
    col_form = np.block([[real, -imag], [imag, real]])
    return (*split_table(row_form), *split_table(col_form))


def split(value):
    high = value.astype(jnp.bfloat16)
    return high, (value - high.astype(jnp.float32)).astype(jnp.bfloat16)


def three_pass(left_high, left_low, right_high, right_low):
    dot = functools.partial(jnp.dot, preferred_element_type=jnp.float32)
    return dot(left_high, right_high) + dot(left_high, right_low) + dot(left_low, right_high)


def aligned(row):
    part = lax.rem(row, SUBLANES)
    return row - part, part


def right_then_left(first_high, first_low, second_high, second_low, x_high, x_low, y_high, y_low, line, plane):
    slots, _, size = plane.shape
    for slot in range(slots):
        here = pl.ds(slot * size, size)
        line[...] = three_pass(x_high[here, :], x_low[here, :], first_high[...], first_low[...])
        for part in range(2):
            high, low = split(line[:, part * size : (part + 1) * size])
            y_high[part * size : (part + 1) * size, here] = high
            y_low[part * size : (part + 1) * size, here] = low
        plane[slot] = three_pass(second_high[...], second_low[...], y_high[:, here], y_low[:, here])


def put_x(x_high, x_low, slot, size, at, real, imag):
    rows = pl.ds(slot * size + at, ROWS)
    for part, value in enumerate((real, imag)):
        high, low = split(value)
        x_high[rows, part * size : (part + 1) * size] = high
        x_low[rows, part * size : (part + 1) * size] = low


def put_sums(sums, info, step, values):
    blocks, _, size = sums.shape
    span = size // blocks
    half = blocks // 2
    for sub in range(ROWS // span):
        block = step * (ROWS // span) + sub
        mine = lax.bitwise_xor(block, info[1])
        place = jnp.where(mine < half, mine, half + lax.bitwise_xor(block, info[2]))
        for kind, value in enumerate(values):
            sums[place, kind * span : (kind + 1) * span, :] = value[sub * span : (sub + 1) * span]


def forward_kernel(
    offsets,
    info,
    padded,
    probe_re,
    probe_im,
    row_high,
    row_low,
    col_high,
    col_low,
    measured_hbm,
    gain_hbm,
    dark_hbm,
    good_hbm,
    kept,
    sent,
    x_high,
    x_low,
    win,
    sums,
    measured,
    gain,
    dark,
    good,
    sem,
    y_high,
    y_low,
    line,
    plane,
):
    slots = measured.shape[0]
    size = probe_re.shape[0]
    side = padded.shape[1]
    steps = size // ROWS
    copies = [
        pltpu.make_async_copy(source, target, sem.at[k])
        for k, (source, target) in enumerate(
            ((measured_hbm, measured), (gain_hbm, gain), (dark_hbm, dark), (good_hbm, good))
        )
    ]
    for copy in copies:
        copy.start()

    for slot in range(slots):
        row, row_part = aligned(offsets[slot, 0])
        back_rows = lax.rem(ROWS + SUBLANES - row_part, ROWS + SUBLANES)
        back_cols = lax.rem(side - offsets[slot, 1], side)

        def load(step, _):
            at = pl.multiple_of(step * ROWS, ROWS)
            here = pl.ds(at, ROWS)
            parts = []
            for part in range(2):
                band = padded[part, pl.ds(pl.multiple_of(row + at, SUBLANES), ROWS + SUBLANES), :]
                band = pltpu.roll(band, back_rows, axis=0)[:ROWS]
                parts.append(pltpu.roll(band, back_cols, axis=1)[:, :size])
                win[slot, part, here, :] = parts[part]
            wr, wi = parts
            pr, pi = probe_re[here, :], probe_im[here, :]
            put_x(x_high, x_low, slot, size, at, pr * wr - pi * wi, pr * wi + pi * wr)
            return 0

        lax.fori_loop(0, steps, load, 0)

    right_then_left(
        row_high, row_low, col_high, col_low, x_high, x_low, y_high, y_low, line, plane
    )
    for copy in copies:
        copy.wait()
    blocks, depth, _ = sums.shape
    live_rows = jnp.full((SUBLANES, size), info[0].astype(jnp.float32), jnp.float32)
    for block in range(blocks):
        sums[block, depth - SUBLANES :, :] = live_rows

    def detect(step, _):
        at = pl.multiple_of(step * ROWS, ROWS)
        here = pl.ds(at, ROWS)
        valid = good[here, :].astype(jnp.float32)
        values = [0.0] * 4
        for slot in range(slots):
            live = jnp.where(slot < info[0], 1.0, 0.0).astype(jnp.float32)
            fr = plane[slot, here, :]
            fi = plane[slot, pl.ds(size + at, ROWS), :]
            inten = fr * fr + fi * fi
            model = gain[here, :] * inten + dark[here, :]
            seen = measured[slot, here, :]
            ratio = valid * (jnp.sqrt(seen / model) - 1.0)
            put_x(x_high, x_low, slot, size, at, ratio * fr, ratio * fi)
            weight = valid * live
            resid = weight * (seen - model)
            wr, wi = win[slot, 0, here, :], win[slot, 1, here, :]
            terms = (live * (wr * wr + wi * wi), resid * inten, weight * inten * inten, resid)
            values = [value + term for value, term in zip(values, terms)]
        put_sums(sums, info, step, values)
        return 0

    lax.fori_loop(0, steps, detect, 0)
    kept[...] = sums[: blocks // 2]
    sent[...] = sums[blocks // 2 :]


def backward_kernel(
    offsets,
    info,
    x_high,
    x_low,
    win,
    probe_re,
    probe_im,
    row_high,
    row_low,
    col_high,
    col_low,
    kept,
    sent,
    to_one,
    inner,
    to_zero,
    sums,
    accum,
    y_high,
    y_low,
    line,
    plane,
):
    slots, _, size, _ = win.shape
    side = accum.shape[1]
    tile = inner.shape[2]
    half = to_one.shape[2]
    steps = size // ROWS
    accum[...] = jnp.zeros_like(accum)
    right_then_left(
        col_high, col_low, row_high, row_low, x_high, x_low, y_high, y_low, line, plane
    )

    def place(step, _):
        at = pl.multiple_of(step * ROWS, ROWS)
        here = pl.ds(at, ROWS)
        pr, pi = probe_re[here, :], probe_im[here, :]
        power = pr * pr + pi * pi
        values = [0.0] * 2
        for slot in range(slots):
            live = jnp.where(slot < info[0], 1.0, 0.0).astype(jnp.float32)
            row, row_part = aligned(offsets[slot, 0])
            col = offsets[slot, 1]
            br = live * plane[slot, here, :]
            bi = live * plane[slot, pl.ds(size + at, ROWS), :]
            wr, wi = win[slot, 0, here, :], win[slot, 1, here, :]
            values = [values[0] + wr * br + wi * bi, values[1] + wr * bi - wi * br]
            there = pl.ds(pl.multiple_of(row + at, SUBLANES), ROWS + SUBLANES)
            for part, term in enumerate((pr * br + pi * bi, pr * bi - pi * br, live * power)):
                wide = jnp.pad(term, ((0, SUBLANES), (0, side - size)))
                wide = pltpu.roll(pltpu.roll(wide, row_part, axis=0), col, axis=1)
                accum[part, there, :] += wide
        put_sums(sums, info, step, values)
        return 0

    lax.fori_loop(0, steps, place, 0)
    kept[...] = sums[: sums.shape[0] // 2]
    sent[...] = sums[sums.shape[0] // 2 :]
    odd = info[3] == 1
    inner[...] = accum[:, :, half : half + tile]

    @pl.when(odd)
    def _():
        to_one[...] = accum[:, :, half + tile :]
        to_zero[...] = accum[:, :, :half]

    @pl.when(jnp.logical_not(odd))
    def _():
        to_one[...] = accum[:, :, :half]
        to_zero[...] = accum[:, :, half + tile :]


SMEM = pl.BlockSpec(memory_space=pltpu.SMEM)
VMEM = pl.BlockSpec(memory_space=pltpu.VMEM)
ANY = pl.BlockSpec(memory_space=pl.ANY)


def work_buffers(slots, size):
    return [
        pltpu.VMEM((2 * size, slots * size), jnp.bfloat16),
        pltpu.VMEM((2 * size, slots * size), jnp.bfloat16),
        pltpu.VMEM((size, 2 * size), jnp.float32),
        pltpu.VMEM((slots, 2 * size, size), jnp.float32),
    ]


def kernel_options(slots, size):
    return dict(
        compiler_params=pltpu.CompilerParams(vmem_limit_bytes=24 * 1024 * 1024),
        cost_estimate=pl.CostEstimate(
            flops=slots * 48 * size**3, bytes_accessed=6 * 1024 * 1024, transcendentals=0
        ),
    )


def forward(offsets, info, padded, probe_re, probe_im, tables, measured, gain, dark, good, blocks):
    slots, size = measured.shape[:2]
    depth = 4 * (size // blocks) + SUBLANES
    return pl.pallas_call(
        forward_kernel,
        out_shape=(
            jax.ShapeDtypeStruct((blocks // 2, depth, size), jnp.float32),
            jax.ShapeDtypeStruct((blocks // 2, depth, size), jnp.float32),
            jax.ShapeDtypeStruct((slots * size, 2 * size), jnp.bfloat16),
            jax.ShapeDtypeStruct((slots * size, 2 * size), jnp.bfloat16),
            jax.ShapeDtypeStruct((slots, 2, size, size), jnp.float32),
        ),
        in_specs=[SMEM] * 2 + [VMEM] * 7 + [ANY] * 4,
        out_specs=(VMEM,) * 5,
        scratch_shapes=[
            pltpu.VMEM((blocks, depth, size), jnp.float32),
            pltpu.VMEM((slots, size, size), jnp.float32),
            pltpu.VMEM((size, size), jnp.float32),
            pltpu.VMEM((size, size), jnp.float32),
            pltpu.VMEM((size, size), jnp.int32),
            pltpu.SemaphoreType.DMA((4,)),
            *work_buffers(slots, size),
        ],
        name="forward",
        **kernel_options(slots, size),
    )(offsets, info, padded, probe_re, probe_im, *tables, measured, gain, dark, good)


def backward(offsets, info, x_high, x_low, win, probe_re, probe_im, tables, tile, blocks):
    slots, _, size, _ = win.shape
    half = size // 2
    side = tile + size
    depth = 2 * (size // blocks)
    return pl.pallas_call(
        backward_kernel,
        out_shape=(
            jax.ShapeDtypeStruct((blocks // 2, depth, size), jnp.float32),
            jax.ShapeDtypeStruct((blocks // 2, depth, size), jnp.float32),
            jax.ShapeDtypeStruct((3, side, half), jnp.float32),
            jax.ShapeDtypeStruct((3, side, tile), jnp.float32),
            jax.ShapeDtypeStruct((3, side, half), jnp.float32),
        ),
        in_specs=[SMEM] * 2 + [VMEM] * 9,
        out_specs=(VMEM,) * 5,
        scratch_shapes=[
            pltpu.VMEM((blocks, depth, size), jnp.float32),
            pltpu.VMEM((3, side, side), jnp.float32),
            *work_buffers(slots, size),
        ],
        name="backward",
        **kernel_options(slots, size),
    )(offsets, info, x_high, x_low, win, probe_re, probe_im, *tables)


def exchange_steps(n_tx, n_ty, n_pa):
    def along(dim, bit):
        def partner(*here):
            return tuple(at ^ bit if k == dim else at for k, at in enumerate(here))

        def upper(*here):
            return (here[dim] // bit) & 1

        return partner, upper

    def by_core(one, two):
        def partner(t, y, p):
            return one[0](t, y, p) if y % 2 == 0 else two[0](t, y, p)

        def upper(t, y, p):
            return jnp.where(y % 2 == 0, one[1](t, y, p), two[1](t, y, p))

        return partner, upper

    tx, ty, pa = (
        [along(dim, 1 << k) for k in range(low, size.bit_length() - 1)]
        for dim, (low, size) in enumerate(((0, n_tx), (1, n_ty), (0, n_pa)))
    )
    halving = [along(1, 1)]
    whole = []
    while tx and pa and len(halving) < 3:
        one, two = pa.pop(0), tx.pop(0)
        halving += [by_core(one, two), by_core(two, one)]
    while tx and ty:
        one, two = ty.pop(0), tx.pop(0)
        whole += [by_core(one, two), by_core(two, one)]
    whole += tx + ty + pa
    return halving, whole


def update(
    object_re,
    object_im,
    probe_real,
    probe_imaginary,
    gain,
    dark,
    measured,
    positions,
    counts,
    pixel_good,
):
    tile_side = object_re.shape[0]
    window = probe_real.shape[0]
    half = window // 2
    tables = dft_tables(window)
    t, y, p = (lax.axis_index(axis) for axis in MESH_AXES)
    n_tx, n_ty, n_pa = (lax.axis_size(axis) for axis in MESH_AXES)

    tile = lax.optimization_barrier(jnp.stack([object_re, object_im]))
    near = neighbour_swap(tile, "tx", 0)
    far = neighbour_swap(tile, "tx", 1)
    before, after = ordered(t % 2, far, near)
    strip = jnp.concatenate([before, tile, after], axis=1)
    near = neighbour_swap(strip, "ty", 0)
    far = neighbour_swap(strip, "ty", 1)
    before, after = ordered(y % 2, far, near)
    padded = jnp.concatenate([before, strip, after], axis=2)
    anchor = jnp.stack([t * tile_side, y * tile_side]).astype(jnp.int32)
    offsets = positions - anchor

    halving, whole = exchange_steps(n_tx, n_ty, n_pa)
    blocks = 1 << len(halving)
    span = window // blocks

    def block_of(t, y, p):
        place = jnp.int32(0)
        for _, bit in halving:
            place = 2 * place + bit(t, y, p)
        return place

    mine = block_of(t, y, p)
    other = block_of(*halving[0][0](t, y, p))
    info = jnp.stack([counts[0], mine, other, y % 2]).astype(jnp.int32)
    *early, x_high, x_low, win = forward(
        offsets, info, padded, probe_real, probe_imaginary, tables,
        measured, gain, dark, pixel_good, blocks,
    )
    *late, to_one, inner, to_zero = backward(
        offsets, info, x_high, x_low, win, probe_real, probe_imaginary, tables,
        tile_side, blocks,
    )

    def total(kept, sent):
        for k, (partner, _) in enumerate(halving):
            if k:
                middle = sums.shape[0] // 2
                kept, sent = sums[:middle], sums[middle:]
            sums = kept + partner_swap(sent, partner)
        for partner, _ in whole:
            sums = sums + partner_swap(sums, partner)
        return sums[0]

    def own(array):
        return lax.dynamic_slice_in_dim(array, mine * span, span, 0)

    early = total(*early)
    late = total(*late).reshape(2, span, window)
    power, gain_num, gain_den, dark_num = early[: 4 * span].reshape(4, span, window)
    dark_den = own(pixel_good).astype(jnp.float32) * early[4 * span : 4 * span + 1]
    new = jnp.stack(
        [
            own(probe_real) + late[0] / (power + 0.5),
            own(probe_imaginary) + late[1] / (power + 0.5),
            own(gain) + gain_num / (gain_den + 1.0),
            own(dark) + 0.5 * dark_num / (dark_den + 1.0),
        ]
    )
    for k, (partner, bit) in reversed(list(enumerate(halving))):
        low, high = ordered(bit(t, y, p), new, partner_swap(new, partner))
        new = jnp.concatenate([low, high], axis=1)

    edge = half + tile_side
    strip = inner + neighbour_swap(to_zero, "ty", 0) + neighbour_swap(to_one, "ty", 1)
    to_one, to_zero = ordered(t % 2, strip[:, :half], strip[:, edge:])
    sums = (
        strip[:, half:edge]
        + neighbour_swap(to_zero, "tx", 0)
        + neighbour_swap(to_one, "tx", 1)
    )
    for k in range(n_pa.bit_length() - 2, -1, -1):
        bit = 1 << k
        rows = sums.shape[1] // 2
        upper = (p // bit) & 1
        kept = lax.dynamic_slice_in_dim(sums, upper * rows, rows, 1)
        sent = lax.dynamic_slice_in_dim(sums, (1 - upper) * rows, rows, 1)
        sums = kept + lax.ppermute(sent, "pa", [(i, i ^ bit) for i in range(n_pa)])
    rows = sums.shape[1]
    own_tile = lax.dynamic_slice_in_dim(tile, p * rows, rows, 1)
    new_re = own_tile[0] + sums[0] / (sums[2] + 0.5)
    new_im = own_tile[1] + sums[1] / (sums[2] + 0.5)
    return (new_re, new_im, new[0], new[1], new[2], new[3])


def solution(mesh):
    placed = (
        P("tx", "ty"),
        P("tx", "ty"),
        P(),
        P(),
        P(),
        P(),
        P(("tx", "ty", "pa"), None, None),
        P(("tx", "ty", "pa"), None),
        P(("tx", "ty", "pa")),
        P(),
    )
    return jax.shard_map(
        update,
        mesh=mesh,
        in_specs=placed,
        out_specs=(P(("tx", "pa"), "ty"), P(("tx", "pa"), "ty"), P(), P(), P(), P()),
        check_vma=False,
    )
```

time: 89.9 us -> 83.7 us (0.931)
  waiting for transfers between devices: 34 us -> 40.9 us
  starting transfers between devices: 28 us -> 22.5 us
  other arithmetic: 10.2 us -> 5.45 us
  local copies, waits for them, and re-layouts: 6.01 us -> 1.96 us
  Pallas kernels: 9.3 us -> 10.9 us
    ppermute x9 -> x1, starting transfers between devices: 14.1 us -> 0.97 us  [update(): sums = kept + lax.ppermute(sent, 'pa', [(i, i ^ bit) for i in range(n_pa)])]
    ppermute x8 -> x21, waiting for transfers between devices: 28.6 us -> 40 us  [partner_swap(): return lax.ppermute(value, MESH_AXES, moves)]
    ppermute x8 -> x21, starting transfers between devices: 13.9 us -> 21.5 us  [partner_swap(): return lax.ppermute(value, MESH_AXES, moves)]
    ppermute x9 -> x1, waiting for transfers between devices: 5.41 us -> 0.91 us  [update(): sums = kept + lax.ppermute(sent, 'pa', [(i, i ^ bit) for i in range(n_pa)])]
    concatenate x8 -> x4, other arithmetic: 2.58 us -> 0.16 us  [the longest x1 0.08 us: update(): padded = jnp.concatenate([before, strip, after], axis=2)]
    slice x6 -> x5, local copies, waits for them, and re-layouts: 2.18 us -> 0.05 us  [the longest x4 0.05 us: total(): kept, sent = (sums[:middle], sums[middle:])]
    pallas_call x1 -> x2, Pallas kernels: 9.3 us -> 10.9 us  [the longest x1 6.04 us: forward(): pl.pallas_call(forward_kernel, out_shape=(jax.ShapeDtypeStruct((blocks //...]
    add x14, other arithmetic: 4.47 us -> 2.94 us  [the longest x1 1.15 us: update(): inner + neighbour_swap(to_zero, 'ty', 0) + neighbour_swap(to_one, 'ty', 1)]
  transfers between devices with their start and end apart: 17 -> 22, of which waited for: 12 -> 15; matrix products, arithmetic and copies ran while one was open for 5% -> 4% of each run, Pallas kernels for 0% -> 6%
where the time goes in v2:
time: 83.7 us; the launch traced here: 83.4 us
  waiting for transfers between devices  40.9 us (49%)
  starting transfers between devices  22.5 us (27%)
  Pallas kernels  10.9 us (13%)
  other arithmetic  5.45 us (7%)
  local copies, waits for them, and re-layouts  1.96 us (2%)
  between operations  1.62 us (2%)
    ppermute x21, waiting for transfers between devices, partner_swap(): return lax.ppermute(value, MESH_AXES, moves)  40 us
    ppermute x21, starting transfers between devices, partner_swap(): return lax.ppermute(value, MESH_AXES, moves)  21.5 us
    pallas_call x1, Pallas kernels, forward(): pl.pallas_call(forward_kernel, out_shape=(jax.ShapeDtypeStruct((blocks //...  6.04 us
    pallas_call x1, Pallas kernels, backward(): pl.pallas_call(backward_kernel, out_shape=(jax.ShapeDtypeStruct((blocks /...  4.91 us
    unnamed x22, local copies, waits for them, and re-layouts  1.89 us
  transfers between devices with their start and end apart: 22, of which 15 were waited for; matrix products, arithmetic and copies ran while one was open for 4% of the time, Pallas kernels for 6%

profile of v2, /device:TPU:0, one launch (start us, length us, event | category | flops | bytes accessed | tf_op | source)
XLA Modules:
  0.0 83.4 jit_solution(16690614578990036156)
XLA Ops:
  0.6 0.9 %pad_maximum_fusion.5 = f32[2,128,128]{2,1,0:T(8,128)S(1)} fusion(f32[1,128,128]{2,1,0:T(8,128)} %bitcast.54, f32[1,128,128]{2,1,0:T(8,128)} %bitcast.55), kind=kLoop, calls=%fused_computation.30 | loop fusion | flops 32768 | bytes 262144 | tf_op jit(solution)/shard_map/stack | solution.py:425
  1.5 3.0 %collective-permute-start = (f32[2,128,128]{2,1,0:T(8,128)S(1)}, f32[2,128,128]{2,1,0:T(8,128)S(1)}, u32[]{:S(2)}, u32[]{:S(2)}) collective-permute-start(f32[2,128,128]{2,1,0:T(8,128)S(1)} %pad_maximum_fusion.5), channel_id=1, source_target_pairs={{0,1},{1,0},{2,3},{3,2},{4,5},{5,4},{6,7},{7,6},{8,16},{9,17},{10,... | collective-permute-start | bytes 393224 | tf_op jit(solution)/shard_map/ppermute | solution.py:26
  4.6 1.7 %collective-permute-start.1 = (f32[2,128,128]{2,1,0:T(8,128)S(1)}, f32[2,128,128]{2,1,0:T(8,128)S(1)}, u32[]{:S(2)}, u32[]{:S(2)}) collective-permute-start(f32[2,128,128]{2,1,0:T(8,128)S(1)} %pad_maximum_fusion.5), channel_id=1, source_target_pairs={{0,8},{1,9},{2,10},{3,11},{4,12},{5,13},{6,14},{7,15},{8,0},{9,1},... | collective-permute-start | bytes 393224 | tf_op jit(solution)/shard_map/ppermute | solution.py:26
  6.9 1.2 %collective-permute-done = f32[2,128,128]{2,1,0:T(8,128)S(1)} collective-permute-done((f32[2,128,128]{2,1,0:T(8,128)S(1)}, f32[2,128,128]{2,1,0:T(8,128)S(1)}, u32[]{:S(2)}, u32[]{:S(2)}) %collective-permute-start) | collective-permute-done | bytes 131104 | tf_op jit(solution)/shard_map/ppermute | solution.py:26
  8.1 1.5 %collective-permute-done.1 = f32[2,128,128]{2,1,0:T(8,128)S(1)} collective-permute-done((f32[2,128,128]{2,1,0:T(8,128)S(1)}, f32[2,128,128]{2,1,0:T(8,128)S(1)}, u32[]{:S(2)}, u32[]{:S(2)}) %collective-permute-start.1) | collective-permute-done | bytes 131104 | tf_op jit(solution)/shard_map/ppermute | solution.py:26
  9.6 1.5 %collective-permute-start.2 = (f32[2,384,128]{2,1,0:T(8,128)S(1)}, f32[2,384,128]{2,1,0:T(8,128)S(1)}, u32[]{:S(2)}, u32[]{:S(2)}) collective-permute-start(f32[2,384,128]{2,1,0:T(8,128)S(1)} %pad_maximum_fusion.2), channel_id=1, source_target_pairs={{0,1},{1,0},{2,4},{3,5},{4,2},{5,3},{6,7},{7,6},{8,9},{9,8},{10,12... | collective-permute-start | bytes 1179656 | tf_op jit(solution)/shard_map/ppermute | solution.py:26
  11.1 0.2 collective-permute-start.3
  11.5 6.0 %collective-permute-done.2 = f32[2,384,128]{2,1,0:T(8,128)S(1)} collective-permute-done((f32[2,384,128]{2,1,0:T(8,128)S(1)}, f32[2,384,128]{2,1,0:T(8,128)S(1)}, u32[]{:S(2)}, u32[]{:S(2)}) %collective-permute-start.2) | collective-permute-done | bytes 393248 | tf_op jit(solution)/shard_map/ppermute | solution.py:26
  17.7 0.8 copy-done.7
  18.5 0.2 copy-done.8
  18.6 0.2 copy-done.9
  19.0 0.1 copy-done.2
  19.0 0.1 copy-done.3
  19.2 0.2 copy-done.5
  19.4 0.2 copy-done.6
  19.5 6.0 %forward.1 = (f32[4,136,256]{2,1,0:T(8,128)S(1)}, f32[4,136,256]{2,1,0:T(8,128)S(1)}, bf16[512,512]{1,0:T(8,128)(2,1)S(1)}, bf16[512,512]{1,0:T(8,128)(2,1)S(1)}, f32[2,2,256,256]{3,2,1,0:T(8,128)S(1)}) custom-call(s32[2,2]{1,0:T(2,128)S(1)} %broadcast_subtract_fusion.offsets, s32[4]{0:T(128)S(1)} %pad_add_fusion.1.info, ...), custom_call_target="tpu_custom_call" | custom-call | flops 1610612736 | bytes 6291456 | tf_op jit(solution)/shard_map/forward/pallas_call | solution.py:320
  25.7 1.9 %collective-permute-done.14 = f32[4,136,256]{2,1,0:T(8,128)S(1)} collective-permute-done((f32[4,136,256]{2,1,0:T(8,128)S(1)}, f32[4,136,256]{2,1,0:T(8,128)S(1)}, u32[]{:S(2)}, u32[]{:S(2)}) %collective-permute-start.14) | collective-permute-done | bytes 557088 | tf_op jit(solution)/shard_map/ppermute | solution.py:26
  27.7 1.5 %collective-permute-start.15 = (f32[2,136,256]{2,1,0:T(8,128)S(1)}, f32[2,136,256]{2,1,0:T(8,128)S(1)}, u32[]{:S(2)}, u32[]{:S(2)}) collective-permute-start(f32[2,136,256]{2,1,0:T(8,128)S(1)} %slice.118), channel_id=1, source_target_pairs={{0,1},{1,0},{2,10},{3,11},{4,5},{5,4},{6,14},{7,15},{8,9},{9,8},{1... | collective-permute-start | bytes 835592 | tf_op jit(solution)/shard_map/ppermute | solution.py:26
  29.2 4.9 %backward.1 = (f32[4,64,256]{2,1,0:T(8,128)S(1)}, f32[4,64,256]{2,1,0:T(8,128)S(1)}, f32[3,384,128]{2,1,0:T(8,128)S(1)}, f32[3,384,128]{2,1,0:T(8,128)S(1)}, f32[3,384,128]{2,1,0:T(8,128)S(1)}) custom-call(s32[2,2]{1,0:T(2,128)S(1)} %broadcast_subtract_fusion.offsets, s32[4]{0:T(128)S(1)} %pad_add_fusion.1.info, ...), custom_call_target="tpu_custom_call" | custom-call | flops 1610612736 | bytes 6291456 | tf_op jit(solution)/shard_map/backward/pallas_call | solution.py:350
  34.1 0.2 collective-permute-start.9
  34.3 0.4 collective-permute-start.4
  34.7 1.2 %collective-permute-start.5 = (f32[3,384,128]{2,1,0:T(8,128)S(1)}, f32[3,384,128]{2,1,0:T(8,128)}, u32[]{:S(2)}, u32[]{:S(2)}) collective-permute-start(f32[3,384,128]{2,1,0:T(8,128)S(1)} %get-tuple-element.21), channel_id=1, source_target_pairs={{0,1},{1,0},{2,4},{3,5},{4,2},{5,3},{6,7},{7,6},{8,9},{9,8},{10,12... | collective-permute-start | bytes 1769480 | tf_op jit(solution)/shard_map/ppermute | solution.py:26
  35.9 1.1 %collective-permute-start.10 = (f32[2,64,256]{2,1,0:T(8,128)S(1)}, f32[2,64,256]{2,1,0:T(8,128)S(1)}, u32[]{:S(2)}, u32[]{:S(2)}) collective-permute-start(f32[2,64,256]{2,1,0:T(8,128)S(1)} %slice.113), channel_id=1, source_target_pairs={{0,1},{1,0},{2,10},{3,11},{4,5},{5,4},{6,14},{7,15},{8,9},{9,8},{1... | collective-permute-start | bytes 393224 | tf_op jit(solution)/shard_map/ppermute | solution.py:26
  37.1 1.6 %collective-permute-start.16 = (f32[1,136,256]{2,1,0:T(8,128)S(1)}, f32[1,136,256]{2,1,0:T(8,128)S(1)}, u32[]{:S(2)}, u32[]{:S(2)}) collective-permute-start(f32[1,136,256]{2,1,0:T(8,128)S(1)} %slice.120), channel_id=1, source_target_pairs={{0,8},{1,9},{2,3},{3,2},{4,12},{5,13},{6,7},{7,6},{8,0},{9,1},{10,... | collective-permute-start | bytes 417800 | tf_op jit(solution)/shard_map/ppermute | solution.py:26
  38.7 9.4 %collective-permute-done.10 = f32[2,64,256]{2,1,0:T(8,128)S(1)} collective-permute-done((f32[2,64,256]{2,1,0:T(8,128)S(1)}, f32[2,64,256]{2,1,0:T(8,128)S(1)}, u32[]{:S(2)}, u32[]{:S(2)}) %collective-permute-start.10) | collective-permute-done | bytes 131104 | tf_op jit(solution)/shard_map/ppermute | solution.py:26
  48.2 1.8 %collective-permute-start.11 = (f32[1,64,256]{2,1,0:T(8,128)S(1)}, f32[1,64,256]{2,1,0:T(8,128)S(1)}, u32[]{:S(2)}, u32[]{:S(2)}) collective-permute-start(f32[1,64,256]{2,1,0:T(8,128)S(1)} %slice.115), channel_id=1, source_target_pairs={{0,8},{1,9},{2,3},{3,2},{4,12},{5,13},{6,7},{7,6},{8,0},{9,1},{10,... | collective-permute-start | bytes 196616 | tf_op jit(solution)/shard_map/ppermute | solution.py:26
  50.1 2.4 %collective-permute-done.11 = f32[1,64,256]{2,1,0:T(8,128)S(1)} collective-permute-done((f32[1,64,256]{2,1,0:T(8,128)S(1)}, f32[1,64,256]{2,1,0:T(8,128)S(1)}, u32[]{:S(2)}, u32[]{:S(2)}) %collective-permute-start.11) | collective-permute-done | bytes 65568 | tf_op jit(solution)/shard_map/ppermute | solution.py:26
  52.6 4.3 %collective-permute-done.12 = f32[1,64,256]{2,1,0:T(8,128)} collective-permute-done((f32[1,64,256]{2,1,0:T(8,128)S(1)}, f32[1,64,256]{2,1,0:T(8,128)}, u32[]{:S(2)}, u32[]{:S(2)}) %collective-permute-start.12) | collective-permute-done | bytes 65568 | tf_op jit(solution)/shard_map/ppermute | solution.py:26
  57.0 0.9 %add.171 = f32[1,64,256]{2,1,0:T(8,128)S(1)} add(f32[1,64,256]{2,1,0:T(8,128)S(1)} %slice_add_fusion.4, f32[1,64,256]{2,1,0:T(8,128)} %collective-permute-done.12) | non-fusion elementwise | flops 16384 | bytes 196608 | tf_op jit(solution)/shard_map/add | solution.py:466
  57.8 2.3 %collective-permute-start.13 = (f32[1,64,256]{2,1,0:T(8,128)S(1)}, f32[1,64,256]{2,1,0:T(8,128)S(1)}, u32[]{:S(2)}, u32[]{:S(2)}) collective-permute-start(f32[1,64,256]{2,1,0:T(8,128)S(1)} %add.171), channel_id=1, source_target_pairs={{0,16},{1,17},{2,6},{3,7},{4,20},{5,21},{6,2},{7,3},{8,24},{9,25},... | collective-permute-start | bytes 196616 | tf_op jit(solution)/shard_map/ppermute | solution.py:26
  60.1 0.8 collective-permute-start.18
  60.9 1.1 %select_add_fusion = f32[3,384,128]{2,1,0:T(8,128)S(1)} fusion(f32[3,384,128]{2,1,0:T(8,128)} %collective-permute-done.5, f32[3,384,128]{2,1,0:T(8,128)S(1)} %get-tuple-element.19, f32[3,384,128]{2,1,0:T(8,128)} %collective-permute-done.4, pred[]{:T(512)S(6)} %and.82), kind=kLoop, calls=%fused_computation.7 | loop fusion | flops 442368 | bytes 2359297 | tf_op jit(solution)/shard_map/add | solution.py:489
  62.1 1.0 %collective-permute-done.13 = f32[1,64,256]{2,1,0:T(8,128)S(1)} collective-permute-done((f32[1,64,256]{2,1,0:T(8,128)S(1)}, f32[1,64,256]{2,1,0:T(8,128)S(1)}, u32[]{:S(2)}, u32[]{:S(2)}) %collective-permute-start.13) | collective-permute-done | bytes 65568 | tf_op jit(solution)/shard_map/ppermute | solution.py:26
  63.1 5.6 %collective-permute-done.18 = f32[1,136,256]{2,1,0:T(8,128)S(1)} collective-permute-done((f32[1,136,256]{2,1,0:T(8,128)S(1)}, f32[1,136,256]{2,1,0:T(8,128)S(1)}, u32[]{:S(2)}, u32[]{:S(2)}) %collective-permute-start.18) | collective-permute-done | bytes 139296 | tf_op jit(solution)/shard_map/ppermute | solution.py:26
  68.7 0.2 collective-permute-start.19
  68.9 2.0 %collective-permute-start.6 = (f32[3,128,128]{2,1,0:T(8,128)S(1)}, f32[3,128,128]{2,1,0:T(8,128)S(1)}, u32[]{:S(2)}, u32[]{:S(2)}) collective-permute-start(f32[3,128,128]{2,1,0:T(8,128)S(1)} %get-tuple-element.35), channel_id=1, source_target_pairs={{0,8},{1,9},{2,10},{3,11},{4,12},{5,13},{6,14},{7,15},{8,0},{9,1},... | collective-permute-start | bytes 589832 | tf_op jit(solution)/shard_map/ppermute | solution.py:26
  70.9 0.9 %collective-permute-start.7 = (f32[3,128,128]{2,1,0:T(8,128)S(1)}, f32[3,128,128]{2,1,0:T(8,128)S(1)}, u32[]{:S(2)}, u32[]{:S(2)}) collective-permute-start(f32[3,128,128]{2,1,0:T(8,128)S(1)} %get-tuple-element.34), channel_id=1, source_target_pairs={{0,1},{1,0},{2,3},{3,2},{4,5},{5,4},{6,7},{7,6},{8,16},{9,17},{10,... | collective-permute-start | bytes 589832 | tf_op jit(solution)/shard_map/ppermute | solution.py:26
  71.8 1.9 %collective-permute-done.19 = f32[4,32,256]{2,1,0:T(8,128)S(1)} collective-permute-done((f32[4,32,256]{2,1,0:T(8,128)S(1)}, f32[4,32,256]{2,1,0:T(8,128)S(1)}, u32[]{:S(2)}, u32[]{:S(2)}) %collective-permute-start.19) | collective-permute-done | bytes 131104 | tf_op jit(solution)/shard_map/ppermute | solution.py:26
  73.8 1.0 %collective-permute-start.20 = (f32[4,64,256]{2,1,0:T(8,128)S(1)}, f32[4,64,256]{2,1,0:T(8,128)S(1)}, u32[]{:S(2)}, u32[]{:S(2)}) collective-permute-start(f32[4,64,256]{2,1,0:T(8,128)S(1)} %pad_maximum_fusion.4), channel_id=1, source_target_pairs={{0,1},{1,0},{2,10},{3,11},{4,5},{5,4},{6,14},{7,15},{8,9},{9,8},{1... | collective-permute-start | bytes 786440 | tf_op jit(solution)/shard_map/ppermute | solution.py:26
  74.8 1.1 %collective-permute-done.6 = f32[3,128,128]{2,1,0:T(8,128)S(1)} collective-permute-done((f32[3,128,128]{2,1,0:T(8,128)S(1)}, f32[3,128,128]{2,1,0:T(8,128)S(1)}, u32[]{:S(2)}, u32[]{:S(2)}) %collective-permute-start.6) | collective-permute-done | bytes 196640 | tf_op jit(solution)/shard_map/ppermute | solution.py:26
  75.9 0.7 collective-permute-done.7
  76.6 1.0 %collective-permute-start.8 = (f32[3,64,128]{2,1,0:T(8,128)S(1)}, f32[3,64,128]{2,1,0:T(8,128)S(1)}, u32[]{:S(2)}, u32[]{:S(2)}) collective-permute-start(f32[3,64,128]{2,1,0:T(8,128)S(1)} %constant_dynamic-slice_fusion), channel_id=1, source_target_pairs={{0,1},{1,0},{2,3},{3,2},{4,5},{5,4},{6,7},{7,6},{8,9},{9,8},{10,11... | collective-permute-start | bytes 294920 | tf_op jit(solution)/shard_map/ppermute | solution.py:502
  77.6 2.6 %collective-permute-done.20 = f32[4,64,256]{2,1,0:T(8,128)S(1)} collective-permute-done((f32[4,64,256]{2,1,0:T(8,128)S(1)}, f32[4,64,256]{2,1,0:T(8,128)S(1)}, u32[]{:S(2)}, u32[]{:S(2)}) %collective-permute-start.20) | collective-permute-done | bytes 262176 | tf_op jit(solution)/shard_map/ppermute | solution.py:26
  80.4 0.9 %collective-permute-done.8 = f32[3,64,128]{2,1,0:T(8,128)S(1)} collective-permute-done((f32[3,64,128]{2,1,0:T(8,128)S(1)}, f32[3,64,128]{2,1,0:T(8,128)S(1)}, u32[]{:S(2)}, u32[]{:S(2)}) %collective-permute-start.8) | collective-permute-done | bytes 98336 | tf_op jit(solution)/shard_map/ppermute | solution.py:502
  81.3 0.6 fusion.23
  82.0 0.3 collective-permute-done.21
  82.3 0.1 broadcast_select_fusion
  82.4 1.0 %fusion.6 = (f32[256,256]{1,0:T(8,128)}, f32[256,256]{1,0:T(8,128)}, f32[256,256]{1,0:T(8,128)}, f32[256,256]{1,0:T(8,128)}) fusion(f32[4,128,256]{2,1,0:T(8,128)S(1)} %get-tuple-element.30, f32[4,128,256]{2,1,0:T(8,128)S(1)} %get-tuple-element.31), kind=kLoop, calls=%fused_computation.20 | loop fusion | flops 262144 | bytes 2097152 | tf_op jit(solution)/shard_map/squeeze | solution.py:507
  (57 shorter events, 1.5 us)
Async XLA Ops:
  0.6 10.8 %copy-start.10 = (s32[2,2]{1,0:T(2,128)S(1)}, s32[2,2]{1,0:T(2,128)}, u32[]{:S(2)}) copy-start(s32[2,2]{1,0:T(2,128)} %param.21) | copy-start | bytes 52
  1.5 6.5 %collective-permute-start = (f32[2,128,128]{2,1,0:T(8,128)S(1)}, f32[2,128,128]{2,1,0:T(8,128)S(1)}, u32[]{:S(2)}, u32[]{:S(2)}) collective-permute-start(f32[2,128,128]{2,1,0:T(8,128)S(1)} %pad_maximum_fusion.5), channel_id=1, source_target_pairs={{0,1},{1,0},{2,3},{3,2},{4,5},{5,4},{6,7},{7,6},{8,16},{9,17},{10,... | collective-permute-start | bytes 393224 | tf_op jit(solution)/shard_map/ppermute | solution.py:26
  4.6 5.0 %collective-permute-start.1 = (f32[2,128,128]{2,1,0:T(8,128)S(1)}, f32[2,128,128]{2,1,0:T(8,128)S(1)}, u32[]{:S(2)}, u32[]{:S(2)}) collective-permute-start(f32[2,128,128]{2,1,0:T(8,128)S(1)} %pad_maximum_fusion.5), channel_id=1, source_target_pairs={{0,8},{1,9},{2,10},{3,11},{4,12},{5,13},{6,14},{7,15},{8,0},{9,1},... | collective-permute-start | bytes 393224 | tf_op jit(solution)/shard_map/ppermute | solution.py:26
  9.6 7.8 %collective-permute-start.2 = (f32[2,384,128]{2,1,0:T(8,128)S(1)}, f32[2,384,128]{2,1,0:T(8,128)S(1)}, u32[]{:S(2)}, u32[]{:S(2)}) collective-permute-start(f32[2,384,128]{2,1,0:T(8,128)S(1)} %pad_maximum_fusion.2), channel_id=1, source_target_pairs={{0,1},{1,0},{2,4},{3,5},{4,2},{5,3},{6,7},{7,6},{8,9},{9,8},{10,12... | collective-permute-start | bytes 1179656 | tf_op jit(solution)/shard_map/ppermute | solution.py:26
  11.1 6.4 %collective-permute-start.3 = (f32[2,384,128]{2,1,0:T(8,128)S(1)}, f32[2,384,128]{2,1,0:T(8,128)S(1)}, u32[]{:S(2)}, u32[]{:S(2)}) collective-permute-start(f32[2,384,128]{2,1,0:T(8,128)S(1)} %pad_maximum_fusion.2), channel_id=1, source_target_pairs={{0,2},{1,3},{2,0},{3,1},{4,6},{5,7},{6,4},{7,5},{8,10},{9,11},{10,... | collective-permute-start | bytes 1179656 | tf_op jit(solution)/shard_map/ppermute | solution.py:26
  17.4 1.0 %copy-start.7 = (bf16[512,512]{1,0:T(8,128)(2,1)S(1)}, bf16[512,512]{1,0:T(8,128)(2,1)}, u32[]{:S(2)}) copy-start(bf16[512,512]{1,0:T(8,128)(2,1)} %constant.132.clone.row_low) | copy-start | bytes 1572868
  17.4 1.2 %copy-start.8 = (bf16[512,512]{1,0:T(8,128)(2,1)S(1)}, bf16[512,512]{1,0:T(8,128)(2,1)}, u32[]{:S(2)}) copy-start(bf16[512,512]{1,0:T(8,128)(2,1)} %constant.133.clone.col_high) | copy-start | bytes 1572868
  17.4 1.4 %copy-start.9 = (bf16[512,512]{1,0:T(8,128)(2,1)S(1)}, bf16[512,512]{1,0:T(8,128)(2,1)}, u32[]{:S(2)}) copy-start(bf16[512,512]{1,0:T(8,128)(2,1)} %constant.134.clone.col_low) | copy-start | bytes 1572868
  17.5 1.4 %copy-start = (f32[256,256]{1,0:T(8,128)S(1)}, f32[256,256]{1,0:T(8,128)}, u32[]{:S(2)}) copy-start(f32[256,256]{1,0:T(8,128)} %probe_re.3) | copy-start | bytes 786436
  17.5 1.4 %copy-start.1 = (f32[256,256]{1,0:T(8,128)S(1)}, f32[256,256]{1,0:T(8,128)}, u32[]{:S(2)}) copy-start(f32[256,256]{1,0:T(8,128)} %probe_im.3) | copy-start | bytes 786436
  17.5 1.5 %copy-start.2 = (f32[256,256]{1,0:T(8,128)S(1)}, f32[256,256]{1,0:T(8,128)}, u32[]{:S(2)}) copy-start(f32[256,256]{1,0:T(8,128)} %gain_hbm.1) | copy-start | bytes 786436
  17.6 1.6 %copy-start.3 = (f32[256,256]{1,0:T(8,128)S(1)}, f32[256,256]{1,0:T(8,128)}, u32[]{:S(2)}) copy-start(f32[256,256]{1,0:T(8,128)} %dark_hbm.1) | copy-start | bytes 786436
  17.6 1.6 %copy-start.4 = (s32[256,256]{1,0:T(8,128)S(1)}, s32[256,256]{1,0:T(8,128)}, u32[]{:S(2)}) copy-start(s32[256,256]{1,0:T(8,128)} %good_hbm.1) | copy-start | bytes 786436
  17.6 1.8 %copy-start.5 = (f32[2,256,256]{2,1,0:T(8,128)S(1)}, f32[2,256,256]{2,1,0:T(8,128)}, u32[]{:S(2)}) copy-start(f32[2,256,256]{2,1,0:T(8,128)} %measured_hbm.1) | copy-start | bytes 1572868
  17.6 2.0 %copy-start.6 = (bf16[512,512]{1,0:T(8,128)(2,1)S(1)}, bf16[512,512]{1,0:T(8,128)(2,1)}, u32[]{:S(2)}) copy-start(bf16[512,512]{1,0:T(8,128)(2,1)} %constant.131.clone.row_high) | copy-start | bytes 1572868
  25.6 2.0 %collective-permute-start.14 = (f32[4,136,256]{2,1,0:T(8,128)S(1)}, f32[4,136,256]{2,1,0:T(8,128)S(1)}, u32[]{:S(2)}, u32[]{:S(2)}) collective-permute-start(f32[4,136,256]{2,1,0:T(8,128)S(1)} %get-tuple-element.25), channel_id=1, source_target_pairs={{0,2},{1,3},{2,0},{3,1},{4,6},{5,7},{6,4},{7,5},{8,10},{9,11},{10,... | collective-permute-start | bytes 1671176 | tf_op jit(solution)/shard_map/ppermute | solution.py:26
  27.7 9.3 %collective-permute-start.15 = (f32[2,136,256]{2,1,0:T(8,128)S(1)}, f32[2,136,256]{2,1,0:T(8,128)S(1)}, u32[]{:S(2)}, u32[]{:S(2)}) collective-permute-start(f32[2,136,256]{2,1,0:T(8,128)S(1)} %slice.118), channel_id=1, source_target_pairs={{0,1},{1,0},{2,10},{3,11},{4,5},{5,4},{6,14},{7,15},{8,9},{9,8},{1... | collective-permute-start | bytes 835592 | tf_op jit(solution)/shard_map/ppermute | solution.py:26
  34.1 1.8 %collective-permute-start.9 = (f32[4,64,256]{2,1,0:T(8,128)S(1)}, f32[4,64,256]{2,1,0:T(8,128)S(1)}, u32[]{:S(2)}, u32[]{:S(2)}) collective-permute-start(f32[4,64,256]{2,1,0:T(8,128)S(1)} %get-tuple-element.23), channel_id=1, source_target_pairs={{0,2},{1,3},{2,0},{3,1},{4,6},{5,7},{6,4},{7,5},{8,10},{9,11},{10,... | collective-permute-start | bytes 786440 | tf_op jit(solution)/shard_map/ppermute | solution.py:26
  34.3 26.6 %collective-permute-start.4 = (f32[3,384,128]{2,1,0:T(8,128)S(1)}, f32[3,384,128]{2,1,0:T(8,128)}, u32[]{:S(2)}, u32[]{:S(2)}) collective-permute-start(f32[3,384,128]{2,1,0:T(8,128)S(1)} %get-tuple-element.20), channel_id=1, source_target_pairs={{0,2},{1,3},{2,0},{3,1},{4,6},{5,7},{6,4},{7,5},{8,10},{9,11},{10,... | collective-permute-start | bytes 1769480 | tf_op jit(solution)/shard_map/ppermute | solution.py:26
  34.7 26.2 %collective-permute-start.5 = (f32[3,384,128]{2,1,0:T(8,128)S(1)}, f32[3,384,128]{2,1,0:T(8,128)}, u32[]{:S(2)}, u32[]{:S(2)}) collective-permute-start(f32[3,384,128]{2,1,0:T(8,128)S(1)} %get-tuple-element.21), channel_id=1, source_target_pairs={{0,1},{1,0},{2,4},{3,5},{4,2},{5,3},{6,7},{7,6},{8,9},{9,8},{10,12... | collective-permute-start | bytes 1769480 | tf_op jit(solution)/shard_map/ppermute | solution.py:26
  35.9 12.2 %collective-permute-start.10 = (f32[2,64,256]{2,1,0:T(8,128)S(1)}, f32[2,64,256]{2,1,0:T(8,128)S(1)}, u32[]{:S(2)}, u32[]{:S(2)}) collective-permute-start(f32[2,64,256]{2,1,0:T(8,128)S(1)} %slice.113), channel_id=1, source_target_pairs={{0,1},{1,0},{2,10},{3,11},{4,5},{5,4},{6,14},{7,15},{8,9},{9,8},{1... | collective-permute-start | bytes 393224 | tf_op jit(solution)/shard_map/ppermute | solution.py:26
  37.1 12.9 %collective-permute-start.16 = (f32[1,136,256]{2,1,0:T(8,128)S(1)}, f32[1,136,256]{2,1,0:T(8,128)S(1)}, u32[]{:S(2)}, u32[]{:S(2)}) collective-permute-start(f32[1,136,256]{2,1,0:T(8,128)S(1)} %slice.120), channel_id=1, source_target_pairs={{0,8},{1,9},{2,3},{3,2},{4,12},{5,13},{6,7},{7,6},{8,0},{9,1},{10,... | collective-permute-start | bytes 417800 | tf_op jit(solution)/shard_map/ppermute | solution.py:26
  48.2 4.3 %collective-permute-start.11 = (f32[1,64,256]{2,1,0:T(8,128)S(1)}, f32[1,64,256]{2,1,0:T(8,128)S(1)}, u32[]{:S(2)}, u32[]{:S(2)}) collective-permute-start(f32[1,64,256]{2,1,0:T(8,128)S(1)} %slice.115), channel_id=1, source_target_pairs={{0,8},{1,9},{2,3},{3,2},{4,12},{5,13},{6,7},{7,6},{8,0},{9,1},{10,... | collective-permute-start | bytes 196616 | tf_op jit(solution)/shard_map/ppermute | solution.py:26
  50.0 10.1 %collective-permute-start.17 = (f32[1,136,256]{2,1,0:T(8,128)S(1)}, f32[1,136,256]{2,1,0:T(8,128)S(1)}, u32[]{:S(2)}, u32[]{:S(2)}) collective-permute-start(f32[1,136,256]{2,1,0:T(8,128)S(1)} %slice_add_fusion.2), channel_id=1, source_target_pairs={{0,4},{1,5},{2,18},{3,19},{4,0},{5,1},{6,22},{7,23},{8,12},{9,13},... | collective-permute-start | bytes 417800 | tf_op jit(solution)/shard_map/ppermute | solution.py:26
  52.5 4.4 %collective-permute-start.12 = (f32[1,64,256]{2,1,0:T(8,128)S(1)}, f32[1,64,256]{2,1,0:T(8,128)}, u32[]{:S(2)}, u32[]{:S(2)}) collective-permute-start(f32[1,64,256]{2,1,0:T(8,128)S(1)} %slice_add_fusion.4), channel_id=1, source_target_pairs={{0,4},{1,5},{2,18},{3,19},{4,0},{5,1},{6,22},{7,23},{8,12},{9,13},... | collective-permute-start | bytes 196616 | tf_op jit(solution)/shard_map/ppermute | solution.py:26
  57.8 5.2 %collective-permute-start.13 = (f32[1,64,256]{2,1,0:T(8,128)S(1)}, f32[1,64,256]{2,1,0:T(8,128)S(1)}, u32[]{:S(2)}, u32[]{:S(2)}) collective-permute-start(f32[1,64,256]{2,1,0:T(8,128)S(1)} %add.171), channel_id=1, source_target_pairs={{0,16},{1,17},{2,6},{3,7},{4,20},{5,21},{6,2},{7,3},{8,24},{9,25},... | collective-permute-start | bytes 196616 | tf_op jit(solution)/shard_map/ppermute | solution.py:26
  60.1 8.5 %collective-permute-start.18 = (f32[1,136,256]{2,1,0:T(8,128)S(1)}, f32[1,136,256]{2,1,0:T(8,128)S(1)}, u32[]{:S(2)}, u32[]{:S(2)}) collective-permute-start(f32[1,136,256]{2,1,0:T(8,128)S(1)} %add.176), channel_id=1, source_target_pairs={{0,16},{1,17},{2,6},{3,7},{4,20},{5,21},{6,2},{7,3},{8,24},{9,25},... | collective-permute-start | bytes 417800 | tf_op jit(solution)/shard_map/ppermute | solution.py:26
  68.7 5.0 %collective-permute-start.19 = (f32[4,32,256]{2,1,0:T(8,128)S(1)}, f32[4,32,256]{2,1,0:T(8,128)S(1)}, u32[]{:S(2)}, u32[]{:S(2)}) collective-permute-start(f32[4,32,256]{2,1,0:T(8,128)S(1)} %pad_maximum_fusion.6), channel_id=1, source_target_pairs={{0,8},{1,9},{2,3},{3,2},{4,12},{5,13},{6,7},{7,6},{8,0},{9,1},{10,... | collective-permute-start | bytes 393224 | tf_op jit(solution)/shard_map/ppermute | solution.py:26
  68.9 6.9 %collective-permute-start.6 = (f32[3,128,128]{2,1,0:T(8,128)S(1)}, f32[3,128,128]{2,1,0:T(8,128)S(1)}, u32[]{:S(2)}, u32[]{:S(2)}) collective-permute-start(f32[3,128,128]{2,1,0:T(8,128)S(1)} %get-tuple-element.35), channel_id=1, source_target_pairs={{0,8},{1,9},{2,10},{3,11},{4,12},{5,13},{6,14},{7,15},{8,0},{9,1},... | collective-permute-start | bytes 589832 | tf_op jit(solution)/shard_map/ppermute | solution.py:26
  70.9 5.7 %collective-permute-start.7 = (f32[3,128,128]{2,1,0:T(8,128)S(1)}, f32[3,128,128]{2,1,0:T(8,128)S(1)}, u32[]{:S(2)}, u32[]{:S(2)}) collective-permute-start(f32[3,128,128]{2,1,0:T(8,128)S(1)} %get-tuple-element.34), channel_id=1, source_target_pairs={{0,1},{1,0},{2,3},{3,2},{4,5},{5,4},{6,7},{7,6},{8,16},{9,17},{10,... | collective-permute-start | bytes 589832 | tf_op jit(solution)/shard_map/ppermute | solution.py:26
  73.8 6.4 %collective-permute-start.20 = (f32[4,64,256]{2,1,0:T(8,128)S(1)}, f32[4,64,256]{2,1,0:T(8,128)S(1)}, u32[]{:S(2)}, u32[]{:S(2)}) collective-permute-start(f32[4,64,256]{2,1,0:T(8,128)S(1)} %pad_maximum_fusion.4), channel_id=1, source_target_pairs={{0,1},{1,0},{2,10},{3,11},{4,5},{5,4},{6,14},{7,15},{8,9},{9,8},{1... | collective-permute-start | bytes 786440 | tf_op jit(solution)/shard_map/ppermute | solution.py:26
  76.6 4.7 %collective-permute-start.8 = (f32[3,64,128]{2,1,0:T(8,128)S(1)}, f32[3,64,128]{2,1,0:T(8,128)S(1)}, u32[]{:S(2)}, u32[]{:S(2)}) collective-permute-start(f32[3,64,128]{2,1,0:T(8,128)S(1)} %constant_dynamic-slice_fusion), channel_id=1, source_target_pairs={{0,1},{1,0},{2,3},{3,2},{4,5},{5,4},{6,7},{7,6},{8,9},{9,8},{10,11... | collective-permute-start | bytes 294920 | tf_op jit(solution)/shard_map/ppermute | solution.py:502
  80.3 2.0 %collective-permute-start.21 = (f32[4,128,256]{2,1,0:T(8,128)S(1)}, f32[4,128,256]{2,1,0:T(8,128)S(1)}, u32[]{:S(2)}, u32[]{:S(2)}) collective-permute-start(f32[4,128,256]{2,1,0:T(8,128)S(1)} %pad_maximum_fusion.1), channel_id=1, source_target_pairs={{0,2},{1,3},{2,0},{3,1},{4,6},{5,7},{6,4},{7,5},{8,10},{9,11},{10,... | collective-permute-start | bytes 1572872 | tf_op jit(solution)/shard_map/ppermute | solution.py:26

commit v3 on v2

--- a/solution.py
+++ b/solution.py
@@ -26,7 +26,7 @@
     return lax.ppermute(value, MESH_AXES, moves)
 
 
-def neighbour_swap(value, axis, parity):
+def neighbour_swap(value, axis, parity, fill=True):
     dim = MESH_AXES.index(axis)
     size = lax.axis_size(axis)
     n_pa = lax.axis_size("pa")
@@ -39,11 +39,11 @@
         other = paired(here[dim])
         if other is None:
             idle = here[2] ^ 1
-            return (here[0], here[1], idle if idle < n_pa else here[2])
+            return (here[0], here[1], idle if fill and idle < n_pa else here[2])
         return tuple(other if k == dim else at for k, at in enumerate(here))
 
     got = partner_swap(value, partner)
-    if all(paired(at) is not None for at in range(size)):
+    if not fill or all(paired(at) is not None for at in range(size)):
         return got
     other = (lax.axis_index(axis) - parity ^ 1) + parity
     return jnp.where((0 <= other) & (other < size), got, 0.0)
@@ -293,7 +293,7 @@
 
 SMEM = pl.BlockSpec(memory_space=pltpu.SMEM)
 VMEM = pl.BlockSpec(memory_space=pltpu.VMEM)
-ANY = pl.BlockSpec(memory_space=pl.ANY)
+HBM = pl.BlockSpec(memory_space=pltpu.HBM)
 
 
 def work_buffers(slots, size):
@@ -307,7 +307,7 @@
 
 def kernel_options(slots, size):
     return dict(
-        compiler_params=pltpu.CompilerParams(vmem_limit_bytes=24 * 1024 * 1024),
+        compiler_params=pltpu.CompilerParams(vmem_limit_bytes=8 * 1024 * 1024),
         cost_estimate=pl.CostEstimate(
             flops=slots * 48 * size**3, bytes_accessed=6 * 1024 * 1024, transcendentals=0
         ),
@@ -326,7 +326,7 @@
             jax.ShapeDtypeStruct((slots * size, 2 * size), jnp.bfloat16),
             jax.ShapeDtypeStruct((slots, 2, size, size), jnp.float32),
         ),
-        in_specs=[SMEM] * 2 + [VMEM] * 7 + [ANY] * 4,
+        in_specs=[SMEM] * 2 + [VMEM] * 7 + [HBM] * 4,
         out_specs=(VMEM,) * 5,
         scratch_shapes=[
             pltpu.VMEM((blocks, depth, size), jnp.float32),
@@ -456,27 +456,29 @@
         tile_side, blocks,
     )
 
-    def total(kept, sent):
-        for k, (partner, _) in enumerate(halving):
-            if k:
-                middle = sums.shape[0] // 2
-                kept, sent = sums[:middle], sums[middle:]
-            sums = kept + partner_swap(sent, partner)
-        for partner, _ in whole:
-            sums = sums + partner_swap(sums, partner)
-        return sums[0]
+    def first_half(kept, sent):
+        return kept + partner_swap(sent, halving[0][0])
+
+    early = first_half(*early)
+    late = first_half(*late)
+    sums = jnp.concatenate([late, early], axis=1)
+    for k, (partner, _) in enumerate(halving[1:], 1):
+        middle = sums.shape[0] // 2
+        sums = sums[:middle] + partner_swap(sums[middle:], partner)
+    for partner, _ in whole:
+        sums = sums + partner_swap(sums, partner)
+    sums = sums[0]
 
     def own(array):
         return lax.dynamic_slice_in_dim(array, mine * span, span, 0)
 
-    early = total(*early)
-    late = total(*late).reshape(2, span, window)
-    power, gain_num, gain_den, dark_num = early[: 4 * span].reshape(4, span, window)
-    dark_den = own(pixel_good).astype(jnp.float32) * early[4 * span : 4 * span + 1]
+    probe_num = sums[: 2 * span].reshape(2, span, window)
+    power, gain_num, gain_den, dark_num = sums[2 * span : 6 * span].reshape(4, span, window)
+    dark_den = own(pixel_good).astype(jnp.float32) * sums[6 * span : 6 * span + 1]
     new = jnp.stack(
         [
-            own(probe_real) + late[0] / (power + 0.5),
-            own(probe_imaginary) + late[1] / (power + 0.5),
+            own(probe_real) + probe_num[0] / (power + 0.5),
+            own(probe_imaginary) + probe_num[1] / (power + 0.5),
             own(gain) + gain_num / (gain_den + 1.0),
             own(dark) + 0.5 * dark_num / (dark_den + 1.0),
         ]
@@ -486,13 +488,13 @@
         new = jnp.concatenate([low, high], axis=1)
 
     edge = half + tile_side
-    strip = inner + neighbour_swap(to_zero, "ty", 0) + neighbour_swap(to_one, "ty", 1)
+    from_zero = neighbour_swap(to_zero, "ty", 0)
+    from_one = neighbour_swap(to_one, "ty", 1, fill=False)
+    strip = inner + from_zero + from_one
     to_one, to_zero = ordered(t % 2, strip[:, :half], strip[:, edge:])
-    sums = (
-        strip[:, half:edge]
-        + neighbour_swap(to_zero, "tx", 0)
-        + neighbour_swap(to_one, "tx", 1)
-    )
+    from_zero = neighbour_swap(to_zero, "tx", 0)
+    from_one = neighbour_swap(to_one, "tx", 1)
+    sums = strip[:, half:edge] + from_zero + from_one
     for k in range(n_pa.bit_length() - 2, -1, -1):
         bit = 1 << k
         rows = sums.shape[1] // 2

time: 83.7 us -> 83.1 us (level)
  waiting for transfers between devices: 40.9 us -> 38.8 us
  starting transfers between devices: 22.5 us -> 23.9 us
    ppermute x21 -> x17, waiting for transfers between devices: 40 us -> 37.8 us  [partner_swap(): return lax.ppermute(value, MESH_AXES, moves)]
    ppermute x21 -> x17, starting transfers between devices: 21.5 us -> 22.3 us  [partner_swap(): return lax.ppermute(value, MESH_AXES, moves)]
    add x12 -> x8, other arithmetic: 2.28 us -> 2.54 us  [the longest x1 1.32 us: update(): strip = inner + from_zero + from_one]
  transfers between devices with their start and end apart: 22 -> 18, of which waited for: 15 -> 14; matrix products, arithmetic and copies ran while one was open for 4% -> 4% of each run, Pallas kernels for 6% -> 6%
where the time goes in v3:
time: 83.1 us; the launch traced here: 82.9 us
  waiting for transfers between devices  38.8 us (47%)
  starting transfers between devices  23.9 us (29%)
  Pallas kernels  10.9 us (13%)
  other arithmetic  5.74 us (7%)
  local copies, waits for them, and re-layouts  1.92 us (2%)
  between operations  1.59 us (2%)
    ppermute x17, waiting for transfers between devices, partner_swap(): return lax.ppermute(value, MESH_AXES, moves)  37.8 us
    ppermute x17, starting transfers between devices, partner_swap(): return lax.ppermute(value, MESH_AXES, moves)  22.3 us
    pallas_call x1, Pallas kernels, forward(): pl.pallas_call(forward_kernel, out_shape=(jax.ShapeDtypeStruct((blocks //...  6.02 us
    pallas_call x1, Pallas kernels, backward(): pl.pallas_call(backward_kernel, out_shape=(jax.ShapeDtypeStruct((blocks /...  4.9 us
    unnamed x22, local copies, waits for them, and re-layouts  1.89 us
  transfers between devices with their start and end apart: 18, of which 14 were waited for; matrix products, arithmetic and copies ran while one was open for 4% of the time, Pallas kernels for 6%

profile of v3, /device:TPU:0, one launch (start us, length us, event | category | flops | bytes accessed | tf_op | source)
XLA Modules:
  0.0 82.9 jit_solution(4159420179179580093)
XLA Ops:
  0.6 0.9 %pad_maximum_fusion.6 = f32[2,128,128]{2,1,0:T(8,128)S(1)} fusion(f32[1,128,128]{2,1,0:T(8,128)} %bitcast.54, f32[1,128,128]{2,1,0:T(8,128)} %bitcast.55), kind=kLoop, calls=%fused_computation.33 | loop fusion | flops 32768 | bytes 262144 | tf_op jit(solution)/shard_map/stack | solution.py:425
  1.5 3.0 %collective-permute-start = (f32[2,128,128]{2,1,0:T(8,128)S(1)}, f32[2,128,128]{2,1,0:T(8,128)S(1)}, u32[]{:S(2)}, u32[]{:S(2)}) collective-permute-start(f32[2,128,128]{2,1,0:T(8,128)S(1)} %pad_maximum_fusion.6), channel_id=1, source_target_pairs={{0,1},{1,0},{2,3},{3,2},{4,5},{5,4},{6,7},{7,6},{8,16},{9,17},{10,... | collective-permute-start | bytes 393224 | tf_op jit(solution)/shard_map/ppermute | solution.py:26
  4.6 1.7 %collective-permute-start.1 = (f32[2,128,128]{2,1,0:T(8,128)S(1)}, f32[2,128,128]{2,1,0:T(8,128)S(1)}, u32[]{:S(2)}, u32[]{:S(2)}) collective-permute-start(f32[2,128,128]{2,1,0:T(8,128)S(1)} %pad_maximum_fusion.6), channel_id=1, source_target_pairs={{0,8},{1,9},{2,10},{3,11},{4,12},{5,13},{6,14},{7,15},{8,0},{9,1},... | collective-permute-start | bytes 393224 | tf_op jit(solution)/shard_map/ppermute | solution.py:26
  6.9 1.2 %collective-permute-done = f32[2,128,128]{2,1,0:T(8,128)S(1)} collective-permute-done((f32[2,128,128]{2,1,0:T(8,128)S(1)}, f32[2,128,128]{2,1,0:T(8,128)S(1)}, u32[]{:S(2)}, u32[]{:S(2)}) %collective-permute-start) | collective-permute-done | bytes 131104 | tf_op jit(solution)/shard_map/ppermute | solution.py:26
  8.1 1.5 %collective-permute-done.1 = f32[2,128,128]{2,1,0:T(8,128)S(1)} collective-permute-done((f32[2,128,128]{2,1,0:T(8,128)S(1)}, f32[2,128,128]{2,1,0:T(8,128)S(1)}, u32[]{:S(2)}, u32[]{:S(2)}) %collective-permute-start.1) | collective-permute-done | bytes 131104 | tf_op jit(solution)/shard_map/ppermute | solution.py:26
  9.6 1.5 %collective-permute-start.2 = (f32[2,384,128]{2,1,0:T(8,128)S(1)}, f32[2,384,128]{2,1,0:T(8,128)S(1)}, u32[]{:S(2)}, u32[]{:S(2)}) collective-permute-start(f32[2,384,128]{2,1,0:T(8,128)S(1)} %pad_maximum_fusion.3), channel_id=1, source_target_pairs={{0,1},{1,0},{2,4},{3,5},{4,2},{5,3},{6,7},{7,6},{8,9},{9,8},{10,12... | collective-permute-start | bytes 1179656 | tf_op jit(solution)/shard_map/ppermute | solution.py:26
  11.1 0.2 collective-permute-start.3
  11.4 0.1 pad_add_fusion.1.info
  11.5 6.0 %collective-permute-done.2 = f32[2,384,128]{2,1,0:T(8,128)S(1)} collective-permute-done((f32[2,384,128]{2,1,0:T(8,128)S(1)}, f32[2,384,128]{2,1,0:T(8,128)S(1)}, u32[]{:S(2)}, u32[]{:S(2)}) %collective-permute-start.2) | collective-permute-done | bytes 393248 | tf_op jit(solution)/shard_map/ppermute | solution.py:26
  17.6 0.1 pad_maximum_fusion.padded
  17.7 0.8 copy-done.7
  18.5 0.2 copy-done.8
  18.6 0.2 copy-done.9
  18.8 0.1 copy-done
  18.9 0.1 copy-done.1
  19.0 0.1 copy-done.2
  19.0 0.1 copy-done.3
  19.1 0.1 copy-done.4
  19.2 0.2 copy-done.5
  19.4 0.2 copy-done.6
  19.5 6.0 %forward.1 = (f32[4,136,256]{2,1,0:T(8,128)S(1)}, f32[4,136,256]{2,1,0:T(8,128)S(1)}, bf16[512,512]{1,0:T(8,128)(2,1)S(1)}, bf16[512,512]{1,0:T(8,128)(2,1)S(1)}, f32[2,2,256,256]{3,2,1,0:T(8,128)S(1)}) custom-call(s32[2,2]{1,0:T(2,128)S(1)} %broadcast_subtract_fusion.offsets, s32[4]{0:T(128)S(1)} %pad_add_fusion.1.info, ...), custom_call_target="tpu_custom_call" | custom-call | flops 1610612736 | bytes 6291456 | tf_op jit(solution)/shard_map/forward/pallas_call | solution.py:320
  25.7 4.9 %backward.1 = (f32[4,64,256]{2,1,0:T(8,128)S(1)}, f32[4,64,256]{2,1,0:T(8,128)S(1)}, f32[3,384,128]{2,1,0:T(8,128)S(1)}, f32[3,384,128]{2,1,0:T(8,128)S(1)}, f32[3,384,128]{2,1,0:T(8,128)S(1)}) custom-call(s32[2,2]{1,0:T(2,128)S(1)} %broadcast_subtract_fusion.offsets, s32[4]{0:T(128)S(1)} %pad_add_fusion.1.info, ...), custom_call_target="tpu_custom_call" | custom-call | flops 1610612736 | bytes 6291456 | tf_op jit(solution)/shard_map/backward/pallas_call | solution.py:350
  30.6 0.6 collective-permute-start.9
  31.1 1.2 %collective-permute-done.9 = f32[4,64,256]{2,1,0:T(8,128)S(1)} collective-permute-done((f32[4,64,256]{2,1,0:T(8,128)S(1)}, f32[4,64,256]{2,1,0:T(8,128)S(1)}, u32[]{:S(2)}, u32[]{:S(2)}) %collective-permute-start.9) | collective-permute-done | bytes 262176 | tf_op jit(solution)/shard_map/ppermute | solution.py:26
  32.5 1.5 %collective-permute-start.11 = (f32[2,200,256]{2,1,0:T(8,128)S(1)}, f32[2,200,256]{2,1,0:T(8,128)S(1)}, u32[]{:S(2)}, u32[]{:S(2)}) collective-permute-start(f32[2,200,256]{2,1,0:T(8,128)S(1)} %pad_maximum_fusion.2), channel_id=1, source_target_pairs={{0,1},{1,0},{2,10},{3,11},{4,5},{5,4},{6,14},{7,15},{8,9},{9,8},{1... | collective-permute-start | bytes 1228808 | tf_op jit(solution)/shard_map/ppermute | solution.py:26
  33.9 6.5 %collective-permute-done.11 = f32[2,200,256]{2,1,0:T(8,128)S(1)} collective-permute-done((f32[2,200,256]{2,1,0:T(8,128)S(1)}, f32[2,200,256]{2,1,0:T(8,128)S(1)}, u32[]{:S(2)}, u32[]{:S(2)}) %collective-permute-start.11) | collective-permute-done | bytes 409632 | tf_op jit(solution)/shard_map/ppermute | solution.py:26
  40.5 1.7 %collective-permute-start.12 = (f32[1,200,256]{2,1,0:T(8,128)S(1)}, f32[1,200,256]{2,1,0:T(8,128)S(1)}, u32[]{:S(2)}, u32[]{:S(2)}) collective-permute-start(f32[1,200,256]{2,1,0:T(8,128)S(1)} %slice.103), channel_id=1, source_target_pairs={{0,8},{1,9},{2,3},{3,2},{4,12},{5,13},{6,7},{7,6},{8,0},{9,1},{10,... | collective-permute-start | bytes 614408 | tf_op jit(solution)/shard_map/ppermute | solution.py:26
  42.3 1.5 %collective-permute-start.5 = (f32[3,384,128]{2,1,0:T(8,128)S(1)}, f32[3,384,128]{2,1,0:T(8,128)}, u32[]{:S(2)}, u32[]{:S(2)}) collective-permute-start(f32[3,384,128]{2,1,0:T(8,128)S(1)} %get-tuple-element.21), channel_id=1, source_target_pairs={{2,4},{3,5},{4,2},{5,3},{10,12},{11,13},{12,10},{13,11},{18,20},{1... | collective-permute-start | bytes 1769480 | tf_op jit(solution)/shard_map/ppermute | solution.py:26
  43.8 2.6 %collective-permute-done.12 = f32[1,200,256]{2,1,0:T(8,128)S(1)} collective-permute-done((f32[1,200,256]{2,1,0:T(8,128)S(1)}, f32[1,200,256]{2,1,0:T(8,128)S(1)}, u32[]{:S(2)}, u32[]{:S(2)}) %collective-permute-start.12) | collective-permute-done | bytes 204832 | tf_op jit(solution)/shard_map/ppermute | solution.py:26
  46.4 1.0 %collective-permute-start.13 = (f32[1,200,256]{2,1,0:T(8,128)S(1)}, f32[1,200,256]{2,1,0:T(8,128)}, u32[]{:S(2)}, u32[]{:S(2)}) collective-permute-start(f32[1,200,256]{2,1,0:T(8,128)S(1)} %slice_add_fusion), channel_id=1, source_target_pairs={{0,4},{1,5},{2,18},{3,19},{4,0},{5,1},{6,22},{7,23},{8,12},{9,13},... | collective-permute-start | bytes 614408 | tf_op jit(solution)/shard_map/ppermute | solution.py:26
  47.4 9.0 %collective-permute-done.13 = f32[1,200,256]{2,1,0:T(8,128)} collective-permute-done((f32[1,200,256]{2,1,0:T(8,128)S(1)}, f32[1,200,256]{2,1,0:T(8,128)}, u32[]{:S(2)}, u32[]{:S(2)}) %collective-permute-start.13) | collective-permute-done | bytes 204832 | tf_op jit(solution)/shard_map/ppermute | solution.py:26
  56.5 1.0 %add.159 = f32[1,200,256]{2,1,0:T(8,128)S(1)} add(f32[1,200,256]{2,1,0:T(8,128)S(1)} %slice_add_fusion, f32[1,200,256]{2,1,0:T(8,128)} %collective-permute-done.13) | non-fusion elementwise | flops 51200 | bytes 614400 | tf_op jit(solution)/shard_map/add | solution.py:469
  57.4 4.2 %collective-permute-start.14 = (f32[1,200,256]{2,1,0:T(8,128)S(1)}, f32[1,200,256]{2,1,0:T(8,128)S(1)}, u32[]{:S(2)}, u32[]{:S(2)}) collective-permute-start(f32[1,200,256]{2,1,0:T(8,128)S(1)} %add.159), channel_id=1, source_target_pairs={{0,16},{1,17},{2,6},{3,7},{4,20},{5,21},{6,2},{7,3},{8,24},{9,25},... | collective-permute-start | bytes 614408 | tf_op jit(solution)/shard_map/ppermute | solution.py:26
  61.7 1.3 %add_add_fusion = f32[3,384,128]{2,1,0:T(8,128)S(1)} fusion(f32[3,384,128]{2,1,0:T(8,128)} %collective-permute-done.5, f32[3,384,128]{2,1,0:T(8,128)S(1)} %get-tuple-element.19, f32[3,384,128]{2,1,0:T(8,128)} %collective-permute-done.4), kind=kLoop, calls=%fused_computation.9 | loop fusion | flops 294912 | bytes 2359296 | tf_op jit(solution)/shard_map/add | solution.py:493
  63.0 5.1 %collective-permute-done.14 = f32[1,200,256]{2,1,0:T(8,128)S(1)} collective-permute-done((f32[1,200,256]{2,1,0:T(8,128)S(1)}, f32[1,200,256]{2,1,0:T(8,128)S(1)}, u32[]{:S(2)}, u32[]{:S(2)}) %collective-permute-start.14) | collective-permute-done | bytes 204832 | tf_op jit(solution)/shard_map/ppermute | solution.py:26
  68.3 2.1 %collective-permute-start.6 = (f32[3,128,128]{2,1,0:T(8,128)S(1)}, f32[3,128,128]{2,1,0:T(8,128)S(1)}, u32[]{:S(2)}, u32[]{:S(2)}) collective-permute-start(f32[3,128,128]{2,1,0:T(8,128)S(1)} %get-tuple-element.35), channel_id=1, source_target_pairs={{0,8},{1,9},{2,10},{3,11},{4,12},{5,13},{6,14},{7,15},{8,0},{9,1},... | collective-permute-start | bytes 589832 | tf_op jit(solution)/shard_map/ppermute | solution.py:26
  70.4 1.5 %collective-permute-start.7 = (f32[3,128,128]{2,1,0:T(8,128)S(1)}, f32[3,128,128]{2,1,0:T(8,128)S(1)}, u32[]{:S(2)}, u32[]{:S(2)}) collective-permute-start(f32[3,128,128]{2,1,0:T(8,128)S(1)} %get-tuple-element.34), channel_id=1, source_target_pairs={{0,1},{1,0},{2,3},{3,2},{4,5},{5,4},{6,7},{7,6},{8,16},{9,17},{10,... | collective-permute-start | bytes 589832 | tf_op jit(solution)/shard_map/ppermute | solution.py:26
  71.9 1.3 %collective-permute-done.15 = f32[4,32,256]{2,1,0:T(8,128)S(1)} collective-permute-done((f32[4,32,256]{2,1,0:T(8,128)S(1)}, f32[4,32,256]{2,1,0:T(8,128)S(1)}, u32[]{:S(2)}, u32[]{:S(2)}) %collective-permute-start.15) | collective-permute-done | bytes 131104 | tf_op jit(solution)/shard_map/ppermute | solution.py:26
  73.3 1.6 %collective-permute-start.16 = (f32[4,64,256]{2,1,0:T(8,128)S(1)}, f32[4,64,256]{2,1,0:T(8,128)S(1)}, u32[]{:S(2)}, u32[]{:S(2)}) collective-permute-start(f32[4,64,256]{2,1,0:T(8,128)S(1)} %pad_maximum_fusion.5), channel_id=1, source_target_pairs={{0,1},{1,0},{2,10},{3,11},{4,5},{5,4},{6,14},{7,15},{8,9},{9,8},{1... | collective-permute-start | bytes 786440 | tf_op jit(solution)/shard_map/ppermute | solution.py:26
  74.9 0.4 collective-permute-done.6
  75.3 0.7 collective-permute-done.7
  76.1 1.6 %collective-permute-start.8 = (f32[3,64,128]{2,1,0:T(8,128)S(1)}, f32[3,64,128]{2,1,0:T(8,128)S(1)}, u32[]{:S(2)}, u32[]{:S(2)}) collective-permute-start(f32[3,64,128]{2,1,0:T(8,128)S(1)} %constant_dynamic-slice_fusion), channel_id=1, source_target_pairs={{0,1},{1,0},{2,3},{3,2},{4,5},{5,4},{6,7},{7,6},{8,9},{9,8},{10,11... | collective-permute-start | bytes 294920 | tf_op jit(solution)/shard_map/ppermute | solution.py:504
  77.7 2.0 %collective-permute-done.16 = f32[4,64,256]{2,1,0:T(8,128)S(1)} collective-permute-done((f32[4,64,256]{2,1,0:T(8,128)S(1)}, f32[4,64,256]{2,1,0:T(8,128)S(1)}, u32[]{:S(2)}, u32[]{:S(2)}) %collective-permute-start.16) | collective-permute-done | bytes 262176 | tf_op jit(solution)/shard_map/ppermute | solution.py:26
  79.9 0.9 %collective-permute-done.8 = f32[3,64,128]{2,1,0:T(8,128)S(1)} collective-permute-done((f32[3,64,128]{2,1,0:T(8,128)S(1)}, f32[3,64,128]{2,1,0:T(8,128)S(1)}, u32[]{:S(2)}, u32[]{:S(2)}) %collective-permute-start.8) | collective-permute-done | bytes 98336 | tf_op jit(solution)/shard_map/ppermute | solution.py:504
  80.8 0.6 fusion.25
  81.5 0.3 collective-permute-done.17
  81.8 0.1 broadcast_select_fusion
  81.9 1.0 %fusion.8 = (f32[256,256]{1,0:T(8,128)}, f32[256,256]{1,0:T(8,128)}, f32[256,256]{1,0:T(8,128)}, f32[256,256]{1,0:T(8,128)}) fusion(f32[4,128,256]{2,1,0:T(8,128)S(1)} %get-tuple-element.30, f32[4,128,256]{2,1,0:T(8,128)S(1)} %get-tuple-element.31), kind=kLoop, calls=%fused_computation.24 | loop fusion | flops 262144 | bytes 2097152 | tf_op jit(solution)/shard_map/squeeze | solution.py:509
  (43 shorter events, 1.0 us)
Async XLA Ops:
  0.6 10.8 %copy-start.10 = (s32[2,2]{1,0:T(2,128)S(1)}, s32[2,2]{1,0:T(2,128)}, u32[]{:S(2)}) copy-start(s32[2,2]{1,0:T(2,128)} %param.21) | copy-start | bytes 52
  1.5 6.5 %collective-permute-start = (f32[2,128,128]{2,1,0:T(8,128)S(1)}, f32[2,128,128]{2,1,0:T(8,128)S(1)}, u32[]{:S(2)}, u32[]{:S(2)}) collective-permute-start(f32[2,128,128]{2,1,0:T(8,128)S(1)} %pad_maximum_fusion.6), channel_id=1, source_target_pairs={{0,1},{1,0},{2,3},{3,2},{4,5},{5,4},{6,7},{7,6},{8,16},{9,17},{10,... | collective-permute-start | bytes 393224 | tf_op jit(solution)/shard_map/ppermute | solution.py:26
  4.6 5.0 %collective-permute-start.1 = (f32[2,128,128]{2,1,0:T(8,128)S(1)}, f32[2,128,128]{2,1,0:T(8,128)S(1)}, u32[]{:S(2)}, u32[]{:S(2)}) collective-permute-start(f32[2,128,128]{2,1,0:T(8,128)S(1)} %pad_maximum_fusion.6), channel_id=1, source_target_pairs={{0,8},{1,9},{2,10},{3,11},{4,12},{5,13},{6,14},{7,15},{8,0},{9,1},... | collective-permute-start | bytes 393224 | tf_op jit(solution)/shard_map/ppermute | solution.py:26
  9.6 7.8 %collective-permute-start.2 = (f32[2,384,128]{2,1,0:T(8,128)S(1)}, f32[2,384,128]{2,1,0:T(8,128)S(1)}, u32[]{:S(2)}, u32[]{:S(2)}) collective-permute-start(f32[2,384,128]{2,1,0:T(8,128)S(1)} %pad_maximum_fusion.3), channel_id=1, source_target_pairs={{0,1},{1,0},{2,4},{3,5},{4,2},{5,3},{6,7},{7,6},{8,9},{9,8},{10,12... | collective-permute-start | bytes 1179656 | tf_op jit(solution)/shard_map/ppermute | solution.py:26
  11.1 6.4 %collective-permute-start.3 = (f32[2,384,128]{2,1,0:T(8,128)S(1)}, f32[2,384,128]{2,1,0:T(8,128)S(1)}, u32[]{:S(2)}, u32[]{:S(2)}) collective-permute-start(f32[2,384,128]{2,1,0:T(8,128)S(1)} %pad_maximum_fusion.3), channel_id=1, source_target_pairs={{0,2},{1,3},{2,0},{3,1},{4,6},{5,7},{6,4},{7,5},{8,10},{9,11},{10,... | collective-permute-start | bytes 1179656 | tf_op jit(solution)/shard_map/ppermute | solution.py:26
  17.4 1.0 %copy-start.7 = (bf16[512,512]{1,0:T(8,128)(2,1)S(1)}, bf16[512,512]{1,0:T(8,128)(2,1)}, u32[]{:S(2)}) copy-start(bf16[512,512]{1,0:T(8,128)(2,1)} %constant.132.clone.row_low) | copy-start | bytes 1572868
  17.4 1.2 %copy-start.8 = (bf16[512,512]{1,0:T(8,128)(2,1)S(1)}, bf16[512,512]{1,0:T(8,128)(2,1)}, u32[]{:S(2)}) copy-start(bf16[512,512]{1,0:T(8,128)(2,1)} %constant.133.clone.col_high) | copy-start | bytes 1572868
  17.4 1.4 %copy-start.9 = (bf16[512,512]{1,0:T(8,128)(2,1)S(1)}, bf16[512,512]{1,0:T(8,128)(2,1)}, u32[]{:S(2)}) copy-start(bf16[512,512]{1,0:T(8,128)(2,1)} %constant.134.clone.col_low) | copy-start | bytes 1572868
  17.5 1.4 %copy-start = (f32[256,256]{1,0:T(8,128)S(1)}, f32[256,256]{1,0:T(8,128)}, u32[]{:S(2)}) copy-start(f32[256,256]{1,0:T(8,128)} %probe_re.3) | copy-start | bytes 786436
  17.5 1.4 %copy-start.1 = (f32[256,256]{1,0:T(8,128)S(1)}, f32[256,256]{1,0:T(8,128)}, u32[]{:S(2)}) copy-start(f32[256,256]{1,0:T(8,128)} %probe_im.3) | copy-start | bytes 786436
  17.5 1.5 %copy-start.2 = (f32[256,256]{1,0:T(8,128)S(1)}, f32[256,256]{1,0:T(8,128)}, u32[]{:S(2)}) copy-start(f32[256,256]{1,0:T(8,128)} %gain_hbm.1) | copy-start | bytes 786436
  17.6 1.6 %copy-start.3 = (f32[256,256]{1,0:T(8,128)S(1)}, f32[256,256]{1,0:T(8,128)}, u32[]{:S(2)}) copy-start(f32[256,256]{1,0:T(8,128)} %dark_hbm.1) | copy-start | bytes 786436
  17.6 1.6 %copy-start.4 = (s32[256,256]{1,0:T(8,128)S(1)}, s32[256,256]{1,0:T(8,128)}, u32[]{:S(2)}) copy-start(s32[256,256]{1,0:T(8,128)} %good_hbm.1) | copy-start | bytes 786436
  17.6 1.8 %copy-start.5 = (f32[2,256,256]{2,1,0:T(8,128)S(1)}, f32[2,256,256]{2,1,0:T(8,128)}, u32[]{:S(2)}) copy-start(f32[2,256,256]{2,1,0:T(8,128)} %measured_hbm.1) | copy-start | bytes 1572868
  17.6 2.0 %copy-start.6 = (bf16[512,512]{1,0:T(8,128)(2,1)S(1)}, bf16[512,512]{1,0:T(8,128)(2,1)}, u32[]{:S(2)}) copy-start(bf16[512,512]{1,0:T(8,128)(2,1)} %constant.131.clone.row_high) | copy-start | bytes 1572868
  25.6 6.8 %collective-permute-start.10 = (f32[4,136,256]{2,1,0:T(8,128)S(1)}, f32[4,136,256]{2,1,0:T(8,128)S(1)}, u32[]{:S(2)}, u32[]{:S(2)}) collective-permute-start(f32[4,136,256]{2,1,0:T(8,128)S(1)} %get-tuple-element.25), channel_id=1, source_target_pairs={{0,2},{1,3},{2,0},{3,1},{4,6},{5,7},{6,4},{7,5},{8,10},{9,11},{10,... | collective-permute-start | bytes 1671176 | tf_op jit(solution)/shard_map/ppermute | solution.py:26
  30.6 1.7 %collective-permute-start.9 = (f32[4,64,256]{2,1,0:T(8,128)S(1)}, f32[4,64,256]{2,1,0:T(8,128)S(1)}, u32[]{:S(2)}, u32[]{:S(2)}) collective-permute-start(f32[4,64,256]{2,1,0:T(8,128)S(1)} %get-tuple-element.23), channel_id=1, source_target_pairs={{0,2},{1,3},{2,0},{3,1},{4,6},{5,7},{6,4},{7,5},{8,10},{9,11},{10,... | collective-permute-start | bytes 786440 | tf_op jit(solution)/shard_map/ppermute | solution.py:26
  32.5 8.0 %collective-permute-start.11 = (f32[2,200,256]{2,1,0:T(8,128)S(1)}, f32[2,200,256]{2,1,0:T(8,128)S(1)}, u32[]{:S(2)}, u32[]{:S(2)}) collective-permute-start(f32[2,200,256]{2,1,0:T(8,128)S(1)} %pad_maximum_fusion.2), channel_id=1, source_target_pairs={{0,1},{1,0},{2,10},{3,11},{4,5},{5,4},{6,14},{7,15},{8,9},{9,8},{1... | collective-permute-start | bytes 1228808 | tf_op jit(solution)/shard_map/ppermute | solution.py:26
  40.5 5.8 %collective-permute-start.12 = (f32[1,200,256]{2,1,0:T(8,128)S(1)}, f32[1,200,256]{2,1,0:T(8,128)S(1)}, u32[]{:S(2)}, u32[]{:S(2)}) collective-permute-start(f32[1,200,256]{2,1,0:T(8,128)S(1)} %slice.103), channel_id=1, source_target_pairs={{0,8},{1,9},{2,3},{3,2},{4,12},{5,13},{6,7},{7,6},{8,0},{9,1},{10,... | collective-permute-start | bytes 614408 | tf_op jit(solution)/shard_map/ppermute | solution.py:26
  42.3 19.4 %collective-permute-start.4 = (f32[3,384,128]{2,1,0:T(8,128)S(1)}, f32[3,384,128]{2,1,0:T(8,128)}, u32[]{:S(2)}, u32[]{:S(2)}) collective-permute-start(f32[3,384,128]{2,1,0:T(8,128)S(1)} %get-tuple-element.20), channel_id=1, source_target_pairs={{0,2},{1,3},{2,0},{3,1},{4,6},{5,7},{6,4},{7,5},{8,10},{9,11},{10,... | collective-permute-start | bytes 1769480 | tf_op jit(solution)/shard_map/ppermute | solution.py:26
  42.3 19.4 %collective-permute-start.5 = (f32[3,384,128]{2,1,0:T(8,128)S(1)}, f32[3,384,128]{2,1,0:T(8,128)}, u32[]{:S(2)}, u32[]{:S(2)}) collective-permute-start(f32[3,384,128]{2,1,0:T(8,128)S(1)} %get-tuple-element.21), channel_id=1, source_target_pairs={{2,4},{3,5},{4,2},{5,3},{10,12},{11,13},{12,10},{13,11},{18,20},{1... | collective-permute-start | bytes 1769480 | tf_op jit(solution)/shard_map/ppermute | solution.py:26
  46.4 10.1 %collective-permute-start.13 = (f32[1,200,256]{2,1,0:T(8,128)S(1)}, f32[1,200,256]{2,1,0:T(8,128)}, u32[]{:S(2)}, u32[]{:S(2)}) collective-permute-start(f32[1,200,256]{2,1,0:T(8,128)S(1)} %slice_add_fusion), channel_id=1, source_target_pairs={{0,4},{1,5},{2,18},{3,19},{4,0},{5,1},{6,22},{7,23},{8,12},{9,13},... | collective-permute-start | bytes 614408 | tf_op jit(solution)/shard_map/ppermute | solution.py:26
  57.4 10.7 %collective-permute-start.14 = (f32[1,200,256]{2,1,0:T(8,128)S(1)}, f32[1,200,256]{2,1,0:T(8,128)S(1)}, u32[]{:S(2)}, u32[]{:S(2)}) collective-permute-start(f32[1,200,256]{2,1,0:T(8,128)S(1)} %add.159), channel_id=1, source_target_pairs={{0,16},{1,17},{2,6},{3,7},{4,20},{5,21},{6,2},{7,3},{8,24},{9,25},... | collective-permute-start | bytes 614408 | tf_op jit(solution)/shard_map/ppermute | solution.py:26
  68.2 5.0 %collective-permute-start.15 = (f32[4,32,256]{2,1,0:T(8,128)S(1)}, f32[4,32,256]{2,1,0:T(8,128)S(1)}, u32[]{:S(2)}, u32[]{:S(2)}) collective-permute-start(f32[4,32,256]{2,1,0:T(8,128)S(1)} %pad_maximum_fusion.7), channel_id=1, source_target_pairs={{0,8},{1,9},{2,3},{3,2},{4,12},{5,13},{6,7},{7,6},{8,0},{9,1},{10,... | collective-permute-start | bytes 393224 | tf_op jit(solution)/shard_map/ppermute | solution.py:26
  68.3 7.0 %collective-permute-start.6 = (f32[3,128,128]{2,1,0:T(8,128)S(1)}, f32[3,128,128]{2,1,0:T(8,128)S(1)}, u32[]{:S(2)}, u32[]{:S(2)}) collective-permute-start(f32[3,128,128]{2,1,0:T(8,128)S(1)} %get-tuple-element.35), channel_id=1, source_target_pairs={{0,8},{1,9},{2,10},{3,11},{4,12},{5,13},{6,14},{7,15},{8,0},{9,1},... | collective-permute-start | bytes 589832 | tf_op jit(solution)/shard_map/ppermute | solution.py:26
  70.4 5.7 %collective-permute-start.7 = (f32[3,128,128]{2,1,0:T(8,128)S(1)}, f32[3,128,128]{2,1,0:T(8,128)S(1)}, u32[]{:S(2)}, u32[]{:S(2)}) collective-permute-start(f32[3,128,128]{2,1,0:T(8,128)S(1)} %get-tuple-element.34), channel_id=1, source_target_pairs={{0,1},{1,0},{2,3},{3,2},{4,5},{5,4},{6,7},{7,6},{8,16},{9,17},{10,... | collective-permute-start | bytes 589832 | tf_op jit(solution)/shard_map/ppermute | solution.py:26
  73.3 6.4 %collective-permute-start.16 = (f32[4,64,256]{2,1,0:T(8,128)S(1)}, f32[4,64,256]{2,1,0:T(8,128)S(1)}, u32[]{:S(2)}, u32[]{:S(2)}) collective-permute-start(f32[4,64,256]{2,1,0:T(8,128)S(1)} %pad_maximum_fusion.5), channel_id=1, source_target_pairs={{0,1},{1,0},{2,10},{3,11},{4,5},{5,4},{6,14},{7,15},{8,9},{9,8},{1... | collective-permute-start | bytes 786440 | tf_op jit(solution)/shard_map/ppermute | solution.py:26
  76.1 4.7 %collective-permute-start.8 = (f32[3,64,128]{2,1,0:T(8,128)S(1)}, f32[3,64,128]{2,1,0:T(8,128)S(1)}, u32[]{:S(2)}, u32[]{:S(2)}) collective-permute-start(f32[3,64,128]{2,1,0:T(8,128)S(1)} %constant_dynamic-slice_fusion), channel_id=1, source_target_pairs={{0,1},{1,0},{2,3},{3,2},{4,5},{5,4},{6,7},{7,6},{8,9},{9,8},{10,11... | collective-permute-start | bytes 294920 | tf_op jit(solution)/shard_map/ppermute | solution.py:504
  79.8 2.0 %collective-permute-start.17 = (f32[4,128,256]{2,1,0:T(8,128)S(1)}, f32[4,128,256]{2,1,0:T(8,128)S(1)}, u32[]{:S(2)}, u32[]{:S(2)}) collective-permute-start(f32[4,128,256]{2,1,0:T(8,128)S(1)} %pad_maximum_fusion.1), channel_id=1, source_target_pairs={{0,2},{1,3},{2,0},{3,1},{4,6},{5,7},{6,4},{7,5},{8,10},{9,11},{10,... | collective-permute-start | bytes 1572872 | tf_op jit(solution)/shard_map/ppermute | solution.py:26

commit v4 on v3

--- a/solution.py
+++ b/solution.py
@@ -13,6 +13,9 @@
 MESH_AXES = ("tx", "ty", "pa")
 ROWS = 32
 SUBLANES = 8
+SMEM = pl.BlockSpec(memory_space=pltpu.SMEM)
+VMEM = pl.BlockSpec(memory_space=pltpu.VMEM)
+HBM = pl.BlockSpec(memory_space=pltpu.HBM)
 
 
 def partner_swap(value, partner_of):
@@ -67,7 +70,7 @@
     imag = (-np.sin(angle) / math.sqrt(size)).astype(np.float32)
     row_form = np.block([[real, imag], [-imag, real]])
     col_form = np.block([[real, -imag], [imag, real]])
-    return (*split_table(row_form), *split_table(col_form))
+    return np.stack([*split_table(row_form), *split_table(col_form)])
 
 
 def split(value):
@@ -85,13 +88,13 @@
     return row - part, part
 
 
-def right_then_left(first_high, first_low, second_high, second_low, x_high, x_low, y_high, y_low, line, plane):
-    slots, _, size = plane.shape
-    for slot in range(slots):
+def right_then_left(which, first_high, first_low, second_high, second_low, x_high, x_low, y_high, y_low, line, plane):
+    size = plane.shape[2]
+    for slot in which:
         here = pl.ds(slot * size, size)
-        line[...] = three_pass(x_high[here, :], x_low[here, :], first_high[...], first_low[...])
+        line[slot] = three_pass(x_high[here, :], x_low[here, :], first_high[...], first_low[...])
         for part in range(2):
-            high, low = split(line[:, part * size : (part + 1) * size])
+            high, low = split(line[slot, :, part * size : (part + 1) * size])
             y_high[part * size : (part + 1) * size, here] = high
             y_low[part * size : (part + 1) * size, here] = low
         plane[slot] = three_pass(second_high[...], second_low[...], y_high[:, here], y_low[:, here])
@@ -123,25 +126,17 @@
     padded,
     probe_re,
     probe_im,
-    row_high,
-    row_low,
-    col_high,
-    col_low,
-    measured_hbm,
-    gain_hbm,
-    dark_hbm,
-    good_hbm,
+    tables,
+    measured,
+    gain,
+    dark,
+    good,
     kept,
     sent,
     x_high,
     x_low,
     win,
     sums,
-    measured,
-    gain,
-    dark,
-    good,
-    sem,
     y_high,
     y_low,
     line,
@@ -151,22 +146,13 @@
     size = probe_re.shape[0]
     side = padded.shape[1]
     steps = size // ROWS
-    copies = [
-        pltpu.make_async_copy(source, target, sem.at[k])
-        for k, (source, target) in enumerate(
-            ((measured_hbm, measured), (gain_hbm, gain), (dark_hbm, dark), (good_hbm, good))
-        )
-    ]
-    for copy in copies:
-        copy.start()
-
     for slot in range(slots):
         row, row_part = aligned(offsets[slot, 0])
         back_rows = lax.rem(ROWS + SUBLANES - row_part, ROWS + SUBLANES)
         back_cols = lax.rem(side - offsets[slot, 1], side)
 
-        def load(step, _):
-            at = pl.multiple_of(step * ROWS, ROWS)
+        def load(step):
+            at = step * ROWS
             here = pl.ds(at, ROWS)
             parts = []
             for part in range(2):
@@ -177,22 +163,20 @@
             wr, wi = parts
             pr, pi = probe_re[here, :], probe_im[here, :]
             put_x(x_high, x_low, slot, size, at, pr * wr - pi * wi, pr * wi + pi * wr)
-            return 0
-
-        lax.fori_loop(0, steps, load, 0)
-
-    right_then_left(
-        row_high, row_low, col_high, col_low, x_high, x_low, y_high, y_low, line, plane
-    )
-    for copy in copies:
-        copy.wait()
+
+        for step in range(steps):
+            load(step)
+        right_then_left(
+            (slot,), *(tables.at[k] for k in (0, 1, 2, 3)), x_high, x_low, y_high, y_low, line, plane
+        )
+
     blocks, depth, _ = sums.shape
     live_rows = jnp.full((SUBLANES, size), info[0].astype(jnp.float32), jnp.float32)
     for block in range(blocks):
         sums[block, depth - SUBLANES :, :] = live_rows
 
-    def detect(step, _):
-        at = pl.multiple_of(step * ROWS, ROWS)
+    def detect(step):
+        at = step * ROWS
         here = pl.ds(at, ROWS)
         valid = good[here, :].astype(jnp.float32)
         values = [0.0] * 4
@@ -211,72 +195,102 @@
             terms = (live * (wr * wr + wi * wi), resid * inten, weight * inten * inten, resid)
             values = [value + term for value, term in zip(values, terms)]
         put_sums(sums, info, step, values)
-        return 0
-
-    lax.fori_loop(0, steps, detect, 0)
+
+    for step in range(steps):
+        detect(step)
     kept[...] = sums[: blocks // 2]
     sent[...] = sums[blocks // 2 :]
 
 
+def stage_kernel(*refs):
+    count = (len(refs) - 1) // 2
+    copies = [
+        pltpu.make_async_copy(source, target, refs[-1].at[k])
+        for k, (source, target) in enumerate(zip(refs[:count], refs[count : 2 * count]))
+    ]
+    for copy in copies:
+        copy.start()
+    for copy in copies:
+        copy.wait()
+
+
+def stage(*arrays):
+    return pl.pallas_call(
+        stage_kernel,
+        out_shape=tuple(jax.ShapeDtypeStruct(a.shape, a.dtype) for a in arrays),
+        in_specs=[HBM] * len(arrays),
+        out_specs=(VMEM,) * len(arrays),
+        scratch_shapes=[pltpu.SemaphoreType.DMA((len(arrays),))],
+        compiler_params=pltpu.CompilerParams(vmem_limit_bytes=1024 * 1024),
+        name="stage",
+    )(*arrays)
+
+
 def backward_kernel(
-    offsets,
     info,
     x_high,
     x_low,
     win,
+    tables,
+    kept,
+    sent,
+    plane,
+    sums,
+    y_high,
+    y_low,
+    line,
+):
+    slots, _, size, _ = win.shape
+    right_then_left(
+        range(slots), *(tables.at[k] for k in (2, 3, 0, 1)), x_high, x_low, y_high, y_low, line, plane
+    )
+    for step in range(size // ROWS):
+        at = step * ROWS
+        here = pl.ds(at, ROWS)
+        values = [0.0] * 2
+        for slot in range(slots):
+            live = jnp.where(slot < info[0], 1.0, 0.0).astype(jnp.float32)
+            br = live * plane[slot, here, :]
+            bi = live * plane[slot, pl.ds(size + at, ROWS), :]
+            wr, wi = win[slot, 0, here, :], win[slot, 1, here, :]
+            values = [values[0] + wr * br + wi * bi, values[1] + wr * bi - wi * br]
+        put_sums(sums, info, step, values)
+    kept[...] = sums[: sums.shape[0] // 2]
+    sent[...] = sums[sums.shape[0] // 2 :]
+
+
+def place_kernel(
+    offsets,
+    info,
+    plane,
     probe_re,
     probe_im,
-    row_high,
-    row_low,
-    col_high,
-    col_low,
-    kept,
-    sent,
     to_one,
     inner,
     to_zero,
-    sums,
     accum,
-    y_high,
-    y_low,
-    line,
-    plane,
 ):
-    slots, _, size, _ = win.shape
+    slots, _, size = plane.shape
     side = accum.shape[1]
     tile = inner.shape[2]
     half = to_one.shape[2]
-    steps = size // ROWS
     accum[...] = jnp.zeros_like(accum)
-    right_then_left(
-        col_high, col_low, row_high, row_low, x_high, x_low, y_high, y_low, line, plane
-    )
-
-    def place(step, _):
-        at = pl.multiple_of(step * ROWS, ROWS)
+    for step in range(size // ROWS):
+        at = step * ROWS
         here = pl.ds(at, ROWS)
         pr, pi = probe_re[here, :], probe_im[here, :]
         power = pr * pr + pi * pi
-        values = [0.0] * 2
         for slot in range(slots):
             live = jnp.where(slot < info[0], 1.0, 0.0).astype(jnp.float32)
             row, row_part = aligned(offsets[slot, 0])
             col = offsets[slot, 1]
             br = live * plane[slot, here, :]
             bi = live * plane[slot, pl.ds(size + at, ROWS), :]
-            wr, wi = win[slot, 0, here, :], win[slot, 1, here, :]
-            values = [values[0] + wr * br + wi * bi, values[1] + wr * bi - wi * br]
             there = pl.ds(pl.multiple_of(row + at, SUBLANES), ROWS + SUBLANES)
             for part, term in enumerate((pr * br + pi * bi, pr * bi - pi * br, live * power)):
                 wide = jnp.pad(term, ((0, SUBLANES), (0, side - size)))
                 wide = pltpu.roll(pltpu.roll(wide, row_part, axis=0), col, axis=1)
                 accum[part, there, :] += wide
-        put_sums(sums, info, step, values)
-        return 0
-
-    lax.fori_loop(0, steps, place, 0)
-    kept[...] = sums[: sums.shape[0] // 2]
-    sent[...] = sums[sums.shape[0] // 2 :]
     odd = info[3] == 1
     inner[...] = accum[:, :, half : half + tile]
 
@@ -291,16 +305,11 @@
         to_zero[...] = accum[:, :, half + tile :]
 
 
-SMEM = pl.BlockSpec(memory_space=pltpu.SMEM)
-VMEM = pl.BlockSpec(memory_space=pltpu.VMEM)
-HBM = pl.BlockSpec(memory_space=pltpu.HBM)
-
-
 def work_buffers(slots, size):
     return [
         pltpu.VMEM((2 * size, slots * size), jnp.bfloat16),
         pltpu.VMEM((2 * size, slots * size), jnp.bfloat16),
-        pltpu.VMEM((size, 2 * size), jnp.float32),
+        pltpu.VMEM((slots, size, 2 * size), jnp.float32),
         pltpu.VMEM((slots, 2 * size, size), jnp.float32),
     ]
 
@@ -326,46 +335,55 @@
             jax.ShapeDtypeStruct((slots * size, 2 * size), jnp.bfloat16),
             jax.ShapeDtypeStruct((slots, 2, size, size), jnp.float32),
         ),
-        in_specs=[SMEM] * 2 + [VMEM] * 7 + [HBM] * 4,
+        in_specs=[SMEM] * 2 + [VMEM] * 8,
         out_specs=(VMEM,) * 5,
         scratch_shapes=[
             pltpu.VMEM((blocks, depth, size), jnp.float32),
-            pltpu.VMEM((slots, size, size), jnp.float32),
-            pltpu.VMEM((size, size), jnp.float32),
-            pltpu.VMEM((size, size), jnp.float32),
-            pltpu.VMEM((size, size), jnp.int32),
-            pltpu.SemaphoreType.DMA((4,)),
             *work_buffers(slots, size),
         ],
         name="forward",
         **kernel_options(slots, size),
-    )(offsets, info, padded, probe_re, probe_im, *tables, measured, gain, dark, good)
-
-
-def backward(offsets, info, x_high, x_low, win, probe_re, probe_im, tables, tile, blocks):
+    )(offsets, info, padded, probe_re, probe_im, tables, measured, gain, dark, good)
+
+
+def backward(info, x_high, x_low, win, tables, blocks):
     slots, _, size, _ = win.shape
-    half = size // 2
-    side = tile + size
     depth = 2 * (size // blocks)
     return pl.pallas_call(
         backward_kernel,
         out_shape=(
             jax.ShapeDtypeStruct((blocks // 2, depth, size), jnp.float32),
             jax.ShapeDtypeStruct((blocks // 2, depth, size), jnp.float32),
+            jax.ShapeDtypeStruct((slots, 2 * size, size), jnp.float32),
+        ),
+        in_specs=[SMEM] + [VMEM] * 4,
+        out_specs=(VMEM,) * 3,
+        scratch_shapes=[
+            pltpu.VMEM((blocks, depth, size), jnp.float32),
+            *work_buffers(slots, size)[:-1],
+        ],
+        name="backward",
+        **kernel_options(slots, size),
+    )(info, x_high, x_low, win, tables)
+
+
+def place(offsets, info, plane, probe_re, probe_im, tile):
+    size = probe_re.shape[0]
+    half = size // 2
+    side = tile + size
+    return pl.pallas_call(
+        place_kernel,
+        out_shape=(
             jax.ShapeDtypeStruct((3, side, half), jnp.float32),
             jax.ShapeDtypeStruct((3, side, tile), jnp.float32),
             jax.ShapeDtypeStruct((3, side, half), jnp.float32),
         ),
-        in_specs=[SMEM] * 2 + [VMEM] * 9,
-        out_specs=(VMEM,) * 5,
-        scratch_shapes=[
-            pltpu.VMEM((blocks, depth, size), jnp.float32),
-            pltpu.VMEM((3, side, side), jnp.float32),
-            *work_buffers(slots, size),
-        ],
-        name="backward",
-        **kernel_options(slots, size),
-    )(offsets, info, x_high, x_low, win, probe_re, probe_im, *tables)
+        in_specs=[SMEM] * 2 + [VMEM] * 3,
+        out_specs=(VMEM,) * 3,
+        scratch_shapes=[pltpu.VMEM((3, side, side), jnp.float32)],
+        name="place",
+        **kernel_options(plane.shape[0], size),
+    )(offsets, info, plane, probe_re, probe_im)
 
 
 def exchange_steps(n_tx, n_ty, n_pa):
@@ -447,13 +465,16 @@
     mine = block_of(t, y, p)
     other = block_of(*halving[0][0](t, y, p))
     info = jnp.stack([counts[0], mine, other, y % 2]).astype(jnp.int32)
+    tables, measured, probe_real, probe_imaginary, gain, dark, pixel_good = stage(
+        jnp.asarray(tables), measured, probe_real, probe_imaginary, gain, dark, pixel_good
+    )
     *early, x_high, x_low, win = forward(
         offsets, info, padded, probe_real, probe_imaginary, tables,
         measured, gain, dark, pixel_good, blocks,
     )
-    *late, to_one, inner, to_zero = backward(
-        offsets, info, x_high, x_low, win, probe_real, probe_imaginary, tables,
-        tile_side, blocks,
+    *late, plane = backward(info, x_high, x_low, win, tables, blocks)
+    to_one, inner, to_zero = place(
+        offsets, info, plane, probe_real, probe_imaginary, tile_side
     )
 
     def first_half(kept, sent):

time: 83.1 us -> 84 us (1.011)
  local copies, waits for them, and re-layouts: 1.92 us -> 7.42 us
  starting transfers between devices: 23.9 us -> 19.2 us
  Pallas kernels: 10.9 us -> 9.67 us
  waiting for transfers between devices: 38.8 us -> 39.9 us
    unnamed x22 -> x16, local copies, waits for them, and re-layouts: 1.89 us -> 7.38 us
    ppermute x17, starting transfers between devices: 22.3 us -> 18.7 us  [partner_swap(): return lax.ppermute(value, MESH_AXES, moves)]
    pallas_call x0 -> x2, Pallas kernels: none -> 2.1 us  [the longest x1 1.76 us: place(): pl.pallas_call(place_kernel, out_shape=(jax.ShapeDtypeStruct((3, side, ha...]
    pallas_call x1, Pallas kernels: 6.02 us -> 4.22 us  [forward(): pl.pallas_call(forward_kernel, out_shape=(jax.ShapeDtypeStruct((blocks //...]
    pallas_call x1, Pallas kernels: 4.9 us -> 3.36 us  [backward(): pl.pallas_call(backward_kernel, out_shape=(jax.ShapeDtypeStruct((blocks /...]
    ppermute x17, waiting for transfers between devices: 37.8 us -> 39 us  [partner_swap(): return lax.ppermute(value, MESH_AXES, moves)]
    ppermute x1, starting transfers between devices: 1.61 us -> 0.43 us  [update(): sums = kept + lax.ppermute(sent, 'pa', [(i, i ^ bit) for i in range(n_pa)])]
  transfers between devices with their start and end apart: 18 -> 18, of which waited for: 14 -> 12; matrix products, arithmetic and copies ran while one was open for 4% -> 4% of each run, Pallas kernels for 6% -> 7%
where the time goes in v4:
time: 84 us; the launch traced here: 83.5 us
  waiting for transfers between devices  39.9 us (48%)
  starting transfers between devices  19.2 us (23%)
  Pallas kernels  9.67 us (12%)
  local copies, waits for them, and re-layouts  7.42 us (9%)
  other arithmetic  5.73 us (7%)
  between operations  1.55 us (2%)
    ppermute x17, waiting for transfers between devices, partner_swap(): return lax.ppermute(value, MESH_AXES, moves)  39 us
    ppermute x17, starting transfers between devices, partner_swap(): return lax.ppermute(value, MESH_AXES, moves)  18.7 us
    unnamed x16, local copies, waits for them, and re-layouts  7.38 us
    pallas_call x1, Pallas kernels, forward(): pl.pallas_call(forward_kernel, out_shape=(jax.ShapeDtypeStruct((blocks //...  4.22 us
    pallas_call x1, Pallas kernels, backward(): pl.pallas_call(backward_kernel, out_shape=(jax.ShapeDtypeStruct((blocks /...  3.36 us
    pallas_call x1, Pallas kernels, place(): pl.pallas_call(place_kernel, out_shape=(jax.ShapeDtypeStruct((3, side, ha...  1.76 us
  transfers between devices with their start and end apart: 18, of which 12 were waited for; matrix products, arithmetic and copies ran while one was open for 4% of the time, Pallas kernels for 7%

profile of v4, /device:TPU:0, one launch (start us, length us, event | category | flops | bytes accessed | tf_op | source)
XLA Modules:
  0.0 83.5 jit_solution(7746552053657449359)
XLA Ops:
  0.6 0.9 %pad_maximum_fusion.6 = f32[2,128,128]{2,1,0:T(8,128)S(1)} fusion(f32[1,128,128]{2,1,0:T(8,128)} %bitcast.54, f32[1,128,128]{2,1,0:T(8,128)} %bitcast.55), kind=kLoop, calls=%fused_computation.33 | loop fusion | flops 32768 | bytes 262144 | tf_op jit(solution)/shard_map/stack | solution.py:443
  1.5 3.0 %collective-permute-start = (f32[2,128,128]{2,1,0:T(8,128)S(1)}, f32[2,128,128]{2,1,0:T(8,128)S(1)}, u32[]{:S(2)}, u32[]{:S(2)}) collective-permute-start(f32[2,128,128]{2,1,0:T(8,128)S(1)} %pad_maximum_fusion.6), channel_id=1, source_target_pairs={{0,1},{1,0},{2,3},{3,2},{4,5},{5,4},{6,7},{7,6},{8,16},{9,17},{10,... | collective-permute-start | bytes 393224 | tf_op jit(solution)/shard_map/ppermute | solution.py:29
  4.5 1.7 %collective-permute-start.1 = (f32[2,128,128]{2,1,0:T(8,128)S(1)}, f32[2,128,128]{2,1,0:T(8,128)S(1)}, u32[]{:S(2)}, u32[]{:S(2)}) collective-permute-start(f32[2,128,128]{2,1,0:T(8,128)S(1)} %pad_maximum_fusion.6), channel_id=1, source_target_pairs={{0,8},{1,9},{2,10},{3,11},{4,12},{5,13},{6,14},{7,15},{8,0},{9,1},... | collective-permute-start | bytes 393224 | tf_op jit(solution)/shard_map/ppermute | solution.py:29
  6.9 1.6 %copy-done = bf16[4,512,512]{2,1,0:T(8,128)(2,1)S(1)} copy-done((bf16[4,512,512]{2,1,0:T(8,128)(2,1)S(1)}, bf16[4,512,512]{2,1,0:T(8,128)(2,1)}, u32[]{:S(2)}) %copy-start) | copy-done | bytes 2097176
  8.5 1.0 %copy-done.1 = f32[2,256,256]{2,1,0:T(8,128)S(1)} copy-done((f32[2,256,256]{2,1,0:T(8,128)S(1)}, f32[2,256,256]{2,1,0:T(8,128)}, u32[]{:S(2)}) %copy-start.1) | copy-done | bytes 524312
  9.5 0.9 %copy-done.2 = f32[256,256]{1,0:T(8,128)S(1)} copy-done((f32[256,256]{1,0:T(8,128)S(1)}, f32[256,256]{1,0:T(8,128)}, u32[]{:S(2)}) %copy-start.2) | copy-done | bytes 262168
  10.5 0.9 %copy-done.3 = f32[256,256]{1,0:T(8,128)S(1)} copy-done((f32[256,256]{1,0:T(8,128)S(1)}, f32[256,256]{1,0:T(8,128)}, u32[]{:S(2)}) %copy-start.3) | copy-done | bytes 262168
  11.4 0.9 %copy-done.4 = f32[256,256]{1,0:T(8,128)S(1)} copy-done((f32[256,256]{1,0:T(8,128)S(1)}, f32[256,256]{1,0:T(8,128)}, u32[]{:S(2)}) %copy-start.4) | copy-done | bytes 262168
  12.4 0.9 %copy-done.5 = f32[256,256]{1,0:T(8,128)S(1)} copy-done((f32[256,256]{1,0:T(8,128)S(1)}, f32[256,256]{1,0:T(8,128)}, u32[]{:S(2)}) %copy-start.5) | copy-done | bytes 262168
  13.3 0.9 %copy-done.6 = s32[256,256]{1,0:T(8,128)S(1)} copy-done((s32[256,256]{1,0:T(8,128)S(1)}, s32[256,256]{1,0:T(8,128)}, u32[]{:S(2)}) %copy-start.6) | copy-done | bytes 262168
  14.3 0.3 stage.1
  14.7 1.6 %collective-permute-start.2 = (f32[2,384,128]{2,1,0:T(8,128)S(1)}, f32[2,384,128]{2,1,0:T(8,128)S(1)}, u32[]{:S(2)}, u32[]{:S(2)}) collective-permute-start(f32[2,384,128]{2,1,0:T(8,128)S(1)} %pad_maximum_fusion.3), channel_id=1, source_target_pairs={{0,1},{1,0},{2,4},{3,5},{4,2},{5,3},{6,7},{7,6},{8,9},{9,8},{10,12... | collective-permute-start | bytes 1179656 | tf_op jit(solution)/shard_map/ppermute | solution.py:29
  16.3 0.1 collective-permute-start.3
  16.4 0.1 pad_add_fusion
  16.5 0.1 pad_add_fusion.1.info
  16.6 6.0 %collective-permute-done.2 = f32[2,384,128]{2,1,0:T(8,128)S(1)} collective-permute-done((f32[2,384,128]{2,1,0:T(8,128)S(1)}, f32[2,384,128]{2,1,0:T(8,128)S(1)}, u32[]{:S(2)}, u32[]{:S(2)}) %collective-permute-start.2) | collective-permute-done | bytes 393248 | tf_op jit(solution)/shard_map/ppermute | solution.py:29
  22.6 0.1 pad_maximum_fusion.padded
  22.7 4.2 %forward.1 = (f32[4,136,256]{2,1,0:T(8,128)S(1)}, f32[4,136,256]{2,1,0:T(8,128)S(1)}, bf16[512,512]{1,0:T(8,128)(2,1)S(1)}, bf16[512,512]{1,0:T(8,128)(2,1)S(1)}, f32[2,2,256,256]{3,2,1,0:T(8,128)S(1)}) custom-call(s32[2,2]{1,0:T(2,128)S(1)} %broadcast_subtract_fusion.offsets, s32[4]{0:T(128)S(1)} %pad_add_fusion.1.info, ...), custom_call_target="tpu_custom_call" | custom-call | flops 1610612736 | bytes 6291456 | tf_op jit(solution)/shard_map/forward/pallas_call | solution.py:329
  27.0 3.4 %backward.1 = (f32[4,64,256]{2,1,0:T(8,128)S(1)}, f32[4,64,256]{2,1,0:T(8,128)S(1)}, f32[2,512,256]{2,1,0:T(8,128)S(1)}) custom-call(s32[4]{0:T(128)S(1)} %pad_add_fusion.1.info, bf16[512,512]{1,0:T(8,128)(2,1)S(1)} %get-tuple-element.31.x_high, bf16[512,512]{1,0:T(8,128)(2,1)S(1)} %get-tuple-element.32.x_low, f32[2,2,256,256]{3,2,1,0:T(8,128)S(1)} %get-tuple-element.33.win, ...), custom_call_target="tpu_custom_call" | custom-call | flops 1610612736 | bytes 6291456 | tf_op jit(solution)/shard_map/backward/pallas_call | solution.py:352
  30.4 0.6 collective-permute-start.9
  30.9 1.2 %collective-permute-done.9 = f32[4,64,256]{2,1,0:T(8,128)S(1)} collective-permute-done((f32[4,64,256]{2,1,0:T(8,128)S(1)}, f32[4,64,256]{2,1,0:T(8,128)S(1)}, u32[]{:S(2)}, u32[]{:S(2)}) %collective-permute-start.9) | collective-permute-done | bytes 262176 | tf_op jit(solution)/shard_map/ppermute | solution.py:29
  32.3 1.6 %collective-permute-start.11 = (f32[2,200,256]{2,1,0:T(8,128)S(1)}, f32[2,200,256]{2,1,0:T(8,128)S(1)}, u32[]{:S(2)}, u32[]{:S(2)}) collective-permute-start(f32[2,200,256]{2,1,0:T(8,128)S(1)} %pad_maximum_fusion.2), channel_id=1, source_target_pairs={{0,1},{1,0},{2,10},{3,11},{4,5},{5,4},{6,14},{7,15},{8,9},{9,8},{1... | collective-permute-start | bytes 1228808 | tf_op jit(solution)/shard_map/ppermute | solution.py:29
  33.8 6.4 %collective-permute-done.11 = f32[2,200,256]{2,1,0:T(8,128)S(1)} collective-permute-done((f32[2,200,256]{2,1,0:T(8,128)S(1)}, f32[2,200,256]{2,1,0:T(8,128)S(1)}, u32[]{:S(2)}, u32[]{:S(2)}) %collective-permute-start.11) | collective-permute-done | bytes 409632 | tf_op jit(solution)/shard_map/ppermute | solution.py:29
  40.4 0.4 collective-permute-start.12
  40.8 1.8 %place.1 = (f32[3,384,128]{2,1,0:T(8,128)S(1)}, f32[3,384,128]{2,1,0:T(8,128)S(1)}, f32[3,384,128]{2,1,0:T(8,128)S(1)}) custom-call(s32[2,2]{1,0:T(2,128)S(1)} %broadcast_subtract_fusion.offsets, s32[4]{0:T(128)S(1)} %pad_add_fusion.1.info, f32[2,512,256]{2,1,0:T(8,128)S(1)} %get-tuple-element.34.plane, f32[256,256]{1,0:T(8,128)S(1)} %get-tuple-element.24.probe_re, ...), custom_call_target="tpu_custom_call" | custom-call | flops 1610612736 | bytes 6291456 | tf_op jit(solution)/shard_map/place/pallas_call | solution.py:374
  42.6 0.4 collective-permute-start.4
  43.0 1.5 %collective-permute-start.5 = (f32[3,384,128]{2,1,0:T(8,128)S(1)}, f32[3,384,128]{2,1,0:T(8,128)}, u32[]{:S(2)}, u32[]{:S(2)}) collective-permute-start(f32[3,384,128]{2,1,0:T(8,128)S(1)} %get-tuple-element.37), channel_id=1, source_target_pairs={{2,4},{3,5},{4,2},{5,3},{10,12},{11,13},{12,10},{13,11},{18,20},{1... | collective-permute-start | bytes 1769480 | tf_op jit(solution)/shard_map/ppermute | solution.py:29
  44.5 1.7 %collective-permute-done.12 = f32[1,200,256]{2,1,0:T(8,128)S(1)} collective-permute-done((f32[1,200,256]{2,1,0:T(8,128)S(1)}, f32[1,200,256]{2,1,0:T(8,128)S(1)}, u32[]{:S(2)}, u32[]{:S(2)}) %collective-permute-start.12) | collective-permute-done | bytes 204832 | tf_op jit(solution)/shard_map/ppermute | solution.py:29
  46.2 1.0 %collective-permute-start.13 = (f32[1,200,256]{2,1,0:T(8,128)S(1)}, f32[1,200,256]{2,1,0:T(8,128)}, u32[]{:S(2)}, u32[]{:S(2)}) collective-permute-start(f32[1,200,256]{2,1,0:T(8,128)S(1)} %slice_add_fusion), channel_id=1, source_target_pairs={{0,4},{1,5},{2,18},{3,19},{4,0},{5,1},{6,22},{7,23},{8,12},{9,13},... | collective-permute-start | bytes 614408 | tf_op jit(solution)/shard_map/ppermute | solution.py:29
  47.2 9.6 %collective-permute-done.13 = f32[1,200,256]{2,1,0:T(8,128)} collective-permute-done((f32[1,200,256]{2,1,0:T(8,128)S(1)}, f32[1,200,256]{2,1,0:T(8,128)}, u32[]{:S(2)}, u32[]{:S(2)}) %collective-permute-start.13) | collective-permute-done | bytes 204832 | tf_op jit(solution)/shard_map/ppermute | solution.py:29
  56.8 1.0 %add.159 = f32[1,200,256]{2,1,0:T(8,128)S(1)} add(f32[1,200,256]{2,1,0:T(8,128)S(1)} %slice_add_fusion, f32[1,200,256]{2,1,0:T(8,128)} %collective-permute-done.13) | non-fusion elementwise | flops 51200 | bytes 614400 | tf_op jit(solution)/shard_map/add | solution.py:490
  57.8 3.9 %collective-permute-start.14 = (f32[1,200,256]{2,1,0:T(8,128)S(1)}, f32[1,200,256]{2,1,0:T(8,128)S(1)}, u32[]{:S(2)}, u32[]{:S(2)}) collective-permute-start(f32[1,200,256]{2,1,0:T(8,128)S(1)} %add.159), channel_id=1, source_target_pairs={{0,16},{1,17},{2,6},{3,7},{4,20},{5,21},{6,2},{7,3},{8,24},{9,25},... | collective-permute-start | bytes 614408 | tf_op jit(solution)/shard_map/ppermute | solution.py:29
  61.6 1.3 %add_add_fusion = f32[3,384,128]{2,1,0:T(8,128)S(1)} fusion(f32[3,384,128]{2,1,0:T(8,128)} %collective-permute-done.5, f32[3,384,128]{2,1,0:T(8,128)S(1)} %get-tuple-element.35, f32[3,384,128]{2,1,0:T(8,128)} %collective-permute-done.4), kind=kLoop, calls=%fused_computation.9 | loop fusion | flops 294912 | bytes 2359296 | tf_op jit(solution)/shard_map/add | solution.py:514
  63.0 5.7 %collective-permute-done.14 = f32[1,200,256]{2,1,0:T(8,128)S(1)} collective-permute-done((f32[1,200,256]{2,1,0:T(8,128)S(1)}, f32[1,200,256]{2,1,0:T(8,128)S(1)}, u32[]{:S(2)}, u32[]{:S(2)}) %collective-permute-start.14) | collective-permute-done | bytes 204832 | tf_op jit(solution)/shard_map/ppermute | solution.py:29
  68.8 0.5 collective-permute-start.15
  69.3 1.7 %collective-permute-start.6 = (f32[3,128,128]{2,1,0:T(8,128)S(1)}, f32[3,128,128]{2,1,0:T(8,128)S(1)}, u32[]{:S(2)}, u32[]{:S(2)}) collective-permute-start(f32[3,128,128]{2,1,0:T(8,128)S(1)} %get-tuple-element.51), channel_id=1, source_target_pairs={{0,8},{1,9},{2,10},{3,11},{4,12},{5,13},{6,14},{7,15},{8,0},{9,1},... | collective-permute-start | bytes 589832 | tf_op jit(solution)/shard_map/ppermute | solution.py:29
  71.0 0.4 collective-permute-start.7
  71.4 2.5 %collective-permute-done.15 = f32[4,32,256]{2,1,0:T(8,128)S(1)} collective-permute-done((f32[4,32,256]{2,1,0:T(8,128)S(1)}, f32[4,32,256]{2,1,0:T(8,128)S(1)}, u32[]{:S(2)}, u32[]{:S(2)}) %collective-permute-start.15) | collective-permute-done | bytes 131104 | tf_op jit(solution)/shard_map/ppermute | solution.py:29
  73.9 0.4 collective-permute-start.16
  74.3 1.7 %collective-permute-done.6 = f32[3,128,128]{2,1,0:T(8,128)S(1)} collective-permute-done((f32[3,128,128]{2,1,0:T(8,128)S(1)}, f32[3,128,128]{2,1,0:T(8,128)S(1)}, u32[]{:S(2)}, u32[]{:S(2)}) %collective-permute-start.6) | collective-permute-done | bytes 196640 | tf_op jit(solution)/shard_map/ppermute | solution.py:29
  75.9 0.7 collective-permute-done.7
  76.7 0.4 collective-permute-start.8
  77.2 3.2 %collective-permute-done.16 = f32[4,64,256]{2,1,0:T(8,128)S(1)} collective-permute-done((f32[4,64,256]{2,1,0:T(8,128)S(1)}, f32[4,64,256]{2,1,0:T(8,128)S(1)}, u32[]{:S(2)}, u32[]{:S(2)}) %collective-permute-start.16) | collective-permute-done | bytes 262176 | tf_op jit(solution)/shard_map/ppermute | solution.py:29
  80.5 0.9 %collective-permute-done.8 = f32[3,64,128]{2,1,0:T(8,128)S(1)} collective-permute-done((f32[3,64,128]{2,1,0:T(8,128)S(1)}, f32[3,64,128]{2,1,0:T(8,128)S(1)}, u32[]{:S(2)}, u32[]{:S(2)}) %collective-permute-start.8) | collective-permute-done | bytes 98336 | tf_op jit(solution)/shard_map/ppermute | solution.py:525
  81.4 0.6 fusion.25
  82.1 0.3 collective-permute-done.17
  82.4 0.1 broadcast_select_fusion
  82.5 1.0 %fusion.8 = (f32[256,256]{1,0:T(8,128)}, f32[256,256]{1,0:T(8,128)}, f32[256,256]{1,0:T(8,128)}, f32[256,256]{1,0:T(8,128)}) fusion(f32[4,128,256]{2,1,0:T(8,128)S(1)} %get-tuple-element.46, f32[4,128,256]{2,1,0:T(8,128)S(1)} %get-tuple-element.47), kind=kLoop, calls=%fused_computation.24 | loop fusion | flops 262144 | bytes 2097152 | tf_op jit(solution)/shard_map/squeeze | solution.py:530
  (39 shorter events, 0.8 us)
Async XLA Ops:
  1.5 13.1 %collective-permute-start = (f32[2,128,128]{2,1,0:T(8,128)S(1)}, f32[2,128,128]{2,1,0:T(8,128)S(1)}, u32[]{:S(2)}, u32[]{:S(2)}) collective-permute-start(f32[2,128,128]{2,1,0:T(8,128)S(1)} %pad_maximum_fusion.6), channel_id=1, source_target_pairs={{0,1},{1,0},{2,3},{3,2},{4,5},{5,4},{6,7},{7,6},{8,16},{9,17},{10,... | collective-permute-start | bytes 393224 | tf_op jit(solution)/shard_map/ppermute | solution.py:29
  4.5 10.1 %collective-permute-start.1 = (f32[2,128,128]{2,1,0:T(8,128)S(1)}, f32[2,128,128]{2,1,0:T(8,128)S(1)}, u32[]{:S(2)}, u32[]{:S(2)}) collective-permute-start(f32[2,128,128]{2,1,0:T(8,128)S(1)} %pad_maximum_fusion.6), channel_id=1, source_target_pairs={{0,8},{1,9},{2,10},{3,11},{4,12},{5,13},{6,14},{7,15},{8,0},{9,1},... | collective-permute-start | bytes 393224 | tf_op jit(solution)/shard_map/ppermute | solution.py:29
  6.9 1.6 %copy-start = (bf16[4,512,512]{2,1,0:T(8,128)(2,1)S(1)}, bf16[4,512,512]{2,1,0:T(8,128)(2,1)}, u32[]{:S(2)}) copy-start(bf16[4,512,512]{2,1,0:T(8,128)(2,1)} %constant.125.clone.refs_0_) | copy-start | bytes 6291460
  8.5 1.0 %copy-start.1 = (f32[2,256,256]{2,1,0:T(8,128)S(1)}, f32[2,256,256]{2,1,0:T(8,128)}, u32[]{:S(2)}) copy-start(f32[2,256,256]{2,1,0:T(8,128)} %refs_1_.1) | copy-start | bytes 1572868
  9.5 0.9 %copy-start.2 = (f32[256,256]{1,0:T(8,128)S(1)}, f32[256,256]{1,0:T(8,128)}, u32[]{:S(2)}) copy-start(f32[256,256]{1,0:T(8,128)} %refs_2_.1) | copy-start | bytes 786436
  10.5 0.9 %copy-start.3 = (f32[256,256]{1,0:T(8,128)S(1)}, f32[256,256]{1,0:T(8,128)}, u32[]{:S(2)}) copy-start(f32[256,256]{1,0:T(8,128)} %refs_3_.1) | copy-start | bytes 786436
  11.4 0.9 %copy-start.4 = (f32[256,256]{1,0:T(8,128)S(1)}, f32[256,256]{1,0:T(8,128)}, u32[]{:S(2)}) copy-start(f32[256,256]{1,0:T(8,128)} %refs_4_.1) | copy-start | bytes 786436
  12.4 0.9 %copy-start.5 = (f32[256,256]{1,0:T(8,128)S(1)}, f32[256,256]{1,0:T(8,128)}, u32[]{:S(2)}) copy-start(f32[256,256]{1,0:T(8,128)} %refs_5_.1) | copy-start | bytes 786436
  13.3 0.9 %copy-start.6 = (s32[256,256]{1,0:T(8,128)S(1)}, s32[256,256]{1,0:T(8,128)}, u32[]{:S(2)}) copy-start(s32[256,256]{1,0:T(8,128)} %refs_6_.1) | copy-start | bytes 786436
  14.6 2.0 %copy-start.7 = (s32[2,2]{1,0:T(2,128)S(1)}, s32[2,2]{1,0:T(2,128)}, u32[]{:S(2)}) copy-start(s32[2,2]{1,0:T(2,128)} %param.18) | copy-start | bytes 52
  14.7 7.8 %collective-permute-start.2 = (f32[2,384,128]{2,1,0:T(8,128)S(1)}, f32[2,384,128]{2,1,0:T(8,128)S(1)}, u32[]{:S(2)}, u32[]{:S(2)}) collective-permute-start(f32[2,384,128]{2,1,0:T(8,128)S(1)} %pad_maximum_fusion.3), channel_id=1, source_target_pairs={{0,1},{1,0},{2,4},{3,5},{4,2},{5,3},{6,7},{7,6},{8,9},{9,8},{10,12... | collective-permute-start | bytes 1179656 | tf_op jit(solution)/shard_map/ppermute | solution.py:29
  16.3 6.3 %collective-permute-start.3 = (f32[2,384,128]{2,1,0:T(8,128)S(1)}, f32[2,384,128]{2,1,0:T(8,128)S(1)}, u32[]{:S(2)}, u32[]{:S(2)}) collective-permute-start(f32[2,384,128]{2,1,0:T(8,128)S(1)} %pad_maximum_fusion.3), channel_id=1, source_target_pairs={{0,2},{1,3},{2,0},{3,1},{4,6},{5,7},{6,4},{7,5},{8,10},{9,11},{10,... | collective-permute-start | bytes 1179656 | tf_op jit(solution)/shard_map/ppermute | solution.py:29
  26.9 5.2 %collective-permute-start.10 = (f32[4,136,256]{2,1,0:T(8,128)S(1)}, f32[4,136,256]{2,1,0:T(8,128)S(1)}, u32[]{:S(2)}, u32[]{:S(2)}) collective-permute-start(f32[4,136,256]{2,1,0:T(8,128)S(1)} %get-tuple-element.41), channel_id=1, source_target_pairs={{0,2},{1,3},{2,0},{3,1},{4,6},{5,7},{6,4},{7,5},{8,10},{9,11},{10,... | collective-permute-start | bytes 1671176 | tf_op jit(solution)/shard_map/ppermute | solution.py:29
  30.4 1.7 %collective-permute-start.9 = (f32[4,64,256]{2,1,0:T(8,128)S(1)}, f32[4,64,256]{2,1,0:T(8,128)S(1)}, u32[]{:S(2)}, u32[]{:S(2)}) collective-permute-start(f32[4,64,256]{2,1,0:T(8,128)S(1)} %get-tuple-element.39), channel_id=1, source_target_pairs={{0,2},{1,3},{2,0},{3,1},{4,6},{5,7},{6,4},{7,5},{8,10},{9,11},{10,... | collective-permute-start | bytes 786440 | tf_op jit(solution)/shard_map/ppermute | solution.py:29
  32.3 8.0 %collective-permute-start.11 = (f32[2,200,256]{2,1,0:T(8,128)S(1)}, f32[2,200,256]{2,1,0:T(8,128)S(1)}, u32[]{:S(2)}, u32[]{:S(2)}) collective-permute-start(f32[2,200,256]{2,1,0:T(8,128)S(1)} %pad_maximum_fusion.2), channel_id=1, source_target_pairs={{0,1},{1,0},{2,10},{3,11},{4,5},{5,4},{6,14},{7,15},{8,9},{9,8},{1... | collective-permute-start | bytes 1228808 | tf_op jit(solution)/shard_map/ppermute | solution.py:29
  40.4 5.8 %collective-permute-start.12 = (f32[1,200,256]{2,1,0:T(8,128)S(1)}, f32[1,200,256]{2,1,0:T(8,128)S(1)}, u32[]{:S(2)}, u32[]{:S(2)}) collective-permute-start(f32[1,200,256]{2,1,0:T(8,128)S(1)} %slice.103), channel_id=1, source_target_pairs={{0,8},{1,9},{2,3},{3,2},{4,12},{5,13},{6,7},{7,6},{8,0},{9,1},{10,... | collective-permute-start | bytes 614408 | tf_op jit(solution)/shard_map/ppermute | solution.py:29
  42.6 19.1 %collective-permute-start.4 = (f32[3,384,128]{2,1,0:T(8,128)S(1)}, f32[3,384,128]{2,1,0:T(8,128)}, u32[]{:S(2)}, u32[]{:S(2)}) collective-permute-start(f32[3,384,128]{2,1,0:T(8,128)S(1)} %get-tuple-element.36), channel_id=1, source_target_pairs={{0,2},{1,3},{2,0},{3,1},{4,6},{5,7},{6,4},{7,5},{8,10},{9,11},{10,... | collective-permute-start | bytes 1769480 | tf_op jit(solution)/shard_map/ppermute | solution.py:29
  43.0 18.6 %collective-permute-start.5 = (f32[3,384,128]{2,1,0:T(8,128)S(1)}, f32[3,384,128]{2,1,0:T(8,128)}, u32[]{:S(2)}, u32[]{:S(2)}) collective-permute-start(f32[3,384,128]{2,1,0:T(8,128)S(1)} %get-tuple-element.37), channel_id=1, source_target_pairs={{2,4},{3,5},{4,2},{5,3},{10,12},{11,13},{12,10},{13,11},{18,20},{1... | collective-permute-start | bytes 1769480 | tf_op jit(solution)/shard_map/ppermute | solution.py:29
  46.2 10.6 %collective-permute-start.13 = (f32[1,200,256]{2,1,0:T(8,128)S(1)}, f32[1,200,256]{2,1,0:T(8,128)}, u32[]{:S(2)}, u32[]{:S(2)}) collective-permute-start(f32[1,200,256]{2,1,0:T(8,128)S(1)} %slice_add_fusion), channel_id=1, source_target_pairs={{0,4},{1,5},{2,18},{3,19},{4,0},{5,1},{6,22},{7,23},{8,12},{9,13},... | collective-permute-start | bytes 614408 | tf_op jit(solution)/shard_map/ppermute | solution.py:29
  57.8 10.9 %collective-permute-start.14 = (f32[1,200,256]{2,1,0:T(8,128)S(1)}, f32[1,200,256]{2,1,0:T(8,128)S(1)}, u32[]{:S(2)}, u32[]{:S(2)}) collective-permute-start(f32[1,200,256]{2,1,0:T(8,128)S(1)} %add.159), channel_id=1, source_target_pairs={{0,16},{1,17},{2,6},{3,7},{4,20},{5,21},{6,2},{7,3},{8,24},{9,25},... | collective-permute-start | bytes 614408 | tf_op jit(solution)/shard_map/ppermute | solution.py:29
  68.8 5.0 %collective-permute-start.15 = (f32[4,32,256]{2,1,0:T(8,128)S(1)}, f32[4,32,256]{2,1,0:T(8,128)S(1)}, u32[]{:S(2)}, u32[]{:S(2)}) collective-permute-start(f32[4,32,256]{2,1,0:T(8,128)S(1)} %pad_maximum_fusion.7), channel_id=1, source_target_pairs={{0,8},{1,9},{2,3},{3,2},{4,12},{5,13},{6,7},{7,6},{8,0},{9,1},{10,... | collective-permute-start | bytes 393224 | tf_op jit(solution)/shard_map/ppermute | solution.py:29
  69.3 6.6 %collective-permute-start.6 = (f32[3,128,128]{2,1,0:T(8,128)S(1)}, f32[3,128,128]{2,1,0:T(8,128)S(1)}, u32[]{:S(2)}, u32[]{:S(2)}) collective-permute-start(f32[3,128,128]{2,1,0:T(8,128)S(1)} %get-tuple-element.51), channel_id=1, source_target_pairs={{0,8},{1,9},{2,10},{3,11},{4,12},{5,13},{6,14},{7,15},{8,0},{9,1},... | collective-permute-start | bytes 589832 | tf_op jit(solution)/shard_map/ppermute | solution.py:29
  71.0 5.7 %collective-permute-start.7 = (f32[3,128,128]{2,1,0:T(8,128)S(1)}, f32[3,128,128]{2,1,0:T(8,128)S(1)}, u32[]{:S(2)}, u32[]{:S(2)}) collective-permute-start(f32[3,128,128]{2,1,0:T(8,128)S(1)} %get-tuple-element.50), channel_id=1, source_target_pairs={{0,1},{1,0},{2,3},{3,2},{4,5},{5,4},{6,7},{7,6},{8,16},{9,17},{10,... | collective-permute-start | bytes 589832 | tf_op jit(solution)/shard_map/ppermute | solution.py:29
  73.9 6.4 %collective-permute-start.16 = (f32[4,64,256]{2,1,0:T(8,128)S(1)}, f32[4,64,256]{2,1,0:T(8,128)S(1)}, u32[]{:S(2)}, u32[]{:S(2)}) collective-permute-start(f32[4,64,256]{2,1,0:T(8,128)S(1)} %pad_maximum_fusion.5), channel_id=1, source_target_pairs={{0,1},{1,0},{2,10},{3,11},{4,5},{5,4},{6,14},{7,15},{8,9},{9,8},{1... | collective-permute-start | bytes 786440 | tf_op jit(solution)/shard_map/ppermute | solution.py:29
  76.7 4.7 %collective-permute-start.8 = (f32[3,64,128]{2,1,0:T(8,128)S(1)}, f32[3,64,128]{2,1,0:T(8,128)S(1)}, u32[]{:S(2)}, u32[]{:S(2)}) collective-permute-start(f32[3,64,128]{2,1,0:T(8,128)S(1)} %constant_dynamic-slice_fusion), channel_id=1, source_target_pairs={{0,1},{1,0},{2,3},{3,2},{4,5},{5,4},{6,7},{7,6},{8,9},{9,8},{10,11... | collective-permute-start | bytes 294920 | tf_op jit(solution)/shard_map/ppermute | solution.py:525
  80.4 2.0 %collective-permute-start.17 = (f32[4,128,256]{2,1,0:T(8,128)S(1)}, f32[4,128,256]{2,1,0:T(8,128)S(1)}, u32[]{:S(2)}, u32[]{:S(2)}) collective-permute-start(f32[4,128,256]{2,1,0:T(8,128)S(1)} %pad_maximum_fusion.1), channel_id=1, source_target_pairs={{0,2},{1,3},{2,0},{3,1},{4,6},{5,7},{6,4},{7,5},{8,10},{9,11},{10,... | collective-permute-start | bytes 1572872 | tf_op jit(solution)/shard_map/ppermute | solution.py:29
